TPU v7x, 256 devices: a whole 4x4x8 slice. The times are simulated.
256 devices in a mesh: section: 4 (over y), expert: 64 (over z, x, core).
Axes of the slice: x: 4, y: 4, z: 8, core: 2. Of those that a mesh axis runs over, the one named last changes fastest.
Arguments:
- inputs: bfloat16 [4, 192, 3072], P(None, 'expert'), may hold values from -6 to 6
- routes: int32 [4, 4, 192, 2], P('section'), may hold values from 0 to 3, all different within a row; in each aligned block of 3 rows (0 to 2, 3 to 5, ..., all dimensions but the last counted through in order) at most 2 rows name the same one
- norm_gain: float32 [4, 3072], P('section'), may hold values from 0.5 to 1.5
- router: bfloat16 [4, 3072, 4], P('section'), may hold values from -0.109375 to 0.109375
- w_gate: bfloat16 [4, 3072, 32768], P('section', None, 'expert'), may hold values from -0.109375 to 0.109375
- w_up: bfloat16 [4, 3072, 32768], P('section', None, 'expert'), may hold values from -0.109375 to 0.109375
- w_down: bfloat16 [4, 32768, 3072], P('section', 'expert'), may hold values from -0.0625 to 0.0625
Outputs:
- layer_outputs: bfloat16 [4, 4, 192, 3072], P('section', None, 'expert')
Inputs may be any that keep to these rules, and one draw needn't show every extreme that they name: `routes`: for each section and micro-batch, the 3 requests of each aligned block name no expert more than 2 times, and a request's two experts differ.
All inputs are finite; a program needn't handle non-finite values.
Results may differ from a plain program's by a relative error of at most 0.017.
Values may be sent and summed in bfloat16 or wider, within the bound.
No kernel may reach another device: no remote copies, remote signals or barrier semaphores. Data moves between devices by JAX's collectives and lax.ppermute only.
A program may use at most 64 MiB of HBM per device.

v0:
```python
import jax
import jax.numpy as jnp
from jax import lax
from jax.sharding import PartitionSpec as P

E = 4
MOST = 2


EPSILON = 1e-05


def from_behind(array, axis, by):
    devices = lax.axis_size(axis)
    pairs = [(i, i + by) for i in range(devices) if 0 <= i + by < devices]
    return lax.ppermute(array, axis, pairs)


def slot_table(route_ids, experts, capacity):
    flat_ids = route_ids.reshape(-1)
    onehot = (flat_ids[:, None] == jnp.arange(experts, dtype=jnp.int32)[None, :]).astype(jnp.int32)
    before = jnp.cumsum(onehot, axis=0) - onehot
    within = jnp.sum(before * onehot, axis=1)
    target = flat_ids * capacity + within
    slot_grid = jnp.arange(experts * capacity, dtype=jnp.int32)[:, None] == target[None, :]
    return (target, slot_grid)


def normalize(hidden, gain_row):
    wide_hidden = hidden.astype(jnp.float32)
    inv_rms = lax.rsqrt(jnp.mean(wide_hidden * wide_hidden, axis=-1, keepdims=True) + EPSILON)
    normed = (wide_hidden * inv_rms * gain_row).astype(jnp.bfloat16)
    return (wide_hidden, inv_rms, normed)


def first_share(normed, router, route_ids):
    logits = jnp.dot(normed, router, preferred_element_type=jnp.float32)
    match_mask = (
        route_ids[:, :, None] == jnp.arange(router.shape[1], dtype=jnp.int32)[None, None, :]
    )
    chosen = jnp.sum(jnp.where(match_mask, logits[:, None, :], 0.0), axis=-1)
    return jax.nn.sigmoid(chosen[:, 0] - chosen[:, 1])


def spread(route_rows, slot_grid, groups):
    model_width = route_rows.shape[1]
    outgoing = jnp.dot(
        slot_grid.astype(jnp.bfloat16), route_rows, preferred_element_type=jnp.float32
    ).astype(jnp.bfloat16)
    layered = jnp.broadcast_to(
        outgoing.reshape(E, 1, MOST, model_width), (E, groups, MOST, model_width)
    )
    return layered.reshape(E * groups, MOST, model_width)


def collect(returned, target, groups):
    model_width = returned.shape[2]
    merged = jnp.sum(returned.reshape(E, groups, MOST, model_width).astype(jnp.float32), axis=1)
    return jnp.take(merged.reshape(E * MOST, model_width), target, axis=0)


def store_at(buffer_all, new_value, slot_index, active):
    previous = lax.dynamic_index_in_dim(buffer_all, slot_index, 0, keepdims=False)
    return lax.dynamic_update_index_in_dim(
        buffer_all, jnp.where(active, new_value, previous), slot_index, 0
    )


def make_forward(gate_mat, up_mat, down_mat):

    def expert_pass(row_block):
        flat_rows = row_block.reshape(-1, row_block.shape[2])
        gate_value = jnp.dot(flat_rows, gate_mat, preferred_element_type=jnp.float32)
        up_value = jnp.dot(flat_rows, up_mat, preferred_element_type=jnp.float32)
        hidden = (jax.nn.silu(gate_value) * up_value).astype(jnp.bfloat16)
        partial_out = jnp.dot(hidden, down_mat, preferred_element_type=jnp.float32).astype(
            jnp.bfloat16
        )
        return lax.all_to_all(
            partial_out.reshape(row_block.shape), "expert", split_axis=0, concat_axis=0, tiled=True
        )

    return expert_pass


def on_device(inputs, routes, norm_gain, router, w_gate, w_up, w_down):
    sections = lax.axis_size("section")
    section_pos = lax.axis_index("section")
    members = lax.axis_size("expert")
    member_pos = lax.axis_index("expert")
    groups = members // E
    micro_count = inputs.shape[0]
    tok_rows = inputs.shape[1]
    model_width = inputs.shape[2]
    gain_row = norm_gain[0]
    router_mat = router[0]
    route_all = routes[0]
    expert_pass = make_forward(w_gate[0], w_up[0], w_down[0])
    tick_count = micro_count + sections - 1
    out_store = jnp.zeros((micro_count, tok_rows, model_width), jnp.bfloat16)
    arriving = jnp.zeros((tok_rows, model_width), jnp.bfloat16)
    for tick_step in range(tick_count):
        micro_index = tick_step - section_pos
        active = (micro_index >= 0) & (micro_index < micro_count)
        slot_index = jnp.clip(micro_index, 0, micro_count - 1)
        hidden = jnp.where(section_pos == 0, inputs[min(tick_step, micro_count - 1)], arriving)
        section_routes = lax.dynamic_index_in_dim(route_all, slot_index, 0, keepdims=False)
        route_ids = lax.dynamic_slice_in_dim(section_routes, member_pos * tok_rows, tok_rows, 0)
        wide_hidden, inv_rms, normed = normalize(hidden, gain_row)
        share = first_share(normed, router_mat, route_ids)
        target, slot_grid = slot_table(route_ids, E, MOST)
        outgoing = spread(jnp.repeat(normed, 2, axis=0), slot_grid, groups)
        returned = expert_pass(
            lax.all_to_all(outgoing, "expert", split_axis=0, concat_axis=0, tiled=True)
        )
        routed = collect(returned, target, groups).reshape(tok_rows, 2, model_width)
        result = (
            wide_hidden + share[:, None] * routed[:, 0] + (1.0 - share)[:, None] * routed[:, 1]
        ).astype(jnp.bfloat16)
        out_store = store_at(out_store, result, slot_index, active)
        if tick_step + 1 < tick_count:
            arriving = from_behind(result, "section", 1)
    return out_store[None]


def solution(mesh):
    placed = (
        P(None, "expert", None),
        P("section", None, None, None),
        P("section", None),
        P("section", None, None),
        P("section", None, "expert"),
        P("section", None, "expert"),
        P("section", "expert", None),
    )
    return jax.shard_map(
        on_device,
        mesh=mesh,
        in_specs=placed,
        out_specs=P("section", None, "expert", None),
        check_vma=False,
    )
```

profile of v0, /device:TPU:16, one launch (start us, length us, event | category | flops | bytes accessed | tf_op | source)
XLA Modules:
  0.0 581.1 jit_solution(11806010081693125422)
XLA Ops:
  5.4 35.1 %all_to_all.70 = bf16[64,2,3072]{2,1,0:T(2,128)(2,1)} all-to-all(bf16[64,2,3072]{2,1,0:T(2,128)(2,1)S(1)} %bitcast.374), channel_id=1, replica_groups=mesh['section'=4,'expert'=64] {'expert'}, dimensions={0} | all-to-all | bytes 1572864 | tf_op jit(solution)/shard_map/all_to_all | solution.py:114
  46.2 4.2 convolution_convert_fusion.6
  53.2 5.9 %all-to-all-start.1 = ((bf16[64,2,3072]{2,1,0:T(2,128)(2,1)}), bf16[64,2,3072]{2,1,0:T(2,128)(2,1)}, u32[]{:S(2)}, u32[]{:S(2)}) async-start(bf16[64,2,3072]{2,1,0:T(2,128)(2,1)} %reshape.464), calls=%async_computation.1 | async-start | bytes 1572864 | tf_op jit(solution)/shard_map/all_to_all | solution.py:79
  61.1 21.1 %all-to-all-done.1 = bf16[64,2,3072]{2,1,0:T(2,128)(2,1)} async-done(((bf16[64,2,3072]{2,1,0:T(2,128)(2,1)}), bf16[64,2,3072]{2,1,0:T(2,128)(2,1)}, u32[]{:S(2)}, u32[]{:S(2)}) %all-to-all-start.1) | async-done | bytes 786464 | tf_op jit(solution)/shard_map/all_to_all | solution.py:79
  93.7 6.1 %all-to-all-start.2 = ((bf16[64,2,3072]{2,1,0:T(2,128)(2,1)}), bf16[64,2,3072]{2,1,0:T(2,128)(2,1)}, u32[]{:S(2)}, u32[]{:S(2)}) async-start(bf16[64,2,3072]{2,1,0:T(2,128)(2,1)} %bitcast.371), calls=%async_computation.2 | async-start | bytes 1572864 | tf_op jit(solution)/shard_map/all_to_all | solution.py:114
  101.1 21.8 %all-to-all-done.2 = bf16[64,2,3072]{2,1,0:T(2,128)(2,1)} async-done(((bf16[64,2,3072]{2,1,0:T(2,128)(2,1)}), bf16[64,2,3072]{2,1,0:T(2,128)(2,1)}, u32[]{:S(2)}, u32[]{:S(2)}) %all-to-all-start.2) | async-done | bytes 786464 | tf_op jit(solution)/shard_map/all_to_all | solution.py:114
  128.6 4.1 convolution_convert_fusion.5
  135.6 5.9 %all-to-all-start.3 = ((bf16[64,2,3072]{2,1,0:T(2,128)(2,1)}), bf16[64,2,3072]{2,1,0:T(2,128)(2,1)}, u32[]{:S(2)}, u32[]{:S(2)}) async-start(bf16[64,2,3072]{2,1,0:T(2,128)(2,1)} %reshape.471), calls=%async_computation.3 | async-start | bytes 1572864 | tf_op jit(solution)/shard_map/all_to_all | solution.py:79
  143.7 20.9 %all-to-all-done.3 = bf16[64,2,3072]{2,1,0:T(2,128)(2,1)} async-done(((bf16[64,2,3072]{2,1,0:T(2,128)(2,1)}), bf16[64,2,3072]{2,1,0:T(2,128)(2,1)}, u32[]{:S(2)}, u32[]{:S(2)}) %all-to-all-start.3) | async-done | bytes 786464 | tf_op jit(solution)/shard_map/all_to_all | solution.py:79
  177.2 6.3 %all-to-all-start.4 = ((bf16[64,2,3072]{2,1,0:T(2,128)(2,1)}), bf16[64,2,3072]{2,1,0:T(2,128)(2,1)}, u32[]{:S(2)}, u32[]{:S(2)}) async-start(bf16[64,2,3072]{2,1,0:T(2,128)(2,1)} %bitcast.372), calls=%async_computation.4 | async-start | bytes 1572864 | tf_op jit(solution)/shard_map/all_to_all | solution.py:114
  183.7 22.9 %all-to-all-done.4 = bf16[64,2,3072]{2,1,0:T(2,128)(2,1)} async-done(((bf16[64,2,3072]{2,1,0:T(2,128)(2,1)}), bf16[64,2,3072]{2,1,0:T(2,128)(2,1)}, u32[]{:S(2)}, u32[]{:S(2)}) %all-to-all-start.4) | async-done | bytes 786464 | tf_op jit(solution)/shard_map/all_to_all | solution.py:114
  213.0 4.1 convolution_convert_fusion.4
  220.0 5.9 %all-to-all-start.5 = ((bf16[64,2,3072]{2,1,0:T(2,128)(2,1)}), bf16[64,2,3072]{2,1,0:T(2,128)(2,1)}, u32[]{:S(2)}, u32[]{:S(2)}) async-start(bf16[64,2,3072]{2,1,0:T(2,128)(2,1)} %reshape.478), calls=%async_computation.5 | async-start | bytes 1572864 | tf_op jit(solution)/shard_map/all_to_all | solution.py:79
  229.3 19.8 %all-to-all-done.5 = bf16[64,2,3072]{2,1,0:T(2,128)(2,1)} async-done(((bf16[64,2,3072]{2,1,0:T(2,128)(2,1)}), bf16[64,2,3072]{2,1,0:T(2,128)(2,1)}, u32[]{:S(2)}, u32[]{:S(2)}) %all-to-all-start.5) | async-done | bytes 786464 | tf_op jit(solution)/shard_map/all_to_all | solution.py:79
  259.2 29.0 %all_to_all.71 = bf16[64,2,3072]{2,1,0:T(2,128)(2,1)} all-to-all(bf16[64,2,3072]{2,1,0:T(2,128)(2,1)S(1)} %bitcast.375), channel_id=1, replica_groups=mesh['section'=4,'expert'=64] {'expert'}, dimensions={0} | all-to-all | bytes 1572864 | tf_op jit(solution)/shard_map/all_to_all | solution.py:114
  291.2 3.4 fusion.27
  294.6 4.1 convolution_convert_fusion.3
  301.6 5.9 %all-to-all-start.7 = ((bf16[64,2,3072]{2,1,0:T(2,128)(2,1)}), bf16[64,2,3072]{2,1,0:T(2,128)(2,1)}, u32[]{:S(2)}, u32[]{:S(2)}) async-start(bf16[64,2,3072]{2,1,0:T(2,128)(2,1)} %reshape.485), calls=%async_computation.7 | async-start | bytes 1572864 | tf_op jit(solution)/shard_map/all_to_all | solution.py:79
  309.7 21.0 %all-to-all-done.7 = bf16[64,2,3072]{2,1,0:T(2,128)(2,1)} async-done(((bf16[64,2,3072]{2,1,0:T(2,128)(2,1)}), bf16[64,2,3072]{2,1,0:T(2,128)(2,1)}, u32[]{:S(2)}, u32[]{:S(2)}) %all-to-all-start.7) | async-done | bytes 786464 | tf_op jit(solution)/shard_map/all_to_all | solution.py:79
  341.7 5.9 %all-to-all-start.8 = ((bf16[64,2,3072]{2,1,0:T(2,128)(2,1)}), bf16[64,2,3072]{2,1,0:T(2,128)(2,1)}, u32[]{:S(2)}, u32[]{:S(2)}) async-start(bf16[64,2,3072]{2,1,0:T(2,128)(2,1)} %bitcast.373), calls=%async_computation.8 | async-start | bytes 1572864 | tf_op jit(solution)/shard_map/all_to_all | solution.py:114
  347.8 22.9 %all-to-all-done.8 = bf16[64,2,3072]{2,1,0:T(2,128)(2,1)} async-done(((bf16[64,2,3072]{2,1,0:T(2,128)(2,1)}), bf16[64,2,3072]{2,1,0:T(2,128)(2,1)}, u32[]{:S(2)}, u32[]{:S(2)}) %all-to-all-start.8) | async-done | bytes 786464 | tf_op jit(solution)/shard_map/all_to_all | solution.py:114
  377.1 4.1 convolution_convert_fusion.2
  384.1 6.1 %all-to-all-start.9 = ((bf16[64,2,3072]{2,1,0:T(2,128)(2,1)}), bf16[64,2,3072]{2,1,0:T(2,128)(2,1)}, u32[]{:S(2)}, u32[]{:S(2)}) async-start(bf16[64,2,3072]{2,1,0:T(2,128)(2,1)} %reshape.492), calls=%async_computation.9 | async-start | bytes 1572864 | tf_op jit(solution)/shard_map/all_to_all | solution.py:79
  392.9 20.4 %all-to-all-done.9 = bf16[64,2,3072]{2,1,0:T(2,128)(2,1)} async-done(((bf16[64,2,3072]{2,1,0:T(2,128)(2,1)}), bf16[64,2,3072]{2,1,0:T(2,128)(2,1)}, u32[]{:S(2)}, u32[]{:S(2)}) %all-to-all-start.9) | async-done | bytes 786464 | tf_op jit(solution)/shard_map/all_to_all | solution.py:79
  423.5 28.8 %all_to_all.72 = bf16[64,2,3072]{2,1,0:T(2,128)(2,1)} all-to-all(bf16[64,2,3072]{2,1,0:T(2,128)(2,1)S(1)} %bitcast.376), channel_id=1, replica_groups=mesh['section'=4,'expert'=64] {'expert'}, dimensions={0} | all-to-all | bytes 1572864 | tf_op jit(solution)/shard_map/all_to_all | solution.py:114
  458.7 4.1 convolution_convert_fusion.1
  465.7 5.9 %all-to-all-start.11 = ((bf16[64,2,3072]{2,1,0:T(2,128)(2,1)}), bf16[64,2,3072]{2,1,0:T(2,128)(2,1)}, u32[]{:S(2)}, u32[]{:S(2)}) async-start(bf16[64,2,3072]{2,1,0:T(2,128)(2,1)} %reshape.499), calls=%async_computation.11 | async-start | bytes 1572864 | tf_op jit(solution)/shard_map/all_to_all | solution.py:79
  473.7 21.0 %all-to-all-done.11 = bf16[64,2,3072]{2,1,0:T(2,128)(2,1)} async-done(((bf16[64,2,3072]{2,1,0:T(2,128)(2,1)}), bf16[64,2,3072]{2,1,0:T(2,128)(2,1)}, u32[]{:S(2)}, u32[]{:S(2)}) %all-to-all-start.11) | async-done | bytes 786464 | tf_op jit(solution)/shard_map/all_to_all | solution.py:79
  504.9 28.8 %all_to_all.73 = bf16[64,2,3072]{2,1,0:T(2,128)(2,1)} all-to-all(bf16[64,2,3072]{2,1,0:T(2,128)(2,1)S(1)} %bitcast.377), channel_id=1, replica_groups=mesh['section'=4,'expert'=64] {'expert'}, dimensions={0} | all-to-all | bytes 1572864 | tf_op jit(solution)/shard_map/all_to_all | solution.py:114
  540.1 4.1 convolution_convert_fusion
  547.1 5.9 %all-to-all-start.13 = ((bf16[64,2,3072]{2,1,0:T(2,128)(2,1)}), bf16[64,2,3072]{2,1,0:T(2,128)(2,1)}, u32[]{:S(2)}, u32[]{:S(2)}) async-start(bf16[64,2,3072]{2,1,0:T(2,128)(2,1)} %reshape.506), calls=%async_computation.13 | async-start | bytes 1572864 | tf_op jit(solution)/shard_map/all_to_all | solution.py:79
  554.0 22.1 %all-to-all-done.13 = bf16[64,2,3072]{2,1,0:T(2,128)(2,1)} async-done(((bf16[64,2,3072]{2,1,0:T(2,128)(2,1)}), bf16[64,2,3072]{2,1,0:T(2,128)(2,1)}, u32[]{:S(2)}, u32[]{:S(2)}) %all-to-all-start.13) | async-done | bytes 786464 | tf_op jit(solution)/shard_map/all_to_all | solution.py:79
  (324 shorter events, 151.6 us)
Async XLA Ops:
  0.0 46.2 %copy-start = (bf16[1,512,3072]{2,1,0:T(8,128)(2,1)S(1)}, bf16[1,512,3072]{2,1,0:T(8,128)(2,1)}, u32[]{:S(2)}) copy-start(bf16[1,512,3072]{2,1,0:T(8,128)(2,1)} %param.15) | copy-start | bytes 9437188
  1.6 57.6 %copy-start.17 = (s32[1,1,3,2]{2,3,1,0:T(2,128)}, s32[1,1,3,2]{2,3,1,0:T(2,128)S(1)}, u32[]{:S(2)}) copy-start(s32[1,1,3,2]{2,3,1,0:T(2,128)S(1)} %get-tuple-element.80) | copy-start | bytes 76
  1.6 58.0 %copy-start.15 = (s32[1,1,3,2]{2,3,1,0:T(2,128)}, s32[1,1,3,2]{2,3,1,0:T(2,128)S(1)}, u32[]{:S(2)}) copy-start(s32[1,1,3,2]{2,3,1,0:T(2,128)S(1)} %get-tuple-element.79) | copy-start | bytes 76
  50.3 40.5 %copy-start.8 = (bf16[1,3,3072]{2,0,1:T(2,128)(2,1)S(1)}, bf16[1,3,3072]{2,0,1:T(2,128)(2,1)}, u32[]{:S(2)}) copy-start(bf16[1,3,3072]{2,0,1:T(2,128)(2,1)} %get-tuple-element.68) | copy-start | bytes 55300
  53.2 29.0 %all-to-all-start.1 = ((bf16[64,2,3072]{2,1,0:T(2,128)(2,1)}), bf16[64,2,3072]{2,1,0:T(2,128)(2,1)}, u32[]{:S(2)}, u32[]{:S(2)}) async-start(bf16[64,2,3072]{2,1,0:T(2,128)(2,1)} %reshape.464), calls=%async_computation.1 | async-start | bytes 1572864 | tf_op jit(solution)/shard_map/all_to_all | solution.py:79
  59.3 40.5 %copy-start.18 = (s32[1,1,3,2]{2,3,1,0:T(2,128)S(1)}, s32[1,1,3,2]{2,3,1,0:T(2,128)}, u32[]{:S(2)}) copy-start(s32[1,1,3,2]{2,3,1,0:T(2,128)} %copy-done.17) | copy-start | bytes 76
  85.1 5.7 collective-permute-start
  93.7 29.2 %all-to-all-start.2 = ((bf16[64,2,3072]{2,1,0:T(2,128)(2,1)}), bf16[64,2,3072]{2,1,0:T(2,128)(2,1)}, u32[]{:S(2)}, u32[]{:S(2)}) async-start(bf16[64,2,3072]{2,1,0:T(2,128)(2,1)} %bitcast.371), calls=%async_computation.2 | async-start | bytes 1572864 | tf_op jit(solution)/shard_map/all_to_all | solution.py:114
  135.6 29.0 %all-to-all-start.3 = ((bf16[64,2,3072]{2,1,0:T(2,128)(2,1)}), bf16[64,2,3072]{2,1,0:T(2,128)(2,1)}, u32[]{:S(2)}, u32[]{:S(2)}) async-start(bf16[64,2,3072]{2,1,0:T(2,128)(2,1)} %reshape.471), calls=%async_computation.3 | async-start | bytes 1572864 | tf_op jit(solution)/shard_map/all_to_all | solution.py:79
  141.5 42.0 %copy-start.14 = (s32[1,1,3,2]{2,3,1,0:T(2,128)S(1)}, s32[1,1,3,2]{2,3,1,0:T(2,128)}, u32[]{:S(2)}) copy-start(s32[1,1,3,2]{2,3,1,0:T(2,128)} %get-tuple-element.78) | copy-start | bytes 76
  169.0 5.7 collective-permute-start.1
  175.6 37.4 %copy-start.3 = (bf16[3,3072]{1,0:T(4,128)(2,1)}, bf16[3,3072]{1,0:T(4,128)(2,1)S(1)}, u32[]{:S(2)}) copy-start(bf16[3,3072]{1,0:T(4,128)(2,1)S(1)} %get-tuple-element.47) | copy-start | bytes 55300
  177.2 29.4 %all-to-all-start.4 = ((bf16[64,2,3072]{2,1,0:T(2,128)(2,1)}), bf16[64,2,3072]{2,1,0:T(2,128)(2,1)}, u32[]{:S(2)}, u32[]{:S(2)}) async-start(bf16[64,2,3072]{2,1,0:T(2,128)(2,1)} %bitcast.372), calls=%async_computation.4 | async-start | bytes 1572864 | tf_op jit(solution)/shard_map/all_to_all | solution.py:114
  217.2 34.4 %copy-start.29 = (pred[6]{0:T(512)(128)(4,1)S(1)}, pred[6]{0:T(512)(128)(4,1)}, u32[]{:S(2)}) copy-start(pred[6]{0:T(512)(128)(4,1)} %get-tuple-element.44) | copy-start | bytes 22
  220.0 29.0 %all-to-all-start.5 = ((bf16[64,2,3072]{2,1,0:T(2,128)(2,1)}), bf16[64,2,3072]{2,1,0:T(2,128)(2,1)}, u32[]{:S(2)}, u32[]{:S(2)}) async-start(bf16[64,2,3072]{2,1,0:T(2,128)(2,1)} %reshape.478), calls=%async_computation.5 | async-start | bytes 1572864 | tf_op jit(solution)/shard_map/all_to_all | solution.py:79
  252.6 5.7 collective-permute-start.2
  258.5 36.1 %copy-start.6 = (bf16[3,3072]{1,0:T(4,128)(2,1)}, bf16[3,3072]{1,0:T(4,128)(2,1)S(1)}, u32[]{:S(2)}) copy-start(bf16[3,3072]{1,0:T(4,128)(2,1)S(1)} %get-tuple-element.41) | copy-start | bytes 55300
  298.7 34.4 %copy-start.31 = (pred[6]{0:T(512)(128)(4,1)S(1)}, pred[6]{0:T(512)(128)(4,1)}, u32[]{:S(2)}) copy-start(pred[6]{0:T(512)(128)(4,1)} %get-tuple-element.38) | copy-start | bytes 22
  301.6 29.0 %all-to-all-start.7 = ((bf16[64,2,3072]{2,1,0:T(2,128)(2,1)}), bf16[64,2,3072]{2,1,0:T(2,128)(2,1)}, u32[]{:S(2)}, u32[]{:S(2)}) async-start(bf16[64,2,3072]{2,1,0:T(2,128)(2,1)} %reshape.485), calls=%async_computation.7 | async-start | bytes 1572864 | tf_op jit(solution)/shard_map/all_to_all | solution.py:79
  307.5 40.1 %copy-start.12 = (s32[1,1,3,2]{2,3,1,0:T(2,128)S(1)}, s32[1,1,3,2]{2,3,1,0:T(2,128)}, u32[]{:S(2)}) copy-start(s32[1,1,3,2]{2,3,1,0:T(2,128)} %get-tuple-element.82) | copy-start | bytes 76
  334.2 5.7 collective-permute-start.3
  340.1 37.0 %copy-start.4 = (bf16[3,3072]{1,0:T(4,128)(2,1)}, bf16[3,3072]{1,0:T(4,128)(2,1)S(1)}, u32[]{:S(2)}) copy-start(bf16[3,3072]{1,0:T(4,128)(2,1)S(1)} %get-tuple-element.35) | copy-start | bytes 55300
  341.7 29.0 %all-to-all-start.8 = ((bf16[64,2,3072]{2,1,0:T(2,128)(2,1)}), bf16[64,2,3072]{2,1,0:T(2,128)(2,1)}, u32[]{:S(2)}, u32[]{:S(2)}) async-start(bf16[64,2,3072]{2,1,0:T(2,128)(2,1)} %bitcast.373), calls=%async_computation.8 | async-start | bytes 1572864 | tf_op jit(solution)/shard_map/all_to_all | solution.py:114
  347.8 43.1 %copy-start.23 = (s32[6]{0:T(128)}, s32[6]{0:T(128)S(1)}, u32[]{:S(2)}) copy-start(s32[6]{0:T(128)S(1)} %reshape.495) | copy-start | bytes 76
  381.2 34.6 %copy-start.30 = (pred[6]{0:T(512)(128)(4,1)S(1)}, pred[6]{0:T(512)(128)(4,1)}, u32[]{:S(2)}) copy-start(pred[6]{0:T(512)(128)(4,1)} %get-tuple-element.32) | copy-start | bytes 22
  384.1 29.2 %all-to-all-start.9 = ((bf16[64,2,3072]{2,1,0:T(2,128)(2,1)}), bf16[64,2,3072]{2,1,0:T(2,128)(2,1)}, u32[]{:S(2)}, u32[]{:S(2)}) async-start(bf16[64,2,3072]{2,1,0:T(2,128)(2,1)} %reshape.492), calls=%async_computation.9 | async-start | bytes 1572864 | tf_op jit(solution)/shard_map/all_to_all | solution.py:79
  416.9 5.7 collective-permute-start.4
  422.8 35.9 %copy-start.7 = (bf16[3,3072]{1,0:T(4,128)(2,1)}, bf16[3,3072]{1,0:T(4,128)(2,1)S(1)}, u32[]{:S(2)}) copy-start(bf16[3,3072]{1,0:T(4,128)(2,1)S(1)} %get-tuple-element.29) | copy-start | bytes 55300
  462.8 38.6 %copy-start.22 = (s32[6]{0:T(128)S(1)}, s32[6]{0:T(128)}, u32[]{:S(2)}) copy-start(s32[6]{0:T(128)} %copy-done.21) | copy-start | bytes 76
  465.7 29.0 %all-to-all-start.11 = ((bf16[64,2,3072]{2,1,0:T(2,128)(2,1)}), bf16[64,2,3072]{2,1,0:T(2,128)(2,1)}, u32[]{:S(2)}, u32[]{:S(2)}) async-start(bf16[64,2,3072]{2,1,0:T(2,128)(2,1)} %reshape.499), calls=%async_computation.11 | async-start | bytes 1572864 | tf_op jit(solution)/shard_map/all_to_all | solution.py:79
  498.3 5.7 collective-permute-start.5
  547.1 29.0 %all-to-all-start.13 = ((bf16[64,2,3072]{2,1,0:T(2,128)(2,1)}), bf16[64,2,3072]{2,1,0:T(2,128)(2,1)}, u32[]{:S(2)}, u32[]{:S(2)}) async-start(bf16[64,2,3072]{2,1,0:T(2,128)(2,1)} %reshape.506), calls=%async_computation.13 | async-start | bytes 1572864 | tf_op jit(solution)/shard_map/all_to_all | solution.py:79
  (25 other events, 318.2 us)
where the time goes:
time: 591 us; the launch traced here: 581 us
  waiting for transfers between devices  222 us (38%)
  blocking collectives  122 us (21%)
  starting transfers between devices  79 us (13%)
  local copies, waits for them, and re-layouts  66.1 us (11%)
  matrix products  53.4 us (9%)
  other arithmetic  37 us (6%)
    all_to_all x7, waiting for transfers between devices, expert_pass(): lax.all_to_all(partial_out.reshape(row_block.shape), 'expert', split_axis...  146 us
    all_to_all x4, blocking collectives, on_device(): lax.all_to_all(outgoing, 'expert', split_axis=0, concat_axis=0, tiled=True)  122 us
    all_to_all x3, waiting for transfers between devices, on_device(): lax.all_to_all(outgoing, 'expert', split_axis=0, concat_axis=0, tiled=True)  67.7 us
    all_to_all x7, starting transfers between devices, expert_pass(): lax.all_to_all(partial_out.reshape(row_block.shape), 'expert', split_axis...  41.5 us
    dot_general x7, matrix products, expert_pass(): jnp.dot(hidden, down_mat, preferred_element_type=jnp.float32)  29 us
    dot_general x7, matrix products, expert_pass(): jnp.dot(flat_rows, gate_mat, preferred_element_type=jnp.float32)  22.5 us
    reshape x7, local copies, waits for them, and re-layouts, expert_pass(): flat_rows = row_block.reshape(-1, row_block.shape[2])  20.7 us
    reshape x7, local copies, waits for them, and re-layouts, expert_pass(): partial_out.reshape(row_block.shape)  20 us
  transfers between devices with their start and end apart: 16, of which 16 were waited for; matrix products, arithmetic and copies ran while one was open for 4% of the time, Pallas kernels for 0%

commit v1 on v0

v1 whole, which is shorter than its diff:
```python
import jax
import jax.numpy as jnp
from jax import lax
from jax.sharding import PartitionSpec as P

E = 4
MOST = 2
PAIR = 2
EPSILON = 1e-05

SLICES = [[e * 16 + j * 2 + c for j in range(8)] for e in range(E) for c in range(2)]
EXPERTS = [[e * 16 + r for e in range(E)] for r in range(16)]
CORES = [(i, i ^ 1) for i in range(64)]


def gather_over(block, groups, count):
    copies = jnp.broadcast_to(block[None], (count,) + block.shape)
    return lax.all_to_all(
        copies, "expert", split_axis=0, concat_axis=0, axis_index_groups=groups, tiled=True
    )


def tables(ids, expert):
    pairs, tokens = ids.shape[0], ids.shape[3]
    blocks = PAIR * E
    flat = ids.reshape(pairs, blocks, tokens * 2)
    same = flat[..., :, None] == flat[..., None, :]
    earlier = jnp.arange(tokens * 2)[:, None] > jnp.arange(tokens * 2)[None, :]
    slot = jnp.sum((same & earlier).astype(jnp.int32), axis=-1)
    block = jnp.arange(blocks, dtype=jnp.int32)[None, :, None]
    row = block * MOST + slot
    rows = blocks * MOST
    mine = jnp.where(flat == expert, row, -1).reshape(pairs, 1, blocks * tokens, 2)
    pick = jnp.any(mine == jnp.arange(rows, dtype=jnp.int32)[None, :, None, None], axis=-1)
    back = (flat * rows + row).reshape(pairs, blocks * tokens, 2)
    back = jnp.swapaxes(back, 1, 2).reshape(pairs, 2 * blocks * tokens, 1)
    place = back == jnp.arange(E * rows, dtype=jnp.int32)[None, None, :]
    return pick.astype(jnp.bfloat16), place.astype(jnp.bfloat16)


def on_device(inputs, routes, norm_gain, router, w_gate, w_up, w_down):
    sections = lax.axis_size("section")
    section_pos = lax.axis_index("section")
    member_pos = lax.axis_index("expert")
    expert, rest = member_pos // 16, member_pos % 16
    micro_count, tokens, width = inputs.shape
    pairs = micro_count // PAIR
    held = PAIR * E * tokens
    gain_row, router_mat = norm_gain[0], router[0]
    gate_mat, up_mat, down_mat = w_gate[0], w_up[0], w_down[0]

    def ffn(rows):
        gate_value = jnp.dot(rows, gate_mat, preferred_element_type=jnp.float32)
        up_value = jnp.dot(rows, up_mat, preferred_element_type=jnp.float32)
        hidden = (jax.nn.silu(gate_value) * up_value).astype(jnp.bfloat16)
        return jnp.dot(hidden, down_mat, preferred_element_type=jnp.float32).astype(jnp.bfloat16)

    ids = routes[0].reshape(pairs, PAIR, E, 16, tokens, 2)
    ids = lax.dynamic_index_in_dim(ids, rest, 3, keepdims=False)
    pick_all, place_all = tables(ids, expert)
    ids_all = ids.reshape(pairs, held, 2)

    entering = gather_over(inputs.reshape(micro_count * tokens, width), EXPERTS, E)
    entering = entering.reshape(E, pairs, PAIR, tokens, width)
    entering = jnp.transpose(entering, (1, 2, 0, 3, 4)).reshape(pairs, held, width)

    arriving = jnp.zeros((held, width), jnp.bfloat16)
    kept = []
    for tick in range(pairs + sections - 1):
        pair = jnp.clip(tick - section_pos, 0, pairs - 1)
        pick = lax.dynamic_index_in_dim(pick_all, pair, 0, keepdims=False)
        place = lax.dynamic_index_in_dim(place_all, pair, 0, keepdims=False)
        route_ids = lax.dynamic_index_in_dim(ids_all, pair, 0, keepdims=False)
        hidden = jnp.where(section_pos == 0, entering[min(tick, pairs - 1)], arriving)
        wide = hidden.astype(jnp.float32)
        inv_rms = lax.rsqrt(jnp.mean(wide * wide, axis=-1, keepdims=True) + EPSILON)
        normed = (wide * inv_rms * gain_row).astype(jnp.bfloat16)
        sent = jnp.dot(pick, normed, preferred_element_type=jnp.float32).astype(jnp.bfloat16)
        own = gather_over(sent, SLICES, 8).reshape(8 * sent.shape[0], width)
        other = lax.ppermute(own, "expert", CORES)
        other_out = lax.ppermute(ffn(other), "expert", CORES)
        own_out = ffn(own)
        both = (own_out.astype(jnp.float32) + other_out.astype(jnp.float32)).astype(jnp.bfloat16)
        parts = lax.all_to_all(
            both.reshape(8, sent.shape[0], width),
            "expert",
            split_axis=0,
            concat_axis=0,
            axis_index_groups=SLICES,
            tiled=True,
        )
        expert_out = jnp.sum(parts.astype(jnp.float32), axis=0).astype(jnp.bfloat16)
        outs = gather_over(expert_out, EXPERTS, E).reshape(E * sent.shape[0], width)
        logits = jnp.dot(normed, router_mat, preferred_element_type=jnp.float32)
        match = route_ids[:, :, None] == jnp.arange(E, dtype=jnp.int32)[None, None, :]
        chosen = jnp.sum(jnp.where(match, logits[:, None, :], 0.0), axis=-1)
        share = jax.nn.sigmoid(chosen[:, 0] - chosen[:, 1])[:, None]
        routed = jnp.dot(place, outs, preferred_element_type=jnp.float32)
        result = (wide + share * routed[:held] + (1.0 - share) * routed[held:]).astype(jnp.bfloat16)
        mine = lax.dynamic_index_in_dim(
            result.reshape(PAIR, E, tokens, width), expert, 1, keepdims=False
        )
        kept.append(mine)
        if tick + 1 < pairs + sections - 1:
            arriving = lax.ppermute(
                result, "section", [(i, i + 1) for i in range(sections - 1)]
            )
    stored = lax.dynamic_slice_in_dim(jnp.stack(kept), section_pos, pairs, 0)
    return stored.reshape(1, micro_count, tokens, width)


def solution(mesh):
    placed = (
        P(None, "expert", None),
        P("section", None, None, None),
        P("section", None),
        P("section", None, None),
        P("section", None, "expert"),
        P("section", None, "expert"),
        P("section", "expert", None),
    )
    return jax.shard_map(
        on_device,
        mesh=mesh,
        in_specs=placed,
        out_specs=P("section", None, "expert", None),
        check_vma=False,
    )
```

time: 591 us -> 424 us (0.72); the launches traced: 581 us -> 421 us
  waiting for transfers between devices: 222 us -> 109 us
  local copies, waits for them, and re-layouts: 66.1 us -> 36.1 us
  starting transfers between devices: 79 us -> 50.9 us
  matrix products: 53.4 us -> 77.5 us
  other arithmetic: 37 us -> 16.3 us
  blocking collectives: 122 us -> 131 us
    all_to_all x10 -> x8, waiting for transfers between devices: 214 us -> 84.4 us  [the longest x6 63.5 us: gather_over(): lax.all_to_all(copies, 'expert', split_axis=0, concat_axis=0, axis_index_...]
    reshape x42 -> x7, local copies, waits for them, and re-layouts: 42.3 us -> 3.07 us  [the longest x5 2.32 us: on_device(): result.reshape(PAIR, E, tokens, width)]
    dot_general x28 -> x35, matrix products: 53.4 us -> 77.5 us  [the longest x10 42.9 us: ffn(): jnp.dot(hidden, down_mat, preferred_element_type=jnp.float32)]
    all_to_all x10 -> x8, starting transfers between devices: 59.8 us -> 37.5 us  [the longest x6 29 us: gather_over(): lax.all_to_all(copies, 'expert', split_axis=0, concat_axis=0, axis_index_...]
    ppermute x6 -> x14, waiting for transfers between devices: 8.43 us -> 24.6 us  [the longest x4 14.5 us: on_device(): lax.ppermute(result, 'section', [(i, i + 1) for i in range(sections - 1)])]
    unnamed x82 -> x89, local copies, waits for them, and re-layouts: 1.27 us -> 16 us
    all_to_all x4 -> x8, blocking collectives: 122 us -> 131 us  [the longest x5 77.4 us: gather_over(): lax.all_to_all(copies, 'expert', split_axis=0, concat_axis=0, axis_index_...]
    and x7 -> x0, other arithmetic: 6.7 us -> none  [collect(): return jnp.take(merged.reshape(E * MOST, model_width), target, axis=0)]
  transfers between devices with their start and end apart: 16 -> 22, of which waited for: 16 -> 17; matrix products, arithmetic and copies ran while one was open for 4% -> 9% of each run, Pallas kernels for 0% -> 0%
where the time goes in v1:
time: 424 us; the launch traced here: 421 us
  blocking collectives  131 us (31%)
  waiting for transfers between devices  109 us (26%)
  matrix products  77.5 us (18%)
  starting transfers between devices  50.9 us (12%)
  local copies, waits for them, and re-layouts  36.1 us (9%)
  other arithmetic  16.3 us (4%)
    all_to_all x5, blocking collectives, gather_over(): lax.all_to_all(copies, 'expert', split_axis=0, concat_axis=0, axis_index_...  77.4 us
    all_to_all x6, waiting for transfers between devices, gather_over(): lax.all_to_all(copies, 'expert', split_axis=0, concat_axis=0, axis_index_...  63.5 us
    all_to_all x3, blocking collectives, on_device(): lax.all_to_all(both.reshape(8, sent.shape[0], width), 'expert', split_axi...  53.2 us
    dot_general x10, matrix products, ffn(): jnp.dot(hidden, down_mat, preferred_element_type=jnp.float32)  42.9 us
    all_to_all x6, starting transfers between devices, gather_over(): lax.all_to_all(copies, 'expert', split_axis=0, concat_axis=0, axis_index_...  29 us
    all_to_all x2, waiting for transfers between devices, on_device(): lax.all_to_all(both.reshape(8, sent.shape[0], width), 'expert', split_axi...  20.9 us
    unnamed x89, local copies, waits for them, and re-layouts  16 us
    ppermute x4, waiting for transfers between devices, on_device(): lax.ppermute(result, 'section', [(i, i + 1) for i in range(sections - 1)])  14.5 us
  transfers between devices with their start and end apart: 22, of which 17 were waited for; matrix products, arithmetic and copies ran while one was open for 9% of the time, Pallas kernels for 0%

profile of v1, /device:TPU:16, one launch (start us, length us, event | category | flops | bytes accessed | tf_op | source)
XLA Modules:
  0.0 421.1 jit_solution(7431309327178708295)
XLA Ops:
  2.0 8.5 %all-to-all-start = ((bf16[4,12,3072]{2,1,0:T(8,128)(2,1)}), bf16[4,12,3072]{2,1,0:T(8,128)(2,1)}, u32[]{:S(2)}, u32[]{:S(2)}) async-start(bf16[4,12,3072]{2,1,0:T(8,128)(2,1)} %broadcast_in_dim.67), calls=%async_computation | async-start | bytes 786432 | tf_op jit(solution)/shard_map/all_to_all | solution.py:18
  12.3 11.4 %all-to-all-done = bf16[4,12,3072]{2,1,0:T(8,128)(2,1)} async-done(((bf16[4,12,3072]{2,1,0:T(8,128)(2,1)}), bf16[4,12,3072]{2,1,0:T(8,128)(2,1)}, u32[]{:S(2)}, u32[]{:S(2)}) %all-to-all-start) | async-done | bytes 294944 | tf_op jit(solution)/shard_map/all_to_all | solution.py:18
  29.6 15.1 %all_to_all.80 = bf16[8,16,3072]{2,1,0:T(8,128)(2,1)S(1)} all-to-all(bf16[8,16,3072]{2,1,0:T(8,128)(2,1)S(1)} %broadcast_in_dim.72), channel_id=1, replica_groups={{0,2,4,6,8,10,12,14},{1,3,5,7,9,11,13,15},{16,18,20,22,24,26,28,30},{17..., dimensions={0} | all-to-all | bytes 1572864 | tf_op jit(solution)/shard_map/all_to_all | solution.py:18
  52.0 4.2 convolution_convert_fusion.8
  59.8 4.4 %add_convert_fusion.4 = bf16[128,3072]{1,0:T(8,128)(2,1)} fusion(bf16[128,3072]{1,0:T(8,128)(2,1)} %collective-permute-done.1, bf16[1,512,3072]{2,1,0:T(8,128)(2,1)S(1)} %copy-done, bf16[128,3072]{1,0:T(8,128)(2,1)} %bitcast.267, bf16[1,3072,512]{2,1,0:T(8,128)(2,1)} %param.12, f32[128,512]{1,0:T(8,128)} %fusion.53), kind=kOutput, calls=%fused_computation.74 | convolution fusion | flops 807665664 | bytes 8912896 | tf_op jit(solution)/shard_map/dot_general | solution.py:56
  64.2 4.2 %all-to-all-start.2 = ((bf16[8,16,3072]{2,1,0:T(8,128)(2,1)}), bf16[8,16,3072]{2,1,0:T(8,128)(2,1)}, u32[]{:S(2)}, u32[]{:S(2)}) async-start(bf16[8,16,3072]{2,1,0:T(8,128)(2,1)} %bitcast.277), calls=%async_computation.2 | async-start | bytes 1572864 | tf_op jit(solution)/shard_map/all_to_all | solution.py:84
  69.2 12.0 %all-to-all-done.2 = bf16[8,16,3072]{2,1,0:T(8,128)(2,1)} async-done(((bf16[8,16,3072]{2,1,0:T(8,128)(2,1)}), bf16[8,16,3072]{2,1,0:T(8,128)(2,1)}, u32[]{:S(2)}, u32[]{:S(2)}) %all-to-all-start.2) | async-done | bytes 786464 | tf_op jit(solution)/shard_map/all_to_all | solution.py:84
  91.0 9.7 %all-to-all-done.3 = bf16[4,16,3072]{2,1,0:T(8,128)(2,1)} async-done(((bf16[4,16,3072]{2,1,0:T(8,128)(2,1)}), bf16[4,16,3072]{2,1,0:T(8,128)(2,1)}, u32[]{:S(2)}, u32[]{:S(2)}) %all-to-all-start.3) | async-done | bytes 393248 | tf_op jit(solution)/shard_map/all_to_all | solution.py:18
  113.1 15.0 %all_to_all.81 = bf16[8,16,3072]{2,1,0:T(8,128)(2,1)S(1)} all-to-all(bf16[8,16,3072]{2,1,0:T(8,128)(2,1)S(1)} %broadcast_in_dim.75), channel_id=1, replica_groups={{0,2,4,6,8,10,12,14},{1,3,5,7,9,11,13,15},{16,18,20,22,24,26,28,30},{17..., dimensions={0} | all-to-all | bytes 1572864 | tf_op jit(solution)/shard_map/all_to_all | solution.py:18
  132.8 4.2 %convolution_convert_fusion.6 = bf16[128,3072]{1,0:T(8,128)(2,1)} fusion(bf16[1,512,3072]{2,1,0:T(8,128)(2,1)S(1)} %copy-done, f32[128,512]{1,0:T(8,128)S(1)} %fusion.27, bf16[128,3072]{1,0:T(8,128)(2,1)} %copy-done.9, bf16[1,3072,512]{2,1,0:T(8,128)(2,1)} %param.11), kind=kOutput, calls=%fused_computation.6 | convolution fusion | flops 806092800 | bytes 8126464 | tf_op jit(solution)/shard_map/dot_general | solution.py:56
  139.9 4.3 %add_convert_fusion.3 = bf16[128,3072]{1,0:T(8,128)(2,1)} fusion(bf16[128,3072]{1,0:T(8,128)(2,1)} %collective-permute-done.4, bf16[1,512,3072]{2,1,0:T(8,128)(2,1)S(1)} %copy-done, bf16[128,3072]{1,0:T(8,128)(2,1)} %bitcast.270, bf16[1,3072,512]{2,1,0:T(8,128)(2,1)} %param.12, f32[128,512]{1,0:T(8,128)S(1)} %fusion.49), kind=kOutput, calls=%fused_computation.73 | convolution fusion | flops 807665664 | bytes 8912896 | tf_op jit(solution)/shard_map/dot_general | solution.py:56
  144.3 17.7 %all_to_all.82 = bf16[8,16,3072]{2,1,0:T(8,128)(2,1)} all-to-all(bf16[8,16,3072]{2,1,0:T(8,128)(2,1)} %bitcast.279), channel_id=1, replica_groups={{0,2,4,6,8,10,12,14},{1,3,5,7,9,11,13,15},{16,18,20,22,24,26,28,30},{17..., dimensions={0} | all-to-all | bytes 1572864 | tf_op jit(solution)/shard_map/all_to_all | solution.py:84
  164.0 4.2 %all-to-all-start.6 = ((bf16[4,16,3072]{2,1,0:T(8,128)(2,1)}), bf16[4,16,3072]{2,1,0:T(8,128)(2,1)}, u32[]{:S(2)}, u32[]{:S(2)}) async-start(bf16[4,16,3072]{2,1,0:T(8,128)(2,1)} %broadcast_in_dim.76), calls=%async_computation.6 | async-start | bytes 786432 | tf_op jit(solution)/shard_map/all_to_all | solution.py:18
  170.0 10.6 %all-to-all-done.6 = bf16[4,16,3072]{2,1,0:T(8,128)(2,1)} async-done(((bf16[4,16,3072]{2,1,0:T(8,128)(2,1)}), bf16[4,16,3072]{2,1,0:T(8,128)(2,1)}, u32[]{:S(2)}, u32[]{:S(2)}) %all-to-all-start.6) | async-done | bytes 393248 | tf_op jit(solution)/shard_map/all_to_all | solution.py:18
  190.4 15.7 %all_to_all.83 = bf16[8,16,3072]{2,1,0:T(8,128)(2,1)S(1)} all-to-all(bf16[8,16,3072]{2,1,0:T(8,128)(2,1)S(1)} %broadcast_in_dim.78), channel_id=1, replica_groups={{0,2,4,6,8,10,12,14},{1,3,5,7,9,11,13,15},{16,18,20,22,24,26,28,30},{17..., dimensions={0} | all-to-all | bytes 1572864 | tf_op jit(solution)/shard_map/all_to_all | solution.py:18
  210.8 4.2 %convolution_convert_fusion.4 = bf16[128,3072]{1,0:T(8,128)(2,1)} fusion(bf16[1,512,3072]{2,1,0:T(8,128)(2,1)S(1)} %copy-done, f32[128,512]{1,0:T(8,128)S(1)} %fusion.23, bf16[128,3072]{1,0:T(8,128)(2,1)} %copy-done.10, bf16[1,3072,512]{2,1,0:T(8,128)(2,1)} %param.11), kind=kOutput, calls=%fused_computation.4 | convolution fusion | flops 806092800 | bytes 8126464 | tf_op jit(solution)/shard_map/dot_general | solution.py:56
  217.9 4.3 %add_convert_fusion.2 = bf16[128,3072]{1,0:T(8,128)(2,1)} fusion(bf16[128,3072]{1,0:T(8,128)(2,1)} %collective-permute-done.7, bf16[1,512,3072]{2,1,0:T(8,128)(2,1)S(1)} %copy-done, bf16[128,3072]{1,0:T(8,128)(2,1)} %bitcast.273, bf16[1,3072,512]{2,1,0:T(8,128)(2,1)} %param.12, f32[128,512]{1,0:T(8,128)S(1)} %fusion.45), kind=kOutput, calls=%fused_computation.72 | convolution fusion | flops 807665664 | bytes 8912896 | tf_op jit(solution)/shard_map/dot_general | solution.py:56
  222.2 17.7 %all_to_all.84 = bf16[8,16,3072]{2,1,0:T(8,128)(2,1)} all-to-all(bf16[8,16,3072]{2,1,0:T(8,128)(2,1)} %bitcast.280), channel_id=1, replica_groups={{0,2,4,6,8,10,12,14},{1,3,5,7,9,11,13,15},{16,18,20,22,24,26,28,30},{17..., dimensions={0} | all-to-all | bytes 1572864 | tf_op jit(solution)/shard_map/all_to_all | solution.py:84
  242.0 4.2 %all-to-all-start.9 = ((bf16[4,16,3072]{2,1,0:T(8,128)(2,1)}), bf16[4,16,3072]{2,1,0:T(8,128)(2,1)}, u32[]{:S(2)}, u32[]{:S(2)}) async-start(bf16[4,16,3072]{2,1,0:T(8,128)(2,1)} %broadcast_in_dim.79), calls=%async_computation.9 | async-start | bytes 786432 | tf_op jit(solution)/shard_map/all_to_all | solution.py:18
  247.9 10.7 %all-to-all-done.9 = bf16[4,16,3072]{2,1,0:T(8,128)(2,1)} async-done(((bf16[4,16,3072]{2,1,0:T(8,128)(2,1)}), bf16[4,16,3072]{2,1,0:T(8,128)(2,1)}, u32[]{:S(2)}, u32[]{:S(2)}) %all-to-all-start.9) | async-done | bytes 393248 | tf_op jit(solution)/shard_map/all_to_all | solution.py:18
  268.3 15.8 %all_to_all.85 = bf16[8,16,3072]{2,1,0:T(8,128)(2,1)S(1)} all-to-all(bf16[8,16,3072]{2,1,0:T(8,128)(2,1)S(1)} %broadcast_in_dim.81), channel_id=1, replica_groups={{0,2,4,6,8,10,12,14},{1,3,5,7,9,11,13,15},{16,18,20,22,24,26,28,30},{17..., dimensions={0} | all-to-all | bytes 1572864 | tf_op jit(solution)/shard_map/all_to_all | solution.py:18
  288.8 4.2 %convolution_convert_fusion.2 = bf16[128,3072]{1,0:T(8,128)(2,1)} fusion(bf16[1,512,3072]{2,1,0:T(8,128)(2,1)S(1)} %copy-done, f32[128,512]{1,0:T(8,128)S(1)} %fusion.19, bf16[128,3072]{1,0:T(8,128)(2,1)} %copy-done.11, bf16[1,3072,512]{2,1,0:T(8,128)(2,1)} %param.11), kind=kOutput, calls=%fused_computation.2 | convolution fusion | flops 806092800 | bytes 8126464 | tf_op jit(solution)/shard_map/dot_general | solution.py:56
  295.9 4.3 %add_convert_fusion.1 = bf16[128,3072]{1,0:T(8,128)(2,1)} fusion(bf16[128,3072]{1,0:T(8,128)(2,1)} %collective-permute-done.10, bf16[1,512,3072]{2,1,0:T(8,128)(2,1)S(1)} %copy-done, bf16[128,3072]{1,0:T(8,128)(2,1)} %bitcast.276, bf16[1,3072,512]{2,1,0:T(8,128)(2,1)} %param.12, f32[128,512]{1,0:T(8,128)S(1)} %fusion.41), kind=kOutput, calls=%fused_computation.71 | convolution fusion | flops 807665664 | bytes 8912896 | tf_op jit(solution)/shard_map/dot_general | solution.py:56
  300.3 17.7 %all_to_all.86 = bf16[8,16,3072]{2,1,0:T(8,128)(2,1)} all-to-all(bf16[8,16,3072]{2,1,0:T(8,128)(2,1)} %bitcast.281), channel_id=1, replica_groups={{0,2,4,6,8,10,12,14},{1,3,5,7,9,11,13,15},{16,18,20,22,24,26,28,30},{17..., dimensions={0} | all-to-all | bytes 1572864 | tf_op jit(solution)/shard_map/all_to_all | solution.py:84
  320.0 4.2 %all-to-all-start.12 = ((bf16[4,16,3072]{2,1,0:T(8,128)(2,1)}), bf16[4,16,3072]{2,1,0:T(8,128)(2,1)}, u32[]{:S(2)}, u32[]{:S(2)}) async-start(bf16[4,16,3072]{2,1,0:T(8,128)(2,1)} %broadcast_in_dim.82), calls=%async_computation.12 | async-start | bytes 786432 | tf_op jit(solution)/shard_map/all_to_all | solution.py:18
  325.9 10.7 %all-to-all-done.12 = bf16[4,16,3072]{2,1,0:T(8,128)(2,1)} async-done(((bf16[4,16,3072]{2,1,0:T(8,128)(2,1)}), bf16[4,16,3072]{2,1,0:T(8,128)(2,1)}, u32[]{:S(2)}, u32[]{:S(2)}) %all-to-all-start.12) | async-done | bytes 393248 | tf_op jit(solution)/shard_map/all_to_all | solution.py:18
  346.2 15.8 %all_to_all.87 = bf16[8,16,3072]{2,1,0:T(8,128)(2,1)} all-to-all(bf16[8,16,3072]{2,1,0:T(8,128)(2,1)S(1)} %broadcast_in_dim.84), channel_id=1, replica_groups={{0,2,4,6,8,10,12,14},{1,3,5,7,9,11,13,15},{16,18,20,22,24,26,28,30},{17..., dimensions={0} | all-to-all | bytes 1572864 | tf_op jit(solution)/shard_map/all_to_all | solution.py:18
  367.4 4.3 %convolution_convert_fusion = bf16[128,3072]{1,0:T(8,128)(2,1)} fusion(bf16[1,512,3072]{2,1,0:T(8,128)(2,1)S(1)} %copy-done, f32[128,512]{1,0:T(8,128)S(1)} %fusion.15, bf16[128,3072]{1,0:T(8,128)(2,1)} %collective-permute-done.12, bf16[1,3072,512]{2,1,0:T(8,128)(2,1)} %param.11), kind=kOutput, calls=%fused_computation | convolution fusion | flops 806092800 | bytes 8126464 | tf_op jit(solution)/shard_map/dot_general | solution.py:56
  376.7 4.4 %add_convert_fusion = bf16[128,3072]{1,0:T(8,128)(2,1)} fusion(bf16[128,3072]{1,0:T(8,128)(2,1)} %collective-permute-done.13, bf16[1,512,3072]{2,1,0:T(8,128)(2,1)S(1)} %copy-done, bf16[128,3072]{1,0:T(8,128)(2,1)} %bitcast.49, bf16[1,3072,512]{2,1,0:T(8,128)(2,1)} %param.12, f32[128,512]{1,0:T(8,128)S(1)} %fusion.37), kind=kOutput, calls=%fused_computation.70 | convolution fusion | flops 807665664 | bytes 8912896 | tf_op jit(solution)/shard_map/dot_general | solution.py:56
  381.1 4.2 all-to-all-start.14
  389.3 8.9 %all-to-all-done.14 = bf16[8,16,3072]{2,1,0:T(8,128)(2,1)} async-done(((bf16[8,16,3072]{2,1,0:T(8,128)(2,1)}), bf16[8,16,3072]{2,1,0:T(8,128)(2,1)}, u32[]{:S(2)}, u32[]{:S(2)}) %all-to-all-start.14) | async-done | bytes 786464 | tf_op jit(solution)/shard_map/all_to_all | solution.py:84
  407.1 10.2 %all-to-all-done.15 = bf16[4,16,3072]{2,1,0:T(8,128)(2,1)S(1)} async-done(((bf16[4,16,3072]{2,1,0:T(8,128)(2,1)}), bf16[4,16,3072]{2,1,0:T(8,128)(2,1)S(1)}, u32[]{:S(2)}, u32[]{:S(2)}) %all-to-all-start.15) | async-done | bytes 393248 | tf_op jit(solution)/shard_map/all_to_all | solution.py:18
  (228 shorter events, 132.8 us)
Async XLA Ops:
  0.0 52.0 %copy-start = (bf16[1,512,3072]{2,1,0:T(8,128)(2,1)S(1)}, bf16[1,512,3072]{2,1,0:T(8,128)(2,1)}, u32[]{:S(2)}) copy-start(bf16[1,512,3072]{2,1,0:T(8,128)(2,1)} %param.13) | copy-start | bytes 9437188
  2.0 21.7 %all-to-all-start = ((bf16[4,12,3072]{2,1,0:T(8,128)(2,1)}), bf16[4,12,3072]{2,1,0:T(8,128)(2,1)}, u32[]{:S(2)}, u32[]{:S(2)}) async-start(bf16[4,12,3072]{2,1,0:T(8,128)(2,1)} %broadcast_in_dim.67), calls=%async_computation | async-start | bytes 786432 | tf_op jit(solution)/shard_map/all_to_all | solution.py:18
  12.2 99.9 %copy-start.33 = (pred[2,16,24]{2,1,0:T(8,128)(4,1)}, pred[2,16,24]{2,1,0:T(8,128)(4,1)S(1)}, u32[]{:S(2)}) copy-start(pred[2,16,24]{2,1,0:T(8,128)(4,1)S(1)} %fusion.207) | copy-start | bytes 2308
  45.6 2.3 collective-permute-start
  56.2 3.6 collective-permute-start.1
  64.2 17.0 %all-to-all-start.2 = ((bf16[8,16,3072]{2,1,0:T(8,128)(2,1)}), bf16[8,16,3072]{2,1,0:T(8,128)(2,1)}, u32[]{:S(2)}, u32[]{:S(2)}) async-start(bf16[8,16,3072]{2,1,0:T(8,128)(2,1)} %bitcast.277), calls=%async_computation.2 | async-start | bytes 1572864 | tf_op jit(solution)/shard_map/all_to_all | solution.py:84
  69.2 34.5 %copy-start.24 = (pred[2,48,64]{2,1,0:T(8,128)(4,1)}, pred[2,48,64]{2,1,0:T(8,128)(4,1)S(1)}, u32[]{:S(2)}) copy-start(pred[2,48,64]{2,1,0:T(8,128)(4,1)S(1)} %iota_compare_fusion) | copy-start | bytes 18436
  83.3 17.5 %all-to-all-start.3 = ((bf16[4,16,3072]{2,1,0:T(8,128)(2,1)}), bf16[4,16,3072]{2,1,0:T(8,128)(2,1)}, u32[]{:S(2)}, u32[]{:S(2)}) async-start(bf16[4,16,3072]{2,1,0:T(8,128)(2,1)} %broadcast_in_dim.73), calls=%async_computation.3 | async-start | bytes 786432 | tf_op jit(solution)/shard_map/all_to_all | solution.py:18
  103.7 7.3 %collective-permute-start.2 = (bf16[24,3072]{1,0:T(8,128)(2,1)}, bf16[24,3072]{1,0:T(8,128)(2,1)}, u32[]{:S(2)}, u32[]{:S(2)}) collective-permute-start(bf16[24,3072]{1,0:T(8,128)(2,1)} %fusion.136), channel_id=1, source_target_pairs={{0,64},{64,128},{128,192},{1,65},{65,129},{129,193},{2,66},{66,130... | collective-permute-start | bytes 442376 | tf_op jit(solution)/shard_map/ppermute | solution.py:105
  129.0 2.3 collective-permute-start.3
  137.1 2.9 collective-permute-start.4
  144.3 36.4 %copy-start.25 = (pred[2,48,64]{2,1,0:T(8,128)(4,1)S(1)}, pred[2,48,64]{2,1,0:T(8,128)(4,1)}, u32[]{:S(2)}) copy-start(pred[2,48,64]{2,1,0:T(8,128)(4,1)} %copy-done.24) | copy-start | bytes 18436
  144.3 45.8 %copy-start.34 = (pred[2,16,24]{2,1,0:T(8,128)(4,1)S(1)}, pred[2,16,24]{2,1,0:T(8,128)(4,1)}, u32[]{:S(2)}) copy-start(pred[2,16,24]{2,1,0:T(8,128)(4,1)} %copy-done.33) | copy-start | bytes 2308
  164.0 16.6 %all-to-all-start.6 = ((bf16[4,16,3072]{2,1,0:T(8,128)(2,1)}), bf16[4,16,3072]{2,1,0:T(8,128)(2,1)}, u32[]{:S(2)}, u32[]{:S(2)}) async-start(bf16[4,16,3072]{2,1,0:T(8,128)(2,1)} %broadcast_in_dim.76), calls=%async_computation.6 | async-start | bytes 786432 | tf_op jit(solution)/shard_map/all_to_all | solution.py:18
  182.2 7.0 %collective-permute-start.5 = (bf16[24,3072]{1,0:T(8,128)(2,1)S(1)}, bf16[24,3072]{1,0:T(8,128)(2,1)S(1)}, u32[]{:S(2)}, u32[]{:S(2)}) collective-permute-start(bf16[24,3072]{1,0:T(8,128)(2,1)S(1)} %fusion.119), channel_id=1, source_target_pairs={{0,64},{64,128},{128,192},{1,65},{65,129},{129,193},{2,66},{66,130... | collective-permute-start | bytes 442376 | tf_op jit(solution)/shard_map/ppermute | solution.py:105
  207.0 2.3 collective-permute-start.6
  215.0 2.9 collective-permute-start.7
  222.2 36.4 %copy-start.26 = (pred[2,48,64]{2,1,0:T(8,128)(4,1)S(1)}, pred[2,48,64]{2,1,0:T(8,128)(4,1)}, u32[]{:S(2)}) copy-start(pred[2,48,64]{2,1,0:T(8,128)(4,1)} %copy-done.24) | copy-start | bytes 18436
  222.2 45.8 %copy-start.35 = (pred[2,16,24]{2,1,0:T(8,128)(4,1)S(1)}, pred[2,16,24]{2,1,0:T(8,128)(4,1)}, u32[]{:S(2)}) copy-start(pred[2,16,24]{2,1,0:T(8,128)(4,1)} %copy-done.33) | copy-start | bytes 2308
  242.0 16.6 %all-to-all-start.9 = ((bf16[4,16,3072]{2,1,0:T(8,128)(2,1)}), bf16[4,16,3072]{2,1,0:T(8,128)(2,1)}, u32[]{:S(2)}, u32[]{:S(2)}) async-start(bf16[4,16,3072]{2,1,0:T(8,128)(2,1)} %broadcast_in_dim.79), calls=%async_computation.9 | async-start | bytes 786432 | tf_op jit(solution)/shard_map/all_to_all | solution.py:18
  260.1 7.0 %collective-permute-start.8 = (bf16[24,3072]{1,0:T(8,128)(2,1)S(1)}, bf16[24,3072]{1,0:T(8,128)(2,1)S(1)}, u32[]{:S(2)}, u32[]{:S(2)}) collective-permute-start(bf16[24,3072]{1,0:T(8,128)(2,1)S(1)} %fusion.124), channel_id=1, source_target_pairs={{0,64},{64,128},{128,192},{1,65},{65,129},{129,193},{2,66},{66,130... | collective-permute-start | bytes 442376 | tf_op jit(solution)/shard_map/ppermute | solution.py:105
  285.0 2.3 collective-permute-start.9
  293.0 2.9 collective-permute-start.10
  300.3 36.4 %copy-start.27 = (pred[2,48,64]{2,1,0:T(8,128)(4,1)S(1)}, pred[2,48,64]{2,1,0:T(8,128)(4,1)}, u32[]{:S(2)}) copy-start(pred[2,48,64]{2,1,0:T(8,128)(4,1)} %copy-done.24) | copy-start | bytes 18436
  300.3 45.6 %copy-start.36 = (pred[2,16,24]{2,1,0:T(8,128)(4,1)S(1)}, pred[2,16,24]{2,1,0:T(8,128)(4,1)}, u32[]{:S(2)}) copy-start(pred[2,16,24]{2,1,0:T(8,128)(4,1)} %copy-done.33) | copy-start | bytes 2308
  320.0 16.6 %all-to-all-start.12 = ((bf16[4,16,3072]{2,1,0:T(8,128)(2,1)}), bf16[4,16,3072]{2,1,0:T(8,128)(2,1)}, u32[]{:S(2)}, u32[]{:S(2)}) async-start(bf16[4,16,3072]{2,1,0:T(8,128)(2,1)} %broadcast_in_dim.82), calls=%async_computation.12 | async-start | bytes 786432 | tf_op jit(solution)/shard_map/all_to_all | solution.py:18
  338.0 7.0 %collective-permute-start.11 = (bf16[24,3072]{1,0:T(8,128)(2,1)S(1)}, bf16[24,3072]{1,0:T(8,128)(2,1)S(1)}, u32[]{:S(2)}, u32[]{:S(2)}) collective-permute-start(bf16[24,3072]{1,0:T(8,128)(2,1)S(1)} %fusion.129), channel_id=1, source_target_pairs={{0,64},{64,128},{128,192},{1,65},{65,129},{129,193},{2,66},{66,130... | collective-permute-start | bytes 442376 | tf_op jit(solution)/shard_map/ppermute | solution.py:105
  362.0 2.6 collective-permute-start.12
  371.7 5.1 %collective-permute-start.13 = (bf16[128,3072]{1,0:T(8,128)(2,1)}, bf16[128,3072]{1,0:T(8,128)(2,1)}, u32[]{:S(2)}, u32[]{:S(2)}) collective-permute-start(bf16[128,3072]{1,0:T(8,128)(2,1)} %convolution_convert_fusion), channel_id=1, source_target_pairs={{0,1},{1,0},{2,3},{3,2},{4,5},{5,4},{6,7},{7,6},{8,9},{9,8},{10,11... | collective-permute-start | bytes 2359304 | tf_op jit(solution)/shard_map/ppermute | solution.py:81
  381.1 17.0 %all-to-all-start.14 = ((bf16[8,16,3072]{2,1,0:T(8,128)(2,1)}), bf16[8,16,3072]{2,1,0:T(8,128)(2,1)}, u32[]{:S(2)}, u32[]{:S(2)}) async-start(bf16[8,16,3072]{2,1,0:T(8,128)(2,1)} %bitcast.278), calls=%async_computation.14 | async-start | bytes 1572864 | tf_op jit(solution)/shard_map/all_to_all | solution.py:84
  386.9 30.4 %copy-start.28 = (pred[2,48,64]{2,1,0:T(8,128)(4,1)S(1)}, pred[2,48,64]{2,1,0:T(8,128)(4,1)}, u32[]{:S(2)}) copy-start(pred[2,48,64]{2,1,0:T(8,128)(4,1)} %copy-done.24) | copy-start | bytes 18436
  400.2 17.2 %all-to-all-start.15 = ((bf16[4,16,3072]{2,1,0:T(8,128)(2,1)}), bf16[4,16,3072]{2,1,0:T(8,128)(2,1)S(1)}, u32[]{:S(2)}, u32[]{:S(2)}) async-start(bf16[4,16,3072]{2,1,0:T(8,128)(2,1)} %broadcast_in_dim.160), calls=%async_computation.15 | async-start | bytes 786432 | tf_op jit(solution)/shard_map/all_to_all | solution.py:18
  (32 other events, 395.8 us)

commit v2 on v1

v2 whole, which is shorter than its diff:
```python
import jax
import jax.numpy as jnp
from jax import lax
from jax.sharding import PartitionSpec as P

E = 4
MOST = 2
PAIR = 2
SHARERS = 8
EPSILON = 1e-05

SLICES = [[e * 16 + j * 2 + c for j in range(8)] for e in range(E) for c in range(2)]
EXPERTS = [[e * 16 + r for e in range(E)] for r in range(16)]
CORES = [(i, i ^ 1) for i in range(64)]


def exchange(block, groups, count):
    rows = block.shape[0] // count
    chunks = block.reshape(count, rows, block.shape[1])
    moved = lax.all_to_all(
        chunks, "expert", split_axis=0, concat_axis=0, axis_index_groups=groups, tiled=True
    )
    return moved.reshape(block.shape)


def choose(picks, rows):
    return jnp.dot(picks, rows, preferred_element_type=jnp.float32)


def tables(ids, expert):
    pairs, tokens = ids.shape[0], ids.shape[3]
    blocks = PAIR * E
    flat = ids.reshape(pairs, blocks, tokens * 2)
    same = flat[..., :, None] == flat[..., None, :]
    earlier = jnp.arange(tokens * 2)[:, None] > jnp.arange(tokens * 2)[None, :]
    slot = jnp.sum((same & earlier).astype(jnp.int32), axis=-1)
    block = jnp.arange(blocks, dtype=jnp.int32)[None, :, None]
    row = block * MOST + slot
    rows = blocks * MOST
    mine = jnp.where(flat == expert, row, -1).reshape(pairs, 1, blocks * tokens, 2)
    wanted = jnp.arange(SHARERS * rows, dtype=jnp.int32)[None, :, None, None] % rows
    pick = jnp.any(mine == wanted, axis=-1)
    back = (flat * rows + row).reshape(pairs, blocks * tokens, 2)
    back = jnp.swapaxes(back, 1, 2).reshape(pairs, 2 * blocks * tokens, 1)
    place = back == jnp.arange(E * rows, dtype=jnp.int32)[None, None, :]
    named = ids.reshape(pairs, blocks * tokens, 2)[..., None] == jnp.arange(E, dtype=jnp.int32)
    sign = named[:, :, 0].astype(jnp.float32) - named[:, :, 1].astype(jnp.float32)
    return pick.astype(jnp.bfloat16), place.astype(jnp.bfloat16), sign


def on_device(inputs, routes, norm_gain, router, w_gate, w_up, w_down):
    barrier = lax.optimization_barrier
    sections = lax.axis_size("section")
    section_pos = lax.axis_index("section")
    member_pos = lax.axis_index("expert")
    expert, rest = member_pos // 16, member_pos % 16
    micro_count, tokens, width = inputs.shape
    pairs = micro_count // PAIR
    held = PAIR * E * tokens
    sent_rows = PAIR * E * MOST
    ticks = pairs + sections - 1
    gain_row, router_mat = norm_gain[0], router[0]
    gate_mat, up_mat, down_mat = w_gate[0], w_up[0], w_down[0]

    def hidden_units(rows):
        gate_value = jnp.dot(rows, gate_mat, preferred_element_type=jnp.float32)
        up_value = jnp.dot(rows, up_mat, preferred_element_type=jnp.float32)
        gate_value, up_value = barrier((gate_value, up_value))
        return barrier((jax.nn.silu(gate_value) * up_value).astype(jnp.bfloat16))

    def project(units):
        return barrier(
            jnp.dot(units, down_mat, preferred_element_type=jnp.float32).astype(jnp.bfloat16)
        )

    ids = routes[0].reshape(pairs, PAIR, E, 16, tokens, 2)
    ids = lax.dynamic_index_in_dim(ids, rest, 3, keepdims=False)
    pick_all, place_all, sign_all = tables(ids, expert)

    spare = 16
    own_rows = jnp.swapaxes(inputs, 0, 1).reshape(tokens * micro_count, width)
    lay_out = (
        jnp.arange(E * spare, dtype=jnp.int32)[:, None] % spare
        == jnp.arange(tokens * micro_count, dtype=jnp.int32)[None, :]
    ).astype(jnp.bfloat16)
    entering = exchange(choose(lay_out, own_rows).astype(jnp.bfloat16), EXPERTS, E)
    spot = jnp.arange(held, dtype=jnp.int32)
    spot_micro, spot_block, spot_token = (
        spot // (E * tokens),
        spot // tokens % E,
        spot % tokens,
    )

    def entrance(pair):
        source = spot_block * spare + spot_token * micro_count + pair * PAIR + spot_micro
        picks = source[:, None] == jnp.arange(E * spare, dtype=jnp.int32)[None, :]
        return choose(picks.astype(jnp.bfloat16), entering).astype(jnp.bfloat16)

    total = jnp.arange(E * sent_rows, dtype=jnp.int32)[:, None] % sent_rows
    total = total == jnp.arange(SHARERS * sent_rows, dtype=jnp.int32)[None, :] % sent_rows
    total = total.astype(jnp.bfloat16)

    arriving = jnp.zeros((held, width), jnp.bfloat16)
    stored = jnp.zeros((16, width), jnp.float32)
    for tick in range(ticks):
        due = tick - section_pos
        pair = jnp.clip(due, 0, pairs - 1)
        pick = lax.dynamic_index_in_dim(pick_all, pair, 0, keepdims=False)
        place = lax.dynamic_index_in_dim(place_all, pair, 0, keepdims=False)
        sign = lax.dynamic_index_in_dim(sign_all, pair, 0, keepdims=False)
        hidden = jnp.where(section_pos == 0, entrance(min(tick, pairs - 1)), arriving)
        hidden = barrier(hidden)
        wide = hidden.astype(jnp.float32)
        inv_rms = lax.rsqrt(jnp.mean(wide * wide, axis=-1, keepdims=True) + EPSILON)
        normed = barrier((wide * inv_rms * gain_row).astype(jnp.bfloat16))
        own = exchange(choose(pick, normed).astype(jnp.bfloat16), SLICES, SHARERS)
        other = lax.ppermute(own, "expert", CORES)
        own_units = hidden_units(own)
        other_out = lax.ppermute(project(hidden_units(other)), "expert", CORES)
        own_out = project(own_units)
        both = (own_out.astype(jnp.float32) + other_out.astype(jnp.float32)).astype(jnp.bfloat16)
        logits = jnp.dot(normed, router_mat, preferred_element_type=jnp.float32)
        share = jax.nn.sigmoid(jnp.sum(logits * sign, axis=-1, keepdims=True))
        both, share, rest_share = barrier((both, share, 1.0 - share))
        parts = exchange(both, SLICES, SHARERS)
        outs = exchange(choose(total, parts).astype(jnp.bfloat16), EXPERTS, E)
        routed = choose(place, outs)
        result = (wide + share * routed[:held] + rest_share * routed[held:]).astype(jnp.bfloat16)
        result = barrier(result)
        if tick + 1 < ticks:
            arriving = lax.ppermute(
                result, "section", [(i, i + 1) for i in range(sections - 1)]
            )
        target = (pair * PAIR + spot_micro) * 4 + spot_token
        target = jnp.where((spot_block == expert) & (due == pair), target, -1)
        keep = target[None, :] == jnp.arange(16, dtype=jnp.int32)[:, None]
        stored = stored + choose(keep.astype(jnp.bfloat16), result)
    stored = stored.astype(jnp.bfloat16).reshape(1, micro_count, 4, width)
    return stored[:, :, :tokens]


def solution(mesh):
    placed = (
        P(None, "expert", None),
        P("section", None, None, None),
        P("section", None),
        P("section", None, None),
        P("section", None, "expert"),
        P("section", None, "expert"),
        P("section", "expert", None),
    )
    return jax.shard_map(
        on_device,
        mesh=mesh,
        in_specs=placed,
        out_specs=P("section", None, "expert", None),
        check_vma=False,
    )
```

time: 424 us -> 357 us (0.84)
  waiting for transfers between devices: 109 us -> 65.1 us
  blocking collectives: 131 us -> 170 us
  matrix products: 77.5 us -> 44.6 us
  local copies, waits for them, and re-layouts: 36.1 us -> 13.6 us
  starting transfers between devices: 50.9 us -> 44.5 us
    all_to_all x8 -> x5, waiting for transfers between devices: 84.4 us -> 40.9 us  [exchange(): lax.all_to_all(chunks, 'expert', split_axis=0, concat_axis=0, axis_index_...]
    all_to_all x8 -> x11, blocking collectives: 131 us -> 170 us  [exchange(): lax.all_to_all(chunks, 'expert', split_axis=0, concat_axis=0, axis_index_...]
    dot_general x30 -> x53, matrix products: 72.3 us -> 42.7 us  [the longest x23 21.5 us: choose(): return jnp.dot(picks, rows, preferred_element_type=jnp.float32)]
    unnamed x89 -> x65, local copies, waits for them, and re-layouts: 16 us -> 1.99 us
    reduce_sum x10 -> x0, other arithmetic: 8.89 us -> none  [the longest x5 6.22 us: on_device(): expert_out = jnp.sum(parts.astype(jnp.float32), axis=0).astype(jnp.bfloat16)]
    all_to_all x8 -> x5, starting transfers between devices: 37.5 us -> 29.2 us  [exchange(): lax.all_to_all(chunks, 'expert', split_axis=0, concat_axis=0, axis_index_...]
    broadcast_in_dim x12 -> x0, local copies, waits for them, and re-layouts: 5.14 us -> none  [gather_over(): copies = jnp.broadcast_to(block[None], (count,) + block.shape)]
    ppermute x5, waiting for transfers between devices: 10.1 us -> 5.82 us  [on_device(): other = lax.ppermute(own, 'expert', CORES)]
  transfers between devices with their start and end apart: 22 -> 19, of which waited for: 17 -> 17; matrix products, arithmetic and copies ran while one was open for 9% -> 10% of each run, Pallas kernels for 0% -> 0%
where the time goes in v2:
time: 357 us; the launch traced here: 355 us
  blocking collectives  170 us (48%)
  waiting for transfers between devices  65.1 us (18%)
  matrix products  44.6 us (12%)
  starting transfers between devices  44.5 us (12%)
  other arithmetic  16.2 us (5%)
  local copies, waits for them, and re-layouts  13.6 us (4%)
    all_to_all x11, blocking collectives, exchange(): lax.all_to_all(chunks, 'expert', split_axis=0, concat_axis=0, axis_index_...  170 us
    all_to_all x5, waiting for transfers between devices, exchange(): lax.all_to_all(chunks, 'expert', split_axis=0, concat_axis=0, axis_index_...  40.9 us
    all_to_all x5, starting transfers between devices, exchange(): lax.all_to_all(chunks, 'expert', split_axis=0, concat_axis=0, axis_index_...  29.2 us
    dot_general x23, matrix products, choose(): return jnp.dot(picks, rows, preferred_element_type=jnp.float32)  21.5 us
    ppermute x4, waiting for transfers between devices, on_device(): lax.ppermute(result, 'section', [(i, i + 1) for i in range(sections - 1)])  15.9 us
    ppermute x4, starting transfers between devices, on_device(): lax.ppermute(result, 'section', [(i, i + 1) for i in range(sections - 1)])  12.8 us
    dot_general x10, matrix products, hidden_units(): up_value = jnp.dot(rows, up_mat, preferred_element_type=jnp.float32)  8.17 us
  transfers between devices with their start and end apart: 19, of which 17 were waited for; matrix products, arithmetic and copies ran while one was open for 10% of the time, Pallas kernels for 0%

profile of v2, /device:TPU:16, one launch (start us, length us, event | category | flops | bytes accessed | tf_op | source)
XLA Modules:
  0.0 355.4 jit_solution(3344615102362511971)
XLA Ops:
  2.1 8.5 %all-to-all-start = ((bf16[4,16,3072]{2,1,0:T(8,128)(2,1)}), bf16[4,16,3072]{2,1,0:T(8,128)(2,1)S(1)}, u32[]{:S(2)}, u32[]{:S(2)}) async-start(bf16[4,16,3072]{2,1,0:T(8,128)(2,1)} %bitcast.283), calls=%async_computation | async-start | bytes 786432 | tf_op jit(solution)/shard_map/all_to_all | solution.py:20
  28.1 5.4 %all-to-all-start.1 = ((bf16[8,16,3072]{2,1,0:T(8,128)(2,1)}), bf16[8,16,3072]{2,1,0:T(8,128)(2,1)}, u32[]{:S(2)}, u32[]{:S(2)}) async-start(bf16[8,16,3072]{2,1,0:T(8,128)(2,1)} %bitcast.269), calls=%async_computation.1 | async-start | bytes 1572864 | tf_op jit(solution)/shard_map/all_to_all | solution.py:20
  33.6 11.3 %all-to-all-done.1 = bf16[8,16,3072]{2,1,0:T(8,128)(2,1)} async-done(((bf16[8,16,3072]{2,1,0:T(8,128)(2,1)}), bf16[8,16,3072]{2,1,0:T(8,128)(2,1)}, u32[]{:S(2)}, u32[]{:S(2)}) %all-to-all-start.1) | async-done | bytes 786464 | tf_op jit(solution)/shard_map/all_to_all | solution.py:20
  47.2 2.9 fusion.30
  55.1 16.4 %all_to_all.80 = bf16[8,16,3072]{2,1,0:T(8,128)(2,1)S(1)} all-to-all(bf16[8,16,3072]{2,1,0:T(8,128)(2,1)S(1)} %bitcast.275), channel_id=1, replica_groups={{0,2,4,6,8,10,12,14},{1,3,5,7,9,11,13,15},{16,18,20,22,24,26,28,30},{17..., dimensions={0} | all-to-all | bytes 1572864 | tf_op jit(solution)/shard_map/all_to_all | solution.py:20
  72.5 7.0 %all-to-all-start.3 = ((bf16[4,16,3072]{2,1,0:T(8,128)(2,1)}), bf16[4,16,3072]{2,1,0:T(8,128)(2,1)}, u32[]{:S(2)}, u32[]{:S(2)}) async-start(bf16[4,16,3072]{2,1,0:T(8,128)(2,1)} %bitcast.288), calls=%async_computation.3 | async-start | bytes 786432 | tf_op jit(solution)/shard_map/all_to_all | solution.py:20
  82.3 9.1 %all-to-all-done.3 = bf16[4,16,3072]{2,1,0:T(8,128)(2,1)} async-done(((bf16[4,16,3072]{2,1,0:T(8,128)(2,1)}), bf16[4,16,3072]{2,1,0:T(8,128)(2,1)}, u32[]{:S(2)}, u32[]{:S(2)}) %all-to-all-start.3) | async-done | bytes 393248 | tf_op jit(solution)/shard_map/all_to_all | solution.py:20
  94.3 3.2 collective-permute-start.2
  97.6 4.1 %collective-permute-done.2 = bf16[24,3072]{1,0:T(8,128)(2,1)} collective-permute-done((bf16[24,3072]{1,0:T(8,128)(2,1)}, bf16[24,3072]{1,0:T(8,128)(2,1)}, u32[]{:S(2)}, u32[]{:S(2)}) %collective-permute-start.2) | collective-permute-done | bytes 147488 | tf_op jit(solution)/shard_map/ppermute | solution.py:131
  101.6 1.8 broadcast_select_fusion.3
  104.8 14.8 %all_to_all.81 = bf16[8,16,3072]{2,1,0:T(8,128)(2,1)S(1)} all-to-all(bf16[8,16,3072]{2,1,0:T(8,128)(2,1)S(1)} %bitcast.271), channel_id=1, replica_groups={{0,2,4,6,8,10,12,14},{1,3,5,7,9,11,13,15},{16,18,20,22,24,26,28,30},{17..., dimensions={0} | all-to-all | bytes 1572864 | tf_op jit(solution)/shard_map/all_to_all | solution.py:20
  126.6 16.1 %all_to_all.82 = bf16[8,16,3072]{2,1,0:T(8,128)(2,1)S(1)} all-to-all(bf16[8,16,3072]{2,1,0:T(8,128)(2,1)S(1)} %bitcast.276), channel_id=1, replica_groups={{0,2,4,6,8,10,12,14},{1,3,5,7,9,11,13,15},{16,18,20,22,24,26,28,30},{17..., dimensions={0} | all-to-all | bytes 1572864 | tf_op jit(solution)/shard_map/all_to_all | solution.py:20
  143.0 15.4 %all_to_all.83 = bf16[4,16,3072]{2,1,0:T(8,128)(2,1)S(1)} all-to-all(bf16[4,16,3072]{2,1,0:T(8,128)(2,1)S(1)} %bitcast.289), channel_id=1, replica_groups={{0,16,32,48},{1,17,33,49},{2,18,34,50},{3,19,35,51},{4,20,36,52},{5,21,..., dimensions={0} | all-to-all | bytes 786432 | tf_op jit(solution)/shard_map/all_to_all | solution.py:20
  158.8 3.2 collective-permute-start.5
  162.0 3.9 %collective-permute-done.5 = bf16[24,3072]{1,0:T(8,128)(2,1)} collective-permute-done((bf16[24,3072]{1,0:T(8,128)(2,1)S(1)}, bf16[24,3072]{1,0:T(8,128)(2,1)}, u32[]{:S(2)}, u32[]{:S(2)}) %collective-permute-start.5) | collective-permute-done | bytes 147488 | tf_op jit(solution)/shard_map/ppermute | solution.py:131
  167.6 14.7 %all_to_all.84 = bf16[8,16,3072]{2,1,0:T(8,128)(2,1)S(1)} all-to-all(bf16[8,16,3072]{2,1,0:T(8,128)(2,1)S(1)} %bitcast.272), channel_id=1, replica_groups={{0,2,4,6,8,10,12,14},{1,3,5,7,9,11,13,15},{16,18,20,22,24,26,28,30},{17..., dimensions={0} | all-to-all | bytes 1572864 | tf_op jit(solution)/shard_map/all_to_all | solution.py:20
  189.0 15.9 %all_to_all.85 = bf16[8,16,3072]{2,1,0:T(8,128)(2,1)S(1)} all-to-all(bf16[8,16,3072]{2,1,0:T(8,128)(2,1)S(1)} %bitcast.277), channel_id=1, replica_groups={{0,2,4,6,8,10,12,14},{1,3,5,7,9,11,13,15},{16,18,20,22,24,26,28,30},{17..., dimensions={0} | all-to-all | bytes 1572864 | tf_op jit(solution)/shard_map/all_to_all | solution.py:20
  205.2 15.9 %all_to_all.86 = bf16[4,16,3072]{2,1,0:T(8,128)(2,1)S(1)} all-to-all(bf16[4,16,3072]{2,1,0:T(8,128)(2,1)S(1)} %bitcast.290), channel_id=1, replica_groups={{0,16,32,48},{1,17,33,49},{2,18,34,50},{3,19,35,51},{4,20,36,52},{5,21,..., dimensions={0} | all-to-all | bytes 786432 | tf_op jit(solution)/shard_map/all_to_all | solution.py:20
  221.5 3.2 collective-permute-start.8
  224.8 3.9 %collective-permute-done.8 = bf16[24,3072]{1,0:T(8,128)(2,1)} collective-permute-done((bf16[24,3072]{1,0:T(8,128)(2,1)S(1)}, bf16[24,3072]{1,0:T(8,128)(2,1)}, u32[]{:S(2)}, u32[]{:S(2)}) %collective-permute-start.8) | collective-permute-done | bytes 147488 | tf_op jit(solution)/shard_map/ppermute | solution.py:131
  230.3 14.7 %all_to_all.87 = bf16[8,16,3072]{2,1,0:T(8,128)(2,1)S(1)} all-to-all(bf16[8,16,3072]{2,1,0:T(8,128)(2,1)S(1)} %bitcast.273), channel_id=1, replica_groups={{0,2,4,6,8,10,12,14},{1,3,5,7,9,11,13,15},{16,18,20,22,24,26,28,30},{17..., dimensions={0} | all-to-all | bytes 1572864 | tf_op jit(solution)/shard_map/all_to_all | solution.py:20
  251.9 15.9 %all_to_all.88 = bf16[8,16,3072]{2,1,0:T(8,128)(2,1)S(1)} all-to-all(bf16[8,16,3072]{2,1,0:T(8,128)(2,1)S(1)} %bitcast.278), channel_id=1, replica_groups={{0,2,4,6,8,10,12,14},{1,3,5,7,9,11,13,15},{16,18,20,22,24,26,28,30},{17..., dimensions={0} | all-to-all | bytes 1572864 | tf_op jit(solution)/shard_map/all_to_all | solution.py:20
  268.2 15.8 %all_to_all.89 = bf16[4,16,3072]{2,1,0:T(8,128)(2,1)S(1)} all-to-all(bf16[4,16,3072]{2,1,0:T(8,128)(2,1)S(1)} %bitcast.291), channel_id=1, replica_groups={{0,16,32,48},{1,17,33,49},{2,18,34,50},{3,19,35,51},{4,20,36,52},{5,21,..., dimensions={0} | all-to-all | bytes 786432 | tf_op jit(solution)/shard_map/all_to_all | solution.py:20
  284.4 3.2 collective-permute-start.11
  287.6 3.9 %collective-permute-done.11 = bf16[24,3072]{1,0:T(8,128)(2,1)} collective-permute-done((bf16[24,3072]{1,0:T(8,128)(2,1)S(1)}, bf16[24,3072]{1,0:T(8,128)(2,1)}, u32[]{:S(2)}, u32[]{:S(2)}) %collective-permute-start.11) | collective-permute-done | bytes 147488 | tf_op jit(solution)/shard_map/ppermute | solution.py:131
  293.2 14.7 %all_to_all.90 = bf16[8,16,3072]{2,1,0:T(8,128)(2,1)S(1)} all-to-all(bf16[8,16,3072]{2,1,0:T(8,128)(2,1)S(1)} %bitcast.270), channel_id=1, replica_groups={{0,2,4,6,8,10,12,14},{1,3,5,7,9,11,13,15},{16,18,20,22,24,26,28,30},{17..., dimensions={0} | all-to-all | bytes 1572864 | tf_op jit(solution)/shard_map/all_to_all | solution.py:20
  315.5 4.2 %all-to-all-start.14 = ((bf16[8,16,3072]{2,1,0:T(8,128)(2,1)}), bf16[8,16,3072]{2,1,0:T(8,128)(2,1)}, u32[]{:S(2)}, u32[]{:S(2)}) async-start(bf16[8,16,3072]{2,1,0:T(8,128)(2,1)} %bitcast.274), calls=%async_computation.14 | async-start | bytes 1572864 | tf_op jit(solution)/shard_map/all_to_all | solution.py:20
  319.8 1.7 fusion.129
  321.6 10.9 %all-to-all-done.14 = bf16[8,16,3072]{2,1,0:T(8,128)(2,1)} async-done(((bf16[8,16,3072]{2,1,0:T(8,128)(2,1)}), bf16[8,16,3072]{2,1,0:T(8,128)(2,1)}, u32[]{:S(2)}, u32[]{:S(2)}) %all-to-all-start.14) | async-done | bytes 786464 | tf_op jit(solution)/shard_map/all_to_all | solution.py:20
  332.5 2.2 convolution_convert_fusion.15
  334.7 4.1 %all-to-all-start.15 = ((bf16[4,16,3072]{2,1,0:T(8,128)(2,1)}), bf16[4,16,3072]{2,1,0:T(8,128)(2,1)}, u32[]{:S(2)}, u32[]{:S(2)}) async-start(bf16[4,16,3072]{2,1,0:T(8,128)(2,1)} %bitcast.287), calls=%async_computation.15 | async-start | bytes 786432 | tf_op jit(solution)/shard_map/all_to_all | solution.py:20
  342.7 9.5 %all-to-all-done.15 = bf16[4,16,3072]{2,1,0:T(8,128)(2,1)} async-done(((bf16[4,16,3072]{2,1,0:T(8,128)(2,1)}), bf16[4,16,3072]{2,1,0:T(8,128)(2,1)}, u32[]{:S(2)}, u32[]{:S(2)}) %all-to-all-start.15) | async-done | bytes 393248 | tf_op jit(solution)/shard_map/all_to_all | solution.py:20
  (217 shorter events, 76.7 us)
Async XLA Ops:
  0.0 51.4 %copy-start = (bf16[1,512,3072]{2,1,0:T(8,128)(2,1)S(1)}, bf16[1,512,3072]{2,1,0:T(8,128)(2,1)}, u32[]{:S(2)}) copy-start(bf16[1,512,3072]{2,1,0:T(8,128)(2,1)} %param.13) | copy-start | bytes 9437188
  2.1 21.6 %all-to-all-start = ((bf16[4,16,3072]{2,1,0:T(8,128)(2,1)}), bf16[4,16,3072]{2,1,0:T(8,128)(2,1)S(1)}, u32[]{:S(2)}, u32[]{:S(2)}) async-start(bf16[4,16,3072]{2,1,0:T(8,128)(2,1)} %bitcast.283), calls=%async_computation | async-start | bytes 786432 | tf_op jit(solution)/shard_map/all_to_all | solution.py:20
  23.6 26.5 %copy-start.20 = (pred[2,128,24]{1,2,0:T(8,128)(4,1)}, pred[2,128,24]{1,2,0:T(8,128)(4,1)S(1)}, u32[]{:S(2)}) copy-start(pred[2,128,24]{1,2,0:T(8,128)(4,1)S(1)} %compare_reduce_fusion) | copy-start | bytes 18436
  28.1 16.7 %all-to-all-start.1 = ((bf16[8,16,3072]{2,1,0:T(8,128)(2,1)}), bf16[8,16,3072]{2,1,0:T(8,128)(2,1)}, u32[]{:S(2)}, u32[]{:S(2)}) async-start(bf16[8,16,3072]{2,1,0:T(8,128)(2,1)} %bitcast.269), calls=%async_computation.1 | async-start | bytes 1572864 | tf_op jit(solution)/shard_map/all_to_all | solution.py:20
  44.9 5.2 %collective-permute-start = (bf16[128,3072]{1,0:T(8,128)(2,1)}, bf16[128,3072]{1,0:T(8,128)(2,1)S(1)}, u32[]{:S(2)}, u32[]{:S(2)}) collective-permute-start(bf16[128,3072]{1,0:T(8,128)(2,1)} %bitcast.6), channel_id=1, source_target_pairs={{0,1},{1,0},{2,3},{3,2},{4,5},{5,4},{6,7},{7,6},{8,9},{9,8},{10,11... | collective-permute-start | bytes 2359304 | tf_op jit(solution)/shard_map/ppermute | solution.py:117
  52.0 2.9 collective-permute-start.1
  55.1 48.5 %copy-start.18 = (f32[1,3072]{1,0:T(1,128)S(1)}, f32[1,3072]{1,0:T(1,128)}, u32[]{:S(2)}) copy-start(f32[1,3072]{1,0:T(1,128)} %param.9) | copy-start | bytes 36868
  72.5 18.8 %all-to-all-start.3 = ((bf16[4,16,3072]{2,1,0:T(8,128)(2,1)}), bf16[4,16,3072]{2,1,0:T(8,128)(2,1)}, u32[]{:S(2)}, u32[]{:S(2)}) async-start(bf16[4,16,3072]{2,1,0:T(8,128)(2,1)} %bitcast.288), calls=%async_computation.3 | async-start | bytes 786432 | tf_op jit(solution)/shard_map/all_to_all | solution.py:20
  94.3 7.3 %collective-permute-start.2 = (bf16[24,3072]{1,0:T(8,128)(2,1)}, bf16[24,3072]{1,0:T(8,128)(2,1)}, u32[]{:S(2)}, u32[]{:S(2)}) collective-permute-start(bf16[24,3072]{1,0:T(8,128)(2,1)} %fusion.61), channel_id=1, source_target_pairs={{0,64},{64,128},{128,192},{1,65},{65,129},{129,193},{2,66},{66,130... | collective-permute-start | bytes 442376 | tf_op jit(solution)/shard_map/ppermute | solution.py:131
  97.5 22.1 %copy-start.28 = (f32[2,24,1,4]{1,3,2,0:T(4,128)S(1)}, f32[2,24,1,4]{1,3,2,0:T(4,128)}, u32[]{:S(2)}) copy-start(f32[2,24,1,4]{1,3,2,0:T(4,128)} %copy-done.27) | copy-start | bytes 2308
  97.5 22.3 %copy-start.2 = (bf16[1,3072,512]{2,1,0:T(8,128)(2,1)S(1)}, bf16[1,3072,512]{2,1,0:T(8,128)(2,1)}, u32[]{:S(2)}) copy-start(bf16[1,3072,512]{2,1,0:T(8,128)(2,1)} %param.12) | copy-start | bytes 9437188
  119.6 2.3 collective-permute-start.3
  123.9 2.6 collective-permute-start.4
  125.7 32.7 %copy-start.19 = (pred[2,48,64]{2,1,0:T(8,128)(4,1)S(1)}, pred[2,48,64]{2,1,0:T(8,128)(4,1)}, u32[]{:S(2)}) copy-start(pred[2,48,64]{2,1,0:T(8,128)(4,1)} %iota_compare_fusion) | copy-start | bytes 18436
  126.6 39.3 %copy-start.11 = (bf16[24,3072]{1,0:T(8,128)(2,1)S(1)}, bf16[24,3072]{1,0:T(8,128)(2,1)}, u32[]{:S(2)}) copy-start(bf16[24,3072]{1,0:T(8,128)(2,1)} %get-tuple-element.78) | copy-start | bytes 442372
  126.6 40.5 %copy-start.21 = (pred[2,128,24]{1,2,0:T(8,128)(4,1)S(1)}, pred[2,128,24]{1,2,0:T(8,128)(4,1)}, u32[]{:S(2)}) copy-start(pred[2,128,24]{1,2,0:T(8,128)(4,1)} %copy-done.20) | copy-start | bytes 18436
  143.0 39.3 %copy-start.29 = (f32[2,24,1,4]{1,3,2,0:T(4,128)S(1)}, f32[2,24,1,4]{1,3,2,0:T(4,128)}, u32[]{:S(2)}) copy-start(f32[2,24,1,4]{1,3,2,0:T(4,128)} %copy-done.27) | copy-start | bytes 2308
  143.0 39.3 %copy-start.31 = (bf16[1,3072,4]{1,2,0:T(4,128)(2,1)S(1)}, bf16[1,3072,4]{1,2,0:T(4,128)(2,1)}, u32[]{:S(2)}) copy-start(bf16[1,3072,4]{1,2,0:T(4,128)(2,1)} %param.10) | copy-start | bytes 73732
  158.8 24.3 %copy-start.13 = (bf16[24,3072]{1,0:T(8,128)(2,1)}, bf16[24,3072]{1,0:T(8,128)(2,1)S(1)}, u32[]{:S(2)}) copy-start(bf16[24,3072]{1,0:T(8,128)(2,1)S(1)} %fusion.66) | copy-start | bytes 442372
  158.8 7.1 %collective-permute-start.5 = (bf16[24,3072]{1,0:T(8,128)(2,1)S(1)}, bf16[24,3072]{1,0:T(8,128)(2,1)}, u32[]{:S(2)}, u32[]{:S(2)}) collective-permute-start(bf16[24,3072]{1,0:T(8,128)(2,1)S(1)} %fusion.66), channel_id=1, source_target_pairs={{0,64},{64,128},{128,192},{1,65},{65,129},{129,193},{2,66},{66,130... | collective-permute-start | bytes 442376 | tf_op jit(solution)/shard_map/ppermute | solution.py:131
  182.3 2.3 collective-permute-start.6
  186.4 2.4 collective-permute-start.7
  221.5 24.3 %copy-start.15 = (bf16[24,3072]{1,0:T(8,128)(2,1)}, bf16[24,3072]{1,0:T(8,128)(2,1)S(1)}, u32[]{:S(2)}) copy-start(bf16[24,3072]{1,0:T(8,128)(2,1)S(1)} %fusion.71) | copy-start | bytes 442372
  221.5 7.1 %collective-permute-start.8 = (bf16[24,3072]{1,0:T(8,128)(2,1)S(1)}, bf16[24,3072]{1,0:T(8,128)(2,1)}, u32[]{:S(2)}, u32[]{:S(2)}) collective-permute-start(bf16[24,3072]{1,0:T(8,128)(2,1)S(1)} %fusion.71), channel_id=1, source_target_pairs={{0,64},{64,128},{128,192},{1,65},{65,129},{129,193},{2,66},{66,130... | collective-permute-start | bytes 442376 | tf_op jit(solution)/shard_map/ppermute | solution.py:131
  245.0 2.3 collective-permute-start.9
  249.1 2.6 collective-permute-start.10
  284.4 7.1 %collective-permute-start.11 = (bf16[24,3072]{1,0:T(8,128)(2,1)S(1)}, bf16[24,3072]{1,0:T(8,128)(2,1)}, u32[]{:S(2)}, u32[]{:S(2)}) collective-permute-start(bf16[24,3072]{1,0:T(8,128)(2,1)S(1)} %fusion.76), channel_id=1, source_target_pairs={{0,64},{64,128},{128,192},{1,65},{65,129},{129,193},{2,66},{66,130... | collective-permute-start | bytes 442376 | tf_op jit(solution)/shard_map/ppermute | solution.py:131
  307.8 2.3 collective-permute-start.12
  312.0 2.4 collective-permute-start.13
  313.7 25.1 %copy-start.14 = (bf16[24,3072]{1,0:T(8,128)(2,1)S(1)}, bf16[24,3072]{1,0:T(8,128)(2,1)}, u32[]{:S(2)}) copy-start(bf16[24,3072]{1,0:T(8,128)(2,1)} %copy-done.13) | copy-start | bytes 442372
  315.5 17.0 %all-to-all-start.14 = ((bf16[8,16,3072]{2,1,0:T(8,128)(2,1)}), bf16[8,16,3072]{2,1,0:T(8,128)(2,1)}, u32[]{:S(2)}, u32[]{:S(2)}) async-start(bf16[8,16,3072]{2,1,0:T(8,128)(2,1)} %bitcast.274), calls=%async_computation.14 | async-start | bytes 1572864 | tf_op jit(solution)/shard_map/all_to_all | solution.py:20
  334.7 17.5 %all-to-all-start.15 = ((bf16[4,16,3072]{2,1,0:T(8,128)(2,1)}), bf16[4,16,3072]{2,1,0:T(8,128)(2,1)}, u32[]{:S(2)}, u32[]{:S(2)}) async-start(bf16[4,16,3072]{2,1,0:T(8,128)(2,1)} %bitcast.287), calls=%async_computation.15 | async-start | bytes 786432 | tf_op jit(solution)/shard_map/all_to_all | solution.py:20
  (19 other events, 177.4 us)

commit v3 on v2

--- a/solution.py
+++ b/solution.py
@@ -27,25 +27,50 @@
     return jnp.dot(picks, rows, preferred_element_type=jnp.float32)
 
 
-def tables(ids, expert):
-    pairs, tokens = ids.shape[0], ids.shape[3]
-    blocks = PAIR * E
-    flat = ids.reshape(pairs, blocks, tokens * 2)
-    same = flat[..., :, None] == flat[..., None, :]
-    earlier = jnp.arange(tokens * 2)[:, None] > jnp.arange(tokens * 2)[None, :]
-    slot = jnp.sum((same & earlier).astype(jnp.int32), axis=-1)
-    block = jnp.arange(blocks, dtype=jnp.int32)[None, :, None]
-    row = block * MOST + slot
-    rows = blocks * MOST
-    mine = jnp.where(flat == expert, row, -1).reshape(pairs, 1, blocks * tokens, 2)
-    wanted = jnp.arange(SHARERS * rows, dtype=jnp.int32)[None, :, None, None] % rows
-    pick = jnp.any(mine == wanted, axis=-1)
-    back = (flat * rows + row).reshape(pairs, blocks * tokens, 2)
-    back = jnp.swapaxes(back, 1, 2).reshape(pairs, 2 * blocks * tokens, 1)
-    place = back == jnp.arange(E * rows, dtype=jnp.int32)[None, None, :]
-    named = ids.reshape(pairs, blocks * tokens, 2)[..., None] == jnp.arange(E, dtype=jnp.int32)
-    sign = named[:, :, 0].astype(jnp.float32) - named[:, :, 1].astype(jnp.float32)
-    return pick.astype(jnp.bfloat16), place.astype(jnp.bfloat16), sign
+def tables(route_all, expert, rest, tokens):
+    micro_count, requests, _ = route_all.shape
+    rows = PAIR * E * MOST
+    spots = micro_count * E * tokens
+
+    def column(values):
+        return values[:, None]
+
+    spot = jnp.arange(spots, dtype=jnp.int32)
+    micro, block, token = spot // (E * tokens), spot // tokens % E, spot % tokens
+    seat = (block * (requests // E // tokens) + rest) * tokens + token
+    seats = column(seat) == jnp.arange(requests, dtype=jnp.int32)[None, :]
+    listed = jnp.transpose(route_all, (0, 2, 1)).reshape(2 * micro_count, requests)
+    named = lax.dot_general(
+        seats.astype(jnp.bfloat16),
+        listed.astype(jnp.bfloat16),
+        (((1,), (1,)), ((), ())),
+        preferred_element_type=jnp.float32,
+    )
+    at = jnp.arange(2 * micro_count, dtype=jnp.int32)[None, :]
+    first = jnp.sum(jnp.where(at == 2 * column(micro), named, 0.0), axis=1, keepdims=True)
+    second = jnp.sum(jnp.where(at == 2 * column(micro) + 1, named, 0.0), axis=1, keepdims=True)
+    first, second = lax.optimization_barrier((first, second))
+    first, second = first.astype(jnp.int32), second.astype(jnp.int32)
+    group = spot // tokens
+    earlier = (column(group) == group[None, :]) & (column(spot) > spot[None, :])
+    earlier = earlier.astype(jnp.bfloat16)
+    begin = column(group % (PAIR * E)) * MOST
+
+    def slots(hits, lanes):
+        before = jnp.dot(earlier, hits.astype(jnp.bfloat16), preferred_element_type=jnp.float32)
+        return before.astype(jnp.int32) == lanes[None, :] % rows - begin
+
+    lanes = jnp.arange(SHARERS * rows, dtype=jnp.int32)
+    hits = jnp.broadcast_to((first == expert) | (second == expert), (spots, SHARERS * rows))
+    pick = (hits & slots(hits, lanes)).astype(jnp.bfloat16)
+    lanes = jnp.arange(E * rows, dtype=jnp.int32)
+    first_hit = first == lanes[None, :] // rows
+    second_hit = second == lanes[None, :] // rows
+    fits = slots(first_hit | second_hit, lanes)
+    place = [(hit & fits).astype(jnp.bfloat16) for hit in (first_hit, second_hit)]
+    ids = jnp.arange(E, dtype=jnp.int32)[None, :]
+    sign = (first == ids).astype(jnp.float32) - (second == ids).astype(jnp.float32)
+    return lax.optimization_barrier((pick, place[0], place[1], sign))
 
 
 def on_device(inputs, routes, norm_gain, router, w_gate, w_up, w_down):
@@ -73,9 +98,7 @@
             jnp.dot(units, down_mat, preferred_element_type=jnp.float32).astype(jnp.bfloat16)
         )
 
-    ids = routes[0].reshape(pairs, PAIR, E, 16, tokens, 2)
-    ids = lax.dynamic_index_in_dim(ids, rest, 3, keepdims=False)
-    pick_all, place_all, sign_all = tables(ids, expert)
+    pick_all, first_all, second_all, sign_all = tables(routes[0], expert, rest, tokens)
 
     spare = 16
     own_rows = jnp.swapaxes(inputs, 0, 1).reshape(tokens * micro_count, width)
@@ -91,7 +114,7 @@
         spot % tokens,
     )
 
-    def entrance(pair):
+    def entrance(pair, entering):
         source = spot_block * spare + spot_token * micro_count + pair * PAIR + spot_micro
         picks = source[:, None] == jnp.arange(E * spare, dtype=jnp.int32)[None, :]
         return choose(picks.astype(jnp.bfloat16), entering).astype(jnp.bfloat16)
@@ -100,20 +123,29 @@
     total = total == jnp.arange(SHARERS * sent_rows, dtype=jnp.int32)[None, :] % sent_rows
     total = total.astype(jnp.bfloat16)
 
+    entry = entrance(0, entering)
     arriving = jnp.zeros((held, width), jnp.bfloat16)
     stored = jnp.zeros((16, width), jnp.float32)
     for tick in range(ticks):
         due = tick - section_pos
         pair = jnp.clip(due, 0, pairs - 1)
-        pick = lax.dynamic_index_in_dim(pick_all, pair, 0, keepdims=False)
-        place = lax.dynamic_index_in_dim(place_all, pair, 0, keepdims=False)
-        sign = lax.dynamic_index_in_dim(sign_all, pair, 0, keepdims=False)
-        hidden = jnp.where(section_pos == 0, entrance(min(tick, pairs - 1)), arriving)
+        pick, first_place, second_place, sign = (
+            lax.dynamic_slice_in_dim(table, pair * held, held, 0)
+            for table in (pick_all, first_all, second_all, sign_all)
+        )
+        hidden = jnp.where(section_pos == 0, entry, arriving)
         hidden = barrier(hidden)
         wide = hidden.astype(jnp.float32)
         inv_rms = lax.rsqrt(jnp.mean(wide * wide, axis=-1, keepdims=True) + EPSILON)
         normed = barrier((wide * inv_rms * gain_row).astype(jnp.bfloat16))
-        own = exchange(choose(pick, normed).astype(jnp.bfloat16), SLICES, SHARERS)
+        sent = lax.dot_general(
+            pick, normed, (((0,), (0,)), ((), ())), preferred_element_type=jnp.float32
+        ).astype(jnp.bfloat16)
+        if tick == 0:
+            sent, first_all, second_all, sign_all, total = barrier(
+                (sent, first_all, second_all, sign_all, total)
+            )
+        own = exchange(sent, SLICES, SHARERS)
         other = lax.ppermute(own, "expert", CORES)
         own_units = hidden_units(own)
         other_out = lax.ppermute(project(hidden_units(other)), "expert", CORES)
@@ -124,17 +156,22 @@
         both, share, rest_share = barrier((both, share, 1.0 - share))
         parts = exchange(both, SLICES, SHARERS)
         outs = exchange(choose(total, parts).astype(jnp.bfloat16), EXPERTS, E)
-        routed = choose(place, outs)
-        result = (wide + share * routed[:held] + rest_share * routed[held:]).astype(jnp.bfloat16)
-        result = barrier(result)
+        first_out, second_out = choose(first_place, outs), choose(second_place, outs)
+        result = (wide + share * first_out + rest_share * second_out).astype(jnp.bfloat16)
+        result, entering, due = barrier((result, entering, due))
         if tick + 1 < ticks:
             arriving = lax.ppermute(
                 result, "section", [(i, i + 1) for i in range(sections - 1)]
             )
-        target = (pair * PAIR + spot_micro) * 4 + spot_token
-        target = jnp.where((spot_block == expert) & (due == pair), target, -1)
+        if tick + 1 < pairs:
+            entry = entrance(tick + 1, entering)
+        target = (due * PAIR + spot_micro) * 4 + spot_token
+        held_now = (spot_block == expert) & (due >= 0) & (due < pairs)
+        target = jnp.where(held_now, target, -1)
         keep = target[None, :] == jnp.arange(16, dtype=jnp.int32)[:, None]
         stored = stored + choose(keep.astype(jnp.bfloat16), result)
+        if tick + 1 < ticks:
+            arriving, stored, entry = barrier((arriving, stored, entry))
     stored = stored.astype(jnp.bfloat16).reshape(1, micro_count, 4, width)
     return stored[:, :, :tokens]
 

time: 357 us -> 357 us (level)
  local copies, waits for them, and re-layouts: 13.6 us -> 5.25 us
  blocking collectives: 170 us -> 175 us
  matrix products: 44.6 us -> 48.2 us
    ppermute x4, waiting for transfers between devices: 15.9 us -> 7.05 us  [on_device(): lax.ppermute(result, 'section', [(i, i + 1) for i in range(sections - 1)])]
    all_to_all x5, waiting for transfers between devices: 40.9 us -> 49 us  [exchange(): lax.all_to_all(chunks, 'expert', split_axis=0, concat_axis=0, axis_index_...]
    dot_general x0 -> x8, matrix products: none -> 7.3 us  [the longest x5 3.37 us: on_device(): lax.dot_general(pick, normed, (((0,), (0,)), ((), ())), preferred_element...]
    add x0 -> x5, other arithmetic: none -> 5.36 us  [the longest x3 4.25 us: on_device(): stored = stored + choose(keep.astype(jnp.bfloat16), result)]
    all_to_all x11, blocking collectives: 170 us -> 175 us  [exchange(): lax.all_to_all(chunks, 'expert', split_axis=0, concat_axis=0, axis_index_...]
  transfers between devices with their start and end apart: 19 -> 19, of which waited for: 17 -> 19; matrix products, arithmetic and copies ran while one was open for 10% -> 9% of each run, Pallas kernels for 0% -> 0%
where the time goes in v3:
time: 357 us; the launch traced here: 355 us
  blocking collectives  175 us (49%)
  waiting for transfers between devices  64.7 us (18%)
  matrix products  48.2 us (14%)
  starting transfers between devices  44.1 us (12%)
  other arithmetic  17.5 us (5%)
  local copies, waits for them, and re-layouts  5.25 us (1%)
    all_to_all x11, blocking collectives, exchange(): lax.all_to_all(chunks, 'expert', split_axis=0, concat_axis=0, axis_index_...  175 us
    all_to_all x5, waiting for transfers between devices, exchange(): lax.all_to_all(chunks, 'expert', split_axis=0, concat_axis=0, axis_index_...  49 us
    all_to_all x5, starting transfers between devices, exchange(): lax.all_to_all(chunks, 'expert', split_axis=0, concat_axis=0, axis_index_...  27.5 us
    dot_general x23, matrix products, choose(): return jnp.dot(picks, rows, preferred_element_type=jnp.float32)  21.7 us
    ppermute x4, starting transfers between devices, on_device(): lax.ppermute(result, 'section', [(i, i + 1) for i in range(sections - 1)])  13.7 us
  transfers between devices with their start and end apart: 19, of which 19 were waited for; matrix products, arithmetic and copies ran while one was open for 9% of the time, Pallas kernels for 0%

profile of v3, /device:TPU:16, one launch (start us, length us, event | category | flops | bytes accessed | tf_op | source)
XLA Modules:
  0.0 355.1 jit_solution(17598054563863301459)
XLA Ops:
  2.1 8.5 %all-to-all-start = ((bf16[4,16,3072]{2,1,0:T(8,128)(2,1)}), bf16[4,16,3072]{2,1,0:T(8,128)(2,1)S(1)}, u32[]{:S(2)}, u32[]{:S(2)}) async-start(bf16[4,16,3072]{2,1,0:T(8,128)(2,1)} %bitcast.256), calls=%async_computation | async-start | bytes 786432 | tf_op jit(solution)/shard_map/all_to_all | solution.py:20
  21.6 2.1 all-to-all-done
  27.3 15.3 %all_to_all.80 = bf16[8,16,3072]{2,1,0:T(8,128)(2,1)S(1)} all-to-all(bf16[8,16,3072]{2,1,0:T(8,128)(2,1)S(1)} %bitcast.247), channel_id=1, replica_groups={{0,2,4,6,8,10,12,14},{1,3,5,7,9,11,13,15},{16,18,20,22,24,26,28,30},{17..., dimensions={0} | all-to-all | bytes 1572864 | tf_op jit(solution)/shard_map/all_to_all | solution.py:20
  50.3 16.0 %all_to_all.81 = bf16[8,16,3072]{2,1,0:T(8,128)(2,1)S(1)} all-to-all(bf16[8,16,3072]{2,1,0:T(8,128)(2,1)S(1)} %bitcast.251), channel_id=1, replica_groups={{0,2,4,6,8,10,12,14},{1,3,5,7,9,11,13,15},{16,18,20,22,24,26,28,30},{17..., dimensions={0} | all-to-all | bytes 1572864 | tf_op jit(solution)/shard_map/all_to_all | solution.py:20
  67.3 6.7 %all-to-all-start.3 = ((bf16[4,16,3072]{2,1,0:T(8,128)(2,1)}), bf16[4,16,3072]{2,1,0:T(8,128)(2,1)S(1)}, u32[]{:S(2)}, u32[]{:S(2)}) async-start(bf16[4,16,3072]{2,1,0:T(8,128)(2,1)} %bitcast.259), calls=%async_computation.3 | async-start | bytes 786432 | tf_op jit(solution)/shard_map/all_to_all | solution.py:20
  74.0 11.5 %all-to-all-done.3 = bf16[4,16,3072]{2,1,0:T(8,128)(2,1)S(1)} async-done(((bf16[4,16,3072]{2,1,0:T(8,128)(2,1)}), bf16[4,16,3072]{2,1,0:T(8,128)(2,1)S(1)}, u32[]{:S(2)}, u32[]{:S(2)}) %all-to-all-start.3) | async-done | bytes 393248 | tf_op jit(solution)/shard_map/all_to_all | solution.py:20
  88.2 3.4 collective-permute-start.2
  92.9 1.8 fusion.111
  97.8 15.9 %all_to_all.82 = bf16[8,16,3072]{2,1,0:T(8,128)(2,1)S(1)} all-to-all(bf16[8,16,3072]{2,1,0:T(8,128)(2,1)S(1)} %bitcast.248), channel_id=1, replica_groups={{0,2,4,6,8,10,12,14},{1,3,5,7,9,11,13,15},{16,18,20,22,24,26,28,30},{17..., dimensions={0} | all-to-all | bytes 1572864 | tf_op jit(solution)/shard_map/all_to_all | solution.py:20
  120.5 15.9 %all_to_all.83 = bf16[8,16,3072]{2,1,0:T(8,128)(2,1)S(1)} all-to-all(bf16[8,16,3072]{2,1,0:T(8,128)(2,1)S(1)} %bitcast.252), channel_id=1, replica_groups={{0,2,4,6,8,10,12,14},{1,3,5,7,9,11,13,15},{16,18,20,22,24,26,28,30},{17..., dimensions={0} | all-to-all | bytes 1572864 | tf_op jit(solution)/shard_map/all_to_all | solution.py:20
  137.5 4.1 %all-to-all-start.6 = ((bf16[4,16,3072]{2,1,0:T(8,128)(2,1)}), bf16[4,16,3072]{2,1,0:T(8,128)(2,1)}, u32[]{:S(2)}, u32[]{:S(2)}) async-start(bf16[4,16,3072]{2,1,0:T(8,128)(2,1)} %bitcast.260), calls=%async_computation.6 | async-start | bytes 786432 | tf_op jit(solution)/shard_map/all_to_all | solution.py:20
  141.6 11.8 %all-to-all-done.6 = bf16[4,16,3072]{2,1,0:T(8,128)(2,1)} async-done(((bf16[4,16,3072]{2,1,0:T(8,128)(2,1)}), bf16[4,16,3072]{2,1,0:T(8,128)(2,1)}, u32[]{:S(2)}, u32[]{:S(2)}) %all-to-all-start.6) | async-done | bytes 393248 | tf_op jit(solution)/shard_map/all_to_all | solution.py:20
  155.8 3.5 collective-permute-start.5
  159.5 1.6 add.644
  161.1 2.0 collective-permute-done.5
  163.8 15.9 %all_to_all.84 = bf16[8,16,3072]{2,1,0:T(8,128)(2,1)S(1)} all-to-all(bf16[8,16,3072]{2,1,0:T(8,128)(2,1)S(1)} %bitcast.249), channel_id=1, replica_groups={{0,2,4,6,8,10,12,14},{1,3,5,7,9,11,13,15},{16,18,20,22,24,26,28,30},{17..., dimensions={0} | all-to-all | bytes 1572864 | tf_op jit(solution)/shard_map/all_to_all | solution.py:20
  186.4 15.9 %all_to_all.85 = bf16[8,16,3072]{2,1,0:T(8,128)(2,1)S(1)} all-to-all(bf16[8,16,3072]{2,1,0:T(8,128)(2,1)S(1)} %bitcast.253), channel_id=1, replica_groups={{0,2,4,6,8,10,12,14},{1,3,5,7,9,11,13,15},{16,18,20,22,24,26,28,30},{17..., dimensions={0} | all-to-all | bytes 1572864 | tf_op jit(solution)/shard_map/all_to_all | solution.py:20
  203.4 4.1 %all-to-all-start.9 = ((bf16[4,16,3072]{2,1,0:T(8,128)(2,1)}), bf16[4,16,3072]{2,1,0:T(8,128)(2,1)}, u32[]{:S(2)}, u32[]{:S(2)}) async-start(bf16[4,16,3072]{2,1,0:T(8,128)(2,1)} %bitcast.258), calls=%async_computation.9 | async-start | bytes 786432 | tf_op jit(solution)/shard_map/all_to_all | solution.py:20
  207.5 11.8 %all-to-all-done.9 = bf16[4,16,3072]{2,1,0:T(8,128)(2,1)} async-done(((bf16[4,16,3072]{2,1,0:T(8,128)(2,1)}), bf16[4,16,3072]{2,1,0:T(8,128)(2,1)}, u32[]{:S(2)}, u32[]{:S(2)}) %all-to-all-start.9) | async-done | bytes 393248 | tf_op jit(solution)/shard_map/all_to_all | solution.py:20
  221.7 3.5 collective-permute-start.8
  225.3 1.6 add.656
  227.0 2.0 collective-permute-done.8
  229.7 15.9 %all_to_all.86 = bf16[8,16,3072]{2,1,0:T(8,128)(2,1)S(1)} all-to-all(bf16[8,16,3072]{2,1,0:T(8,128)(2,1)S(1)} %bitcast.250), channel_id=1, replica_groups={{0,2,4,6,8,10,12,14},{1,3,5,7,9,11,13,15},{16,18,20,22,24,26,28,30},{17..., dimensions={0} | all-to-all | bytes 1572864 | tf_op jit(solution)/shard_map/all_to_all | solution.py:20
  252.5 15.9 %all_to_all.87 = bf16[8,16,3072]{2,1,0:T(8,128)(2,1)S(1)} all-to-all(bf16[8,16,3072]{2,1,0:T(8,128)(2,1)S(1)} %bitcast.254), channel_id=1, replica_groups={{0,2,4,6,8,10,12,14},{1,3,5,7,9,11,13,15},{16,18,20,22,24,26,28,30},{17..., dimensions={0} | all-to-all | bytes 1572864 | tf_op jit(solution)/shard_map/all_to_all | solution.py:20
  269.5 4.1 %all-to-all-start.12 = ((bf16[4,16,3072]{2,1,0:T(8,128)(2,1)}), bf16[4,16,3072]{2,1,0:T(8,128)(2,1)}, u32[]{:S(2)}, u32[]{:S(2)}) async-start(bf16[4,16,3072]{2,1,0:T(8,128)(2,1)} %bitcast.257), calls=%async_computation.12 | async-start | bytes 786432 | tf_op jit(solution)/shard_map/all_to_all | solution.py:20
  273.6 11.8 %all-to-all-done.12 = bf16[4,16,3072]{2,1,0:T(8,128)(2,1)} async-done(((bf16[4,16,3072]{2,1,0:T(8,128)(2,1)}), bf16[4,16,3072]{2,1,0:T(8,128)(2,1)}, u32[]{:S(2)}, u32[]{:S(2)}) %all-to-all-start.12) | async-done | bytes 393248 | tf_op jit(solution)/shard_map/all_to_all | solution.py:20
  286.6 1.8 fusion.13
  288.4 3.4 collective-permute-start.11
  293.9 2.0 collective-permute-done.11
  296.6 15.9 %all_to_all.88 = bf16[8,16,3072]{2,1,0:T(8,128)(2,1)S(1)} all-to-all(bf16[8,16,3072]{2,1,0:T(8,128)(2,1)S(1)} %bitcast.246), channel_id=1, replica_groups={{0,2,4,6,8,10,12,14},{1,3,5,7,9,11,13,15},{16,18,20,22,24,26,28,30},{17..., dimensions={0} | all-to-all | bytes 1572864 | tf_op jit(solution)/shard_map/all_to_all | solution.py:20
  320.0 16.0 %all_to_all.89 = bf16[8,16,3072]{2,1,0:T(8,128)(2,1)S(1)} all-to-all(bf16[8,16,3072]{2,1,0:T(8,128)(2,1)S(1)} %bitcast.255), channel_id=1, replica_groups={{0,2,4,6,8,10,12,14},{1,3,5,7,9,11,13,15},{16,18,20,22,24,26,28,30},{17..., dimensions={0} | all-to-all | bytes 1572864 | tf_op jit(solution)/shard_map/all_to_all | solution.py:20
  336.2 16.1 %all_to_all.90 = bf16[4,16,3072]{2,1,0:T(8,128)(2,1)S(1)} all-to-all(bf16[4,16,3072]{2,1,0:T(8,128)(2,1)S(1)} %bitcast.261), channel_id=1, replica_groups={{0,16,32,48},{1,17,33,49},{2,18,34,50},{3,19,35,51},{4,20,36,52},{5,21,..., dimensions={0} | all-to-all | bytes 786432 | tf_op jit(solution)/shard_map/all_to_all | solution.py:20
  (205 shorter events, 76.5 us)
Async XLA Ops:
  0.0 47.0 %copy-start = (bf16[1,512,3072]{2,1,0:T(8,128)(2,1)S(1)}, bf16[1,512,3072]{2,1,0:T(8,128)(2,1)}, u32[]{:S(2)}) copy-start(bf16[1,512,3072]{2,1,0:T(8,128)(2,1)} %param.13) | copy-start | bytes 9437188
  0.0 20.3 %copy-start.17 = (s32[64]{0:T(128)}, s32[64]{0:T(128)S(1)}, u32[]{:S(2)}) copy-start(s32[64]{0:T(128)S(1)} %and_select_fusion.12) | copy-start | bytes 772
  2.1 21.6 %all-to-all-start = ((bf16[4,16,3072]{2,1,0:T(8,128)(2,1)}), bf16[4,16,3072]{2,1,0:T(8,128)(2,1)S(1)}, u32[]{:S(2)}, u32[]{:S(2)}) async-start(bf16[4,16,3072]{2,1,0:T(8,128)(2,1)} %bitcast.256), calls=%async_computation | async-start | bytes 786432 | tf_op jit(solution)/shard_map/all_to_all | solution.py:20
  23.7 20.7 %copy-start.11 = (bf16[4,16,3072]{2,1,0:T(8,128)(2,1)}, bf16[4,16,3072]{2,1,0:T(8,128)(2,1)S(1)}, u32[]{:S(2)}) copy-start(bf16[4,16,3072]{2,1,0:T(8,128)(2,1)S(1)} %all-to-all-done) | copy-start | bytes 1179652
  42.6 2.3 collective-permute-start
  47.6 2.5 collective-permute-start.1
  67.3 18.2 %all-to-all-start.3 = ((bf16[4,16,3072]{2,1,0:T(8,128)(2,1)}), bf16[4,16,3072]{2,1,0:T(8,128)(2,1)S(1)}, u32[]{:S(2)}, u32[]{:S(2)}) async-start(bf16[4,16,3072]{2,1,0:T(8,128)(2,1)} %bitcast.259), calls=%async_computation.3 | async-start | bytes 786432 | tf_op jit(solution)/shard_map/all_to_all | solution.py:20
  88.2 25.5 %copy-start.19 = (f32[48,4]{0,1:T(4,128)S(1)}, f32[48,4]{0,1:T(4,128)}, u32[]{:S(2)}) copy-start(f32[48,4]{0,1:T(4,128)} %convert_subtract_fusion) | copy-start | bytes 2308
  88.2 25.5 %copy-start.24 = (bf16[1,3072,4]{1,2,0:T(4,128)(2,1)S(1)}, bf16[1,3072,4]{1,2,0:T(4,128)(2,1)}, u32[]{:S(2)}) copy-start(bf16[1,3072,4]{1,2,0:T(4,128)(2,1)} %param.10) | copy-start | bytes 73732
  88.2 25.7 %copy-start.2 = (bf16[1,3072,512]{2,1,0:T(8,128)(2,1)S(1)}, bf16[1,3072,512]{2,1,0:T(8,128)(2,1)}, u32[]{:S(2)}) copy-start(bf16[1,3072,512]{2,1,0:T(8,128)(2,1)} %param.12) | copy-start | bytes 9437188
  88.2 7.5 %collective-permute-start.2 = (bf16[24,3072]{1,0:T(8,128)(2,1)}, bf16[24,3072]{1,0:T(8,128)(2,1)S(1)}, u32[]{:S(2)}, u32[]{:S(2)}) collective-permute-start(bf16[24,3072]{1,0:T(8,128)(2,1)} %fusion.10), channel_id=1, source_target_pairs={{0,64},{64,128},{128,192},{1,65},{65,129},{129,193},{2,66},{66,130... | collective-permute-start | bytes 442376 | tf_op jit(solution)/shard_map/ppermute | solution.py:163
  113.6 2.3 collective-permute-start.3
  117.8 2.6 collective-permute-start.4
  119.7 33.7 %copy-start.15 = (bf16[48,64]{1,0:T(8,128)(2,1)S(1)}, bf16[48,64]{1,0:T(8,128)(2,1)}, u32[]{:S(2)}) copy-start(bf16[48,64]{1,0:T(8,128)(2,1)} %get-tuple-element.100) | copy-start | bytes 18436
  119.7 34.9 %copy-start.14 = (bf16[48,64]{1,0:T(8,128)(2,1)S(1)}, bf16[48,64]{1,0:T(8,128)(2,1)}, u32[]{:S(2)}) copy-start(bf16[48,64]{1,0:T(8,128)(2,1)} %get-tuple-element.103) | copy-start | bytes 18436
  120.5 42.8 %copy-start.13 = (f32[1,3072]{1,0:T(1,128)S(1)}, f32[1,3072]{1,0:T(1,128)}, u32[]{:S(2)}) copy-start(f32[1,3072]{1,0:T(1,128)} %param.9) | copy-start | bytes 36868
  136.5 26.9 %copy-start.16 = (bf16[48,128]{1,0:T(8,128)(2,1)S(1)}, bf16[48,128]{1,0:T(8,128)(2,1)}, u32[]{:S(2)}) copy-start(bf16[48,128]{1,0:T(8,128)(2,1)} %fusion.69) | copy-start | bytes 36868
  137.5 15.9 %all-to-all-start.6 = ((bf16[4,16,3072]{2,1,0:T(8,128)(2,1)}), bf16[4,16,3072]{2,1,0:T(8,128)(2,1)}, u32[]{:S(2)}, u32[]{:S(2)}) async-start(bf16[4,16,3072]{2,1,0:T(8,128)(2,1)} %bitcast.260), calls=%async_computation.6 | async-start | bytes 786432 | tf_op jit(solution)/shard_map/all_to_all | solution.py:20
  155.8 24.1 %copy-start.3 = (bf16[1,3072,512]{2,1,0:T(8,128)(2,1)S(1)}, bf16[1,3072,512]{2,1,0:T(8,128)(2,1)}, u32[]{:S(2)}) copy-start(bf16[1,3072,512]{2,1,0:T(8,128)(2,1)} %param.12) | copy-start | bytes 9437188
  155.8 7.3 %collective-permute-start.5 = (bf16[24,3072]{1,0:T(8,128)(2,1)S(1)}, bf16[24,3072]{1,0:T(8,128)(2,1)S(1)}, u32[]{:S(2)}, u32[]{:S(2)}) collective-permute-start(bf16[24,3072]{1,0:T(8,128)(2,1)S(1)} %fusion.11), channel_id=1, source_target_pairs={{0,64},{64,128},{128,192},{1,65},{65,129},{129,193},{2,66},{66,130... | collective-permute-start | bytes 442376 | tf_op jit(solution)/shard_map/ppermute | solution.py:163
  179.7 2.3 collective-permute-start.6
  183.8 2.4 collective-permute-start.7
  203.4 15.9 %all-to-all-start.9 = ((bf16[4,16,3072]{2,1,0:T(8,128)(2,1)}), bf16[4,16,3072]{2,1,0:T(8,128)(2,1)}, u32[]{:S(2)}, u32[]{:S(2)}) async-start(bf16[4,16,3072]{2,1,0:T(8,128)(2,1)} %bitcast.258), calls=%async_computation.9 | async-start | bytes 786432 | tf_op jit(solution)/shard_map/all_to_all | solution.py:20
  221.6 24.1 %copy-start.4 = (bf16[1,3072,512]{2,1,0:T(8,128)(2,1)S(1)}, bf16[1,3072,512]{2,1,0:T(8,128)(2,1)}, u32[]{:S(2)}) copy-start(bf16[1,3072,512]{2,1,0:T(8,128)(2,1)} %param.12) | copy-start | bytes 9437188
  221.7 7.3 %collective-permute-start.8 = (bf16[24,3072]{1,0:T(8,128)(2,1)S(1)}, bf16[24,3072]{1,0:T(8,128)(2,1)S(1)}, u32[]{:S(2)}, u32[]{:S(2)}) collective-permute-start(bf16[24,3072]{1,0:T(8,128)(2,1)S(1)} %fusion.12), channel_id=1, source_target_pairs={{0,64},{64,128},{128,192},{1,65},{65,129},{129,193},{2,66},{66,130... | collective-permute-start | bytes 442376 | tf_op jit(solution)/shard_map/ppermute | solution.py:163
  245.6 2.3 collective-permute-start.9
  249.7 2.6 collective-permute-start.10
  269.5 15.9 %all-to-all-start.12 = ((bf16[4,16,3072]{2,1,0:T(8,128)(2,1)}), bf16[4,16,3072]{2,1,0:T(8,128)(2,1)}, u32[]{:S(2)}, u32[]{:S(2)}) async-start(bf16[4,16,3072]{2,1,0:T(8,128)(2,1)} %bitcast.257), calls=%async_computation.12 | async-start | bytes 786432 | tf_op jit(solution)/shard_map/all_to_all | solution.py:20
  288.4 25.0 %copy-start.5 = (bf16[1,3072,512]{2,1,0:T(8,128)(2,1)S(1)}, bf16[1,3072,512]{2,1,0:T(8,128)(2,1)}, u32[]{:S(2)}) copy-start(bf16[1,3072,512]{2,1,0:T(8,128)(2,1)} %param.12) | copy-start | bytes 9437188
  288.4 7.5 %collective-permute-start.11 = (bf16[24,3072]{1,0:T(8,128)(2,1)}, bf16[24,3072]{1,0:T(8,128)(2,1)S(1)}, u32[]{:S(2)}, u32[]{:S(2)}) collective-permute-start(bf16[24,3072]{1,0:T(8,128)(2,1)} %fusion.13), channel_id=1, source_target_pairs={{0,64},{64,128},{128,192},{1,65},{65,129},{129,193},{2,66},{66,130... | collective-permute-start | bytes 442376 | tf_op jit(solution)/shard_map/ppermute | solution.py:163
  312.5 2.3 collective-permute-start.12
  317.3 2.5 collective-permute-start.13
  (12 other events, 78.2 us)

commit v4 on v3

--- a/solution.py
+++ b/solution.py
@@ -123,14 +123,15 @@
     total = total == jnp.arange(SHARERS * sent_rows, dtype=jnp.int32)[None, :] % sent_rows
     total = total.astype(jnp.bfloat16)
 
+    dues = [jnp.int32(tick) - section_pos for tick in range(ticks)]
+    starts = [(jnp.clip(due, 0, pairs - 1) * held).astype(jnp.uint32) for due in dues]
     entry = entrance(0, entering)
     arriving = jnp.zeros((held, width), jnp.bfloat16)
     stored = jnp.zeros((16, width), jnp.float32)
     for tick in range(ticks):
-        due = tick - section_pos
-        pair = jnp.clip(due, 0, pairs - 1)
+        due, start = dues[tick], starts[tick]
         pick, first_place, second_place, sign = (
-            lax.dynamic_slice_in_dim(table, pair * held, held, 0)
+            lax.dynamic_slice_in_dim(table, start, held, 0)
             for table in (pick_all, first_all, second_all, sign_all)
         )
         hidden = jnp.where(section_pos == 0, entry, arriving)
@@ -142,8 +143,8 @@
             pick, normed, (((0,), (0,)), ((), ())), preferred_element_type=jnp.float32
         ).astype(jnp.bfloat16)
         if tick == 0:
-            sent, first_all, second_all, sign_all, total = barrier(
-                (sent, first_all, second_all, sign_all, total)
+            sent, first_all, second_all, sign_all, total, dues, starts = barrier(
+                (sent, first_all, second_all, sign_all, total, dues, starts)
             )
         own = exchange(sent, SLICES, SHARERS)
         other = lax.ppermute(own, "expert", CORES)

time: 357 us -> 346 us (0.969)
  blocking collectives: 175 us -> 218 us
  waiting for transfers between devices: 64.7 us -> 29.9 us
  starting transfers between devices: 44.1 us -> 30.2 us
  matrix products: 48.2 us -> 44.2 us
    all_to_all x11 -> x14, blocking collectives: 175 us -> 218 us  [exchange(): lax.all_to_all(chunks, 'expert', split_axis=0, concat_axis=0, axis_index_...]
    all_to_all x5 -> x2, waiting for transfers between devices: 49 us -> 14.8 us  [exchange(): lax.all_to_all(chunks, 'expert', split_axis=0, concat_axis=0, axis_index_...]
    all_to_all x5 -> x2, starting transfers between devices: 27.5 us -> 13.5 us  [exchange(): lax.all_to_all(chunks, 'expert', split_axis=0, concat_axis=0, axis_index_...]
    dot_general x23, matrix products: 21.7 us -> 16.7 us  [choose(): return jnp.dot(picks, rows, preferred_element_type=jnp.float32)]
  transfers between devices with their start and end apart: 19 -> 16, of which waited for: 19 -> 16; matrix products, arithmetic and copies ran while one was open for 9% -> 9% of each run, Pallas kernels for 0% -> 0%
where the time goes in v4:
time: 346 us; the launch traced here: 344 us
  blocking collectives  218 us (63%)
  matrix products  44.2 us (13%)
  starting transfers between devices  30.2 us (9%)
  waiting for transfers between devices  29.9 us (9%)
  other arithmetic  15.3 us (4%)
  local copies, waits for them, and re-layouts  5.97 us (2%)
    all_to_all x14, blocking collectives, exchange(): lax.all_to_all(chunks, 'expert', split_axis=0, concat_axis=0, axis_index_...  218 us
    dot_general x23, matrix products, choose(): return jnp.dot(picks, rows, preferred_element_type=jnp.float32)  16.7 us
    all_to_all x2, waiting for transfers between devices, exchange(): lax.all_to_all(chunks, 'expert', split_axis=0, concat_axis=0, axis_index_...  14.8 us
    ppermute x4, starting transfers between devices, on_device(): lax.ppermute(result, 'section', [(i, i + 1) for i in range(sections - 1)])  13.8 us
    all_to_all x2, starting transfers between devices, exchange(): lax.all_to_all(chunks, 'expert', split_axis=0, concat_axis=0, axis_index_...  13.5 us
    ppermute x4, waiting for transfers between devices, on_device(): lax.ppermute(result, 'section', [(i, i + 1) for i in range(sections - 1)])  7.16 us
  transfers between devices with their start and end apart: 16, of which 16 were waited for; matrix products, arithmetic and copies ran while one was open for 9% of the time, Pallas kernels for 0%

profile of v4, /device:TPU:16, one launch (start us, length us, event | category | flops | bytes accessed | tf_op | source)
XLA Modules:
  0.0 344.4 jit_solution(12291445802787013539)
XLA Ops:
  2.8 8.5 %all-to-all-start = ((bf16[4,16,3072]{2,1,0:T(8,128)(2,1)}), bf16[4,16,3072]{2,1,0:T(8,128)(2,1)S(1)}, u32[]{:S(2)}, u32[]{:S(2)}) async-start(bf16[4,16,3072]{2,1,0:T(8,128)(2,1)} %bitcast.262), calls=%async_computation | async-start | bytes 786432 | tf_op jit(solution)/shard_map/all_to_all | solution.py:20
  15.7 1.5 fusion.69
  17.8 1.5 fusion.99
  20.6 3.8 %all-to-all-done = bf16[4,16,3072]{2,1,0:T(8,128)(2,1)S(1)} async-done(((bf16[4,16,3072]{2,1,0:T(8,128)(2,1)}), bf16[4,16,3072]{2,1,0:T(8,128)(2,1)S(1)}, u32[]{:S(2)}, u32[]{:S(2)}) %all-to-all-start) | async-done | bytes 393248 | tf_op jit(solution)/shard_map/all_to_all | solution.py:20
  28.1 15.3 %all_to_all.80 = bf16[8,16,3072]{2,1,0:T(8,128)(2,1)S(1)} all-to-all(bf16[8,16,3072]{2,1,0:T(8,128)(2,1)S(1)} %bitcast.253), channel_id=1, replica_groups={{0,2,4,6,8,10,12,14},{1,3,5,7,9,11,13,15},{16,18,20,22,24,26,28,30},{17..., dimensions={0} | all-to-all | bytes 1572864 | tf_op jit(solution)/shard_map/all_to_all | solution.py:20
  51.1 16.0 %all_to_all.81 = bf16[8,16,3072]{2,1,0:T(8,128)(2,1)S(1)} all-to-all(bf16[8,16,3072]{2,1,0:T(8,128)(2,1)S(1)} %bitcast.257), channel_id=1, replica_groups={{0,2,4,6,8,10,12,14},{1,3,5,7,9,11,13,15},{16,18,20,22,24,26,28,30},{17..., dimensions={0} | all-to-all | bytes 1572864 | tf_op jit(solution)/shard_map/all_to_all | solution.py:20
  68.1 5.1 %all-to-all-start.3 = ((bf16[4,16,3072]{2,1,0:T(8,128)(2,1)}), bf16[4,16,3072]{2,1,0:T(8,128)(2,1)S(1)}, u32[]{:S(2)}, u32[]{:S(2)}) async-start(bf16[4,16,3072]{2,1,0:T(8,128)(2,1)} %bitcast.263), calls=%async_computation.3 | async-start | bytes 786432 | tf_op jit(solution)/shard_map/all_to_all | solution.py:20
  73.7 11.0 %all-to-all-done.3 = bf16[4,16,3072]{2,1,0:T(8,128)(2,1)S(1)} async-done(((bf16[4,16,3072]{2,1,0:T(8,128)(2,1)}), bf16[4,16,3072]{2,1,0:T(8,128)(2,1)S(1)}, u32[]{:S(2)}, u32[]{:S(2)}) %all-to-all-start.3) | async-done | bytes 393248 | tf_op jit(solution)/shard_map/all_to_all | solution.py:20
  85.8 1.5 fusion.10
  87.3 3.4 collective-permute-start.2
  90.8 1.2 convolution_convert_fusion.21
  92.0 1.8 fusion.111
  96.9 15.9 %all_to_all.82 = bf16[8,16,3072]{2,1,0:T(8,128)(2,1)S(1)} all-to-all(bf16[8,16,3072]{2,1,0:T(8,128)(2,1)S(1)} %bitcast.254), channel_id=1, replica_groups={{0,2,4,6,8,10,12,14},{1,3,5,7,9,11,13,15},{16,18,20,22,24,26,28,30},{17..., dimensions={0} | all-to-all | bytes 1572864 | tf_op jit(solution)/shard_map/all_to_all | solution.py:20
  113.6 1.5 collective-permute-done.3
  119.8 15.9 %all_to_all.83 = bf16[8,16,3072]{2,1,0:T(8,128)(2,1)S(1)} all-to-all(bf16[8,16,3072]{2,1,0:T(8,128)(2,1)S(1)} %bitcast.258), channel_id=1, replica_groups={{0,2,4,6,8,10,12,14},{1,3,5,7,9,11,13,15},{16,18,20,22,24,26,28,30},{17..., dimensions={0} | all-to-all | bytes 1572864 | tf_op jit(solution)/shard_map/all_to_all | solution.py:20
  136.0 15.5 %all_to_all.84 = bf16[4,16,3072]{2,1,0:T(8,128)(2,1)S(1)} all-to-all(bf16[4,16,3072]{2,1,0:T(8,128)(2,1)S(1)} %bitcast.265), channel_id=1, replica_groups={{0,16,32,48},{1,17,33,49},{2,18,34,50},{3,19,35,51},{4,20,36,52},{5,21,..., dimensions={0} | all-to-all | bytes 786432 | tf_op jit(solution)/shard_map/all_to_all | solution.py:20
  152.5 3.4 collective-permute-start.5
  158.1 2.0 collective-permute-done.5
  160.8 14.6 %all_to_all.85 = bf16[8,16,3072]{2,1,0:T(8,128)(2,1)S(1)} all-to-all(bf16[8,16,3072]{2,1,0:T(8,128)(2,1)S(1)} %bitcast.255), channel_id=1, replica_groups={{0,2,4,6,8,10,12,14},{1,3,5,7,9,11,13,15},{16,18,20,22,24,26,28,30},{17..., dimensions={0} | all-to-all | bytes 1572864 | tf_op jit(solution)/shard_map/all_to_all | solution.py:20
  182.8 16.0 %all_to_all.86 = bf16[8,16,3072]{2,1,0:T(8,128)(2,1)S(1)} all-to-all(bf16[8,16,3072]{2,1,0:T(8,128)(2,1)S(1)} %bitcast.259), channel_id=1, replica_groups={{0,2,4,6,8,10,12,14},{1,3,5,7,9,11,13,15},{16,18,20,22,24,26,28,30},{17..., dimensions={0} | all-to-all | bytes 1572864 | tf_op jit(solution)/shard_map/all_to_all | solution.py:20
  199.1 16.0 %all_to_all.87 = bf16[4,16,3072]{2,1,0:T(8,128)(2,1)S(1)} all-to-all(bf16[4,16,3072]{2,1,0:T(8,128)(2,1)S(1)} %bitcast.266), channel_id=1, replica_groups={{0,16,32,48},{1,17,33,49},{2,18,34,50},{3,19,35,51},{4,20,36,52},{5,21,..., dimensions={0} | all-to-all | bytes 786432 | tf_op jit(solution)/shard_map/all_to_all | solution.py:20
  216.1 3.4 collective-permute-start.8
  221.4 2.2 collective-permute-done.8
  224.3 14.7 %all_to_all.88 = bf16[8,16,3072]{2,1,0:T(8,128)(2,1)S(1)} all-to-all(bf16[8,16,3072]{2,1,0:T(8,128)(2,1)S(1)} %bitcast.256), channel_id=1, replica_groups={{0,2,4,6,8,10,12,14},{1,3,5,7,9,11,13,15},{16,18,20,22,24,26,28,30},{17..., dimensions={0} | all-to-all | bytes 1572864 | tf_op jit(solution)/shard_map/all_to_all | solution.py:20
  239.8 1.5 collective-permute-done.9
  246.0 15.9 %all_to_all.89 = bf16[8,16,3072]{2,1,0:T(8,128)(2,1)S(1)} all-to-all(bf16[8,16,3072]{2,1,0:T(8,128)(2,1)S(1)} %bitcast.260), channel_id=1, replica_groups={{0,2,4,6,8,10,12,14},{1,3,5,7,9,11,13,15},{16,18,20,22,24,26,28,30},{17..., dimensions={0} | all-to-all | bytes 1572864 | tf_op jit(solution)/shard_map/all_to_all | solution.py:20
  262.2 15.7 %all_to_all.90 = bf16[4,16,3072]{2,1,0:T(8,128)(2,1)S(1)} all-to-all(bf16[4,16,3072]{2,1,0:T(8,128)(2,1)S(1)} %bitcast.267), channel_id=1, replica_groups={{0,16,32,48},{1,17,33,49},{2,18,34,50},{3,19,35,51},{4,20,36,52},{5,21,..., dimensions={0} | all-to-all | bytes 786432 | tf_op jit(solution)/shard_map/all_to_all | solution.py:20
  279.0 3.4 collective-permute-start.11
  284.5 2.0 collective-permute-done.11
  287.2 14.6 %all_to_all.91 = bf16[8,16,3072]{2,1,0:T(8,128)(2,1)S(1)} all-to-all(bf16[8,16,3072]{2,1,0:T(8,128)(2,1)S(1)} %bitcast.252), channel_id=1, replica_groups={{0,2,4,6,8,10,12,14},{1,3,5,7,9,11,13,15},{16,18,20,22,24,26,28,30},{17..., dimensions={0} | all-to-all | bytes 1572864 | tf_op jit(solution)/shard_map/all_to_all | solution.py:20
  309.3 16.0 %all_to_all.92 = bf16[8,16,3072]{2,1,0:T(8,128)(2,1)S(1)} all-to-all(bf16[8,16,3072]{2,1,0:T(8,128)(2,1)S(1)} %bitcast.261), channel_id=1, replica_groups={{0,2,4,6,8,10,12,14},{1,3,5,7,9,11,13,15},{16,18,20,22,24,26,28,30},{17..., dimensions={0} | all-to-all | bytes 1572864 | tf_op jit(solution)/shard_map/all_to_all | solution.py:20
  325.6 16.0 %all_to_all.93 = bf16[4,16,3072]{2,1,0:T(8,128)(2,1)S(1)} all-to-all(bf16[4,16,3072]{2,1,0:T(8,128)(2,1)S(1)} %bitcast.264), channel_id=1, replica_groups={{0,16,32,48},{1,17,33,49},{2,18,34,50},{3,19,35,51},{4,20,36,52},{5,21,..., dimensions={0} | all-to-all | bytes 786432 | tf_op jit(solution)/shard_map/all_to_all | solution.py:20
  (204 shorter events, 66.9 us)
Async XLA Ops:
  0.0 47.8 %copy-start = (bf16[1,512,3072]{2,1,0:T(8,128)(2,1)S(1)}, bf16[1,512,3072]{2,1,0:T(8,128)(2,1)}, u32[]{:S(2)}) copy-start(bf16[1,512,3072]{2,1,0:T(8,128)(2,1)} %param.13) | copy-start | bytes 9437188
  2.8 21.6 %all-to-all-start = ((bf16[4,16,3072]{2,1,0:T(8,128)(2,1)}), bf16[4,16,3072]{2,1,0:T(8,128)(2,1)S(1)}, u32[]{:S(2)}, u32[]{:S(2)}) async-start(bf16[4,16,3072]{2,1,0:T(8,128)(2,1)} %bitcast.262), calls=%async_computation | async-start | bytes 786432 | tf_op jit(solution)/shard_map/all_to_all | solution.py:20
  24.4 20.8 %copy-start.11 = (bf16[4,16,3072]{2,1,0:T(8,128)(2,1)}, bf16[4,16,3072]{2,1,0:T(8,128)(2,1)S(1)}, u32[]{:S(2)}) copy-start(bf16[4,16,3072]{2,1,0:T(8,128)(2,1)S(1)} %all-to-all-done) | copy-start | bytes 1179652
  24.4 18.9 %copy-start.24 = (bf16[1,3072,4]{1,2,0:T(4,128)(2,1)S(1)}, bf16[1,3072,4]{1,2,0:T(4,128)(2,1)}, u32[]{:S(2)}) copy-start(bf16[1,3072,4]{1,2,0:T(4,128)(2,1)} %param.10) | copy-start | bytes 73732
  24.4 20.2 %copy-start.1 = (bf16[1,3072,512]{2,1,0:T(8,128)(2,1)S(1)}, bf16[1,3072,512]{2,1,0:T(8,128)(2,1)}, u32[]{:S(2)}) copy-start(bf16[1,3072,512]{2,1,0:T(8,128)(2,1)} %param.12) | copy-start | bytes 9437188
  43.3 2.3 collective-permute-start
  48.4 2.5 collective-permute-start.1
  68.1 16.6 %all-to-all-start.3 = ((bf16[4,16,3072]{2,1,0:T(8,128)(2,1)}), bf16[4,16,3072]{2,1,0:T(8,128)(2,1)S(1)}, u32[]{:S(2)}, u32[]{:S(2)}) async-start(bf16[4,16,3072]{2,1,0:T(8,128)(2,1)} %bitcast.263), calls=%async_computation.3 | async-start | bytes 786432 | tf_op jit(solution)/shard_map/all_to_all | solution.py:20
  87.3 25.5 %copy-start.19 = (f32[48,4]{0,1:T(4,128)S(1)}, f32[48,4]{0,1:T(4,128)}, u32[]{:S(2)}) copy-start(f32[48,4]{0,1:T(4,128)} %convert_subtract_fusion) | copy-start | bytes 2308
  87.3 25.5 %copy-start.25 = (bf16[1,3072,4]{1,2,0:T(4,128)(2,1)S(1)}, bf16[1,3072,4]{1,2,0:T(4,128)(2,1)}, u32[]{:S(2)}) copy-start(bf16[1,3072,4]{1,2,0:T(4,128)(2,1)} %param.10) | copy-start | bytes 73732
  87.3 25.7 %copy-start.2 = (bf16[1,3072,512]{2,1,0:T(8,128)(2,1)S(1)}, bf16[1,3072,512]{2,1,0:T(8,128)(2,1)}, u32[]{:S(2)}) copy-start(bf16[1,3072,512]{2,1,0:T(8,128)(2,1)} %param.12) | copy-start | bytes 9437188
  87.3 7.5 %collective-permute-start.2 = (bf16[24,3072]{1,0:T(8,128)(2,1)}, bf16[24,3072]{1,0:T(8,128)(2,1)S(1)}, u32[]{:S(2)}, u32[]{:S(2)}) collective-permute-start(bf16[24,3072]{1,0:T(8,128)(2,1)} %fusion.10), channel_id=1, source_target_pairs={{0,64},{64,128},{128,192},{1,65},{65,129},{129,193},{2,66},{66,130... | collective-permute-start | bytes 442376 | tf_op jit(solution)/shard_map/ppermute | solution.py:164
  112.8 2.3 collective-permute-start.3
  117.0 2.6 collective-permute-start.4
  118.8 32.7 %copy-start.16 = (bf16[48,64]{1,0:T(8,128)(2,1)S(1)}, bf16[48,64]{1,0:T(8,128)(2,1)}, u32[]{:S(2)}) copy-start(bf16[48,64]{1,0:T(8,128)(2,1)} %get-tuple-element.109) | copy-start | bytes 18436
  118.8 32.8 %copy-start.15 = (bf16[48,64]{1,0:T(8,128)(2,1)S(1)}, bf16[48,64]{1,0:T(8,128)(2,1)}, u32[]{:S(2)}) copy-start(bf16[48,64]{1,0:T(8,128)(2,1)} %get-tuple-element.112) | copy-start | bytes 18436
  119.8 40.5 %copy-start.13 = (f32[1,3072]{1,0:T(1,128)S(1)}, f32[1,3072]{1,0:T(1,128)}, u32[]{:S(2)}) copy-start(f32[1,3072]{1,0:T(1,128)} %param.9) | copy-start | bytes 36868
  135.7 24.6 %copy-start.14 = (bf16[48,128]{1,0:T(8,128)(2,1)S(1)}, bf16[48,128]{1,0:T(8,128)(2,1)}, u32[]{:S(2)}) copy-start(bf16[48,128]{1,0:T(8,128)(2,1)} %fusion.69) | copy-start | bytes 36868
  152.5 23.8 %copy-start.3 = (bf16[1,3072,512]{2,1,0:T(8,128)(2,1)S(1)}, bf16[1,3072,512]{2,1,0:T(8,128)(2,1)}, u32[]{:S(2)}) copy-start(bf16[1,3072,512]{2,1,0:T(8,128)(2,1)} %param.12) | copy-start | bytes 9437188
  152.5 7.5 %collective-permute-start.5 = (bf16[24,3072]{1,0:T(8,128)(2,1)}, bf16[24,3072]{1,0:T(8,128)(2,1)S(1)}, u32[]{:S(2)}, u32[]{:S(2)}) collective-permute-start(bf16[24,3072]{1,0:T(8,128)(2,1)} %fusion.11), channel_id=1, source_target_pairs={{0,64},{64,128},{128,192},{1,65},{65,129},{129,193},{2,66},{66,130... | collective-permute-start | bytes 442376 | tf_op jit(solution)/shard_map/ppermute | solution.py:164
  175.4 2.3 collective-permute-start.6
  180.2 2.5 collective-permute-start.7
  216.1 22.9 %copy-start.20 = (f32[48,4]{0,1:T(4,128)S(1)}, f32[48,4]{0,1:T(4,128)}, u32[]{:S(2)}) copy-start(f32[48,4]{0,1:T(4,128)} %convert_subtract_fusion) | copy-start | bytes 2308
  216.1 22.9 %copy-start.26 = (bf16[1,3072,4]{1,2,0:T(4,128)(2,1)S(1)}, bf16[1,3072,4]{1,2,0:T(4,128)(2,1)}, u32[]{:S(2)}) copy-start(bf16[1,3072,4]{1,2,0:T(4,128)(2,1)} %param.10) | copy-start | bytes 73732
  216.1 23.1 %copy-start.4 = (bf16[1,3072,512]{2,1,0:T(8,128)(2,1)S(1)}, bf16[1,3072,512]{2,1,0:T(8,128)(2,1)}, u32[]{:S(2)}) copy-start(bf16[1,3072,512]{2,1,0:T(8,128)(2,1)} %param.12) | copy-start | bytes 9437188
  216.1 7.5 %collective-permute-start.8 = (bf16[24,3072]{1,0:T(8,128)(2,1)}, bf16[24,3072]{1,0:T(8,128)(2,1)S(1)}, u32[]{:S(2)}, u32[]{:S(2)}) collective-permute-start(bf16[24,3072]{1,0:T(8,128)(2,1)} %fusion.12), channel_id=1, source_target_pairs={{0,64},{64,128},{128,192},{1,65},{65,129},{129,193},{2,66},{66,130... | collective-permute-start | bytes 442376 | tf_op jit(solution)/shard_map/ppermute | solution.py:164
  239.0 2.3 collective-permute-start.9
  243.2 2.6 collective-permute-start.10
  279.0 23.8 %copy-start.5 = (bf16[1,3072,512]{2,1,0:T(8,128)(2,1)S(1)}, bf16[1,3072,512]{2,1,0:T(8,128)(2,1)}, u32[]{:S(2)}) copy-start(bf16[1,3072,512]{2,1,0:T(8,128)(2,1)} %param.12) | copy-start | bytes 9437188
  279.0 7.5 %collective-permute-start.11 = (bf16[24,3072]{1,0:T(8,128)(2,1)}, bf16[24,3072]{1,0:T(8,128)(2,1)S(1)}, u32[]{:S(2)}, u32[]{:S(2)}) collective-permute-start(bf16[24,3072]{1,0:T(8,128)(2,1)} %fusion.13), channel_id=1, source_target_pairs={{0,64},{64,128},{128,192},{1,65},{65,129},{129,193},{2,66},{66,130... | collective-permute-start | bytes 442376 | tf_op jit(solution)/shard_map/ppermute | solution.py:164
  301.8 2.3 collective-permute-start.12
  306.6 2.5 collective-permute-start.13
  (11 other events, 57.4 us)

commit v5 on v4

--- a/solution.py
+++ b/solution.py
@@ -114,10 +114,10 @@
         spot % tokens,
     )
 
-    def entrance(pair, entering):
+    def entry_picks(pair):
         source = spot_block * spare + spot_token * micro_count + pair * PAIR + spot_micro
         picks = source[:, None] == jnp.arange(E * spare, dtype=jnp.int32)[None, :]
-        return choose(picks.astype(jnp.bfloat16), entering).astype(jnp.bfloat16)
+        return picks.astype(jnp.bfloat16)
 
     total = jnp.arange(E * sent_rows, dtype=jnp.int32)[:, None] % sent_rows
     total = total == jnp.arange(SHARERS * sent_rows, dtype=jnp.int32)[None, :] % sent_rows
@@ -125,7 +125,8 @@
 
     dues = [jnp.int32(tick) - section_pos for tick in range(ticks)]
     starts = [(jnp.clip(due, 0, pairs - 1) * held).astype(jnp.uint32) for due in dues]
-    entry = entrance(0, entering)
+    entries = [entry_picks(pair) for pair in range(pairs)]
+    entry = choose(entries[0], entering).astype(jnp.bfloat16)
     arriving = jnp.zeros((held, width), jnp.bfloat16)
     stored = jnp.zeros((16, width), jnp.float32)
     for tick in range(ticks):
@@ -143,8 +144,8 @@
             pick, normed, (((0,), (0,)), ((), ())), preferred_element_type=jnp.float32
         ).astype(jnp.bfloat16)
         if tick == 0:
-            sent, first_all, second_all, sign_all, total, dues, starts = barrier(
-                (sent, first_all, second_all, sign_all, total, dues, starts)
+            sent, first_all, second_all, sign_all, total, dues, starts, entries = barrier(
+                (sent, first_all, second_all, sign_all, total, dues, starts, entries)
             )
         own = exchange(sent, SLICES, SHARERS)
         other = lax.ppermute(own, "expert", CORES)
@@ -165,7 +166,7 @@
                 result, "section", [(i, i + 1) for i in range(sections - 1)]
             )
         if tick + 1 < pairs:
-            entry = entrance(tick + 1, entering)
+            entry = choose(entries[tick + 1], entering).astype(jnp.bfloat16)
         target = (due * PAIR + spot_micro) * 4 + spot_token
         held_now = (spot_block == expert) & (due >= 0) & (due < pairs)
         target = jnp.where(held_now, target, -1)

time: 346 us -> 340 us (0.983)
  blocking collectives: 218 us -> 235 us
  waiting for transfers between devices: 29.9 us -> 20.1 us
  starting transfers between devices: 30.2 us -> 25 us
  matrix products: 44.2 us -> 39.6 us
    all_to_all x14 -> x15, blocking collectives: 218 us -> 235 us  [exchange(): lax.all_to_all(chunks, 'expert', split_axis=0, concat_axis=0, axis_index_...]
    all_to_all x2 -> x1, waiting for transfers between devices: 14.8 us -> 3.03 us  [exchange(): lax.all_to_all(chunks, 'expert', split_axis=0, concat_axis=0, axis_index_...]
    all_to_all x2 -> x1, starting transfers between devices: 13.5 us -> 8.46 us  [exchange(): lax.all_to_all(chunks, 'expert', split_axis=0, concat_axis=0, axis_index_...]
    dot_general x23, matrix products: 16.7 us -> 12.6 us  [choose(): return jnp.dot(picks, rows, preferred_element_type=jnp.float32)]
  transfers between devices with their start and end apart: 16 -> 15, of which waited for: 16 -> 15; matrix products, arithmetic and copies ran while one was open for 9% -> 9% of each run, Pallas kernels for 0% -> 0%
where the time goes in v5:
time: 340 us; the launch traced here: 339 us
  blocking collectives  235 us (69%)
  matrix products  39.6 us (12%)
  starting transfers between devices  25 us (7%)
  waiting for transfers between devices  20.1 us (6%)
  other arithmetic  13.5 us (4%)
  local copies, waits for them, and re-layouts  4.52 us (1%)
    all_to_all x15, blocking collectives, exchange(): lax.all_to_all(chunks, 'expert', split_axis=0, concat_axis=0, axis_index_...  235 us
    ppermute x4, starting transfers between devices, on_device(): lax.ppermute(result, 'section', [(i, i + 1) for i in range(sections - 1)])  13.8 us
    dot_general x23, matrix products, choose(): return jnp.dot(picks, rows, preferred_element_type=jnp.float32)  12.6 us
    all_to_all x1, starting transfers between devices, exchange(): lax.all_to_all(chunks, 'expert', split_axis=0, concat_axis=0, axis_index_...  8.46 us
    ppermute x4, waiting for transfers between devices, on_device(): lax.ppermute(result, 'section', [(i, i + 1) for i in range(sections - 1)])  7.93 us
  transfers between devices with their start and end apart: 15, of which 15 were waited for; matrix products, arithmetic and copies ran while one was open for 9% of the time, Pallas kernels for 0%

profile of v5, /device:TPU:16, one launch (start us, length us, event | category | flops | bytes accessed | tf_op | source)
XLA Modules:
  0.0 338.8 jit_solution(8662487202295722392)
XLA Ops:
  0.5 1.2 reshape.597
  2.7 8.5 %all-to-all-start = ((bf16[4,16,3072]{2,1,0:T(8,128)(2,1)}), bf16[4,16,3072]{2,1,0:T(8,128)(2,1)S(1)}, u32[]{:S(2)}, u32[]{:S(2)}) async-start(bf16[4,16,3072]{2,1,0:T(8,128)(2,1)} %bitcast.263), calls=%async_computation | async-start | bytes 786432 | tf_op jit(solution)/shard_map/all_to_all | solution.py:20
  16.3 1.5 fusion.99
  17.8 1.5 fusion.69
  21.3 3.0 all-to-all-done
  27.4 15.2 %all_to_all.80 = bf16[8,16,3072]{2,1,0:T(8,128)(2,1)S(1)} all-to-all(bf16[8,16,3072]{2,1,0:T(8,128)(2,1)S(1)} %bitcast.254), channel_id=1, replica_groups={{0,2,4,6,8,10,12,14},{1,3,5,7,9,11,13,15},{16,18,20,22,24,26,28,30},{17..., dimensions={0} | all-to-all | bytes 1572864 | tf_op jit(solution)/shard_map/all_to_all | solution.py:20
  43.5 1.4 collective-permute-done
  49.6 16.0 %all_to_all.81 = bf16[8,16,3072]{2,1,0:T(8,128)(2,1)S(1)} all-to-all(bf16[8,16,3072]{2,1,0:T(8,128)(2,1)S(1)} %bitcast.258), channel_id=1, replica_groups={{0,2,4,6,8,10,12,14},{1,3,5,7,9,11,13,15},{16,18,20,22,24,26,28,30},{17..., dimensions={0} | all-to-all | bytes 1572864 | tf_op jit(solution)/shard_map/all_to_all | solution.py:20
  65.9 18.0 %all_to_all.82 = bf16[4,16,3072]{2,1,0:T(8,128)(2,1)S(1)} all-to-all(bf16[4,16,3072]{2,1,0:T(8,128)(2,1)S(1)} %bitcast.265), channel_id=1, replica_groups={{0,16,32,48},{1,17,33,49},{2,18,34,50},{3,19,35,51},{4,20,36,52},{5,21,..., dimensions={0} | all-to-all | bytes 786432 | tf_op jit(solution)/shard_map/all_to_all | solution.py:20
  84.3 3.5 %collective-permute-start.2 = (bf16[24,3072]{1,0:T(8,128)(2,1)S(1)}, bf16[24,3072]{1,0:T(8,128)(2,1)S(1)}, u32[]{:S(2)}, u32[]{:S(2)}) collective-permute-start(bf16[24,3072]{1,0:T(8,128)(2,1)S(1)} %fusion.10), channel_id=1, source_target_pairs={{0,64},{64,128},{128,192},{1,65},{65,129},{129,193},{2,66},{66,130... | collective-permute-start | bytes 442376 | tf_op jit(solution)/shard_map/ppermute | solution.py:165
  87.8 1.2 convolution_convert_fusion.21
  89.8 1.8 collective-permute-done.2
  92.3 14.6 %all_to_all.83 = bf16[8,16,3072]{2,1,0:T(8,128)(2,1)S(1)} all-to-all(bf16[8,16,3072]{2,1,0:T(8,128)(2,1)S(1)} %bitcast.255), channel_id=1, replica_groups={{0,2,4,6,8,10,12,14},{1,3,5,7,9,11,13,15},{16,18,20,22,24,26,28,30},{17..., dimensions={0} | all-to-all | bytes 1572864 | tf_op jit(solution)/shard_map/all_to_all | solution.py:20
  107.8 1.5 collective-permute-done.3
  113.9 15.9 %all_to_all.84 = bf16[8,16,3072]{2,1,0:T(8,128)(2,1)S(1)} all-to-all(bf16[8,16,3072]{2,1,0:T(8,128)(2,1)S(1)} %bitcast.259), channel_id=1, replica_groups={{0,2,4,6,8,10,12,14},{1,3,5,7,9,11,13,15},{16,18,20,22,24,26,28,30},{17..., dimensions={0} | all-to-all | bytes 1572864 | tf_op jit(solution)/shard_map/all_to_all | solution.py:20
  130.1 15.8 %all_to_all.85 = bf16[4,16,3072]{2,1,0:T(8,128)(2,1)S(1)} all-to-all(bf16[4,16,3072]{2,1,0:T(8,128)(2,1)S(1)} %bitcast.266), channel_id=1, replica_groups={{0,16,32,48},{1,17,33,49},{2,18,34,50},{3,19,35,51},{4,20,36,52},{5,21,..., dimensions={0} | all-to-all | bytes 786432 | tf_op jit(solution)/shard_map/all_to_all | solution.py:20
  147.0 3.4 %collective-permute-start.5 = (bf16[24,3072]{1,0:T(8,128)(2,1)}, bf16[24,3072]{1,0:T(8,128)(2,1)S(1)}, u32[]{:S(2)}, u32[]{:S(2)}) collective-permute-start(bf16[24,3072]{1,0:T(8,128)(2,1)} %fusion.11), channel_id=1, source_target_pairs={{0,64},{64,128},{128,192},{1,65},{65,129},{129,193},{2,66},{66,130... | collective-permute-start | bytes 442376 | tf_op jit(solution)/shard_map/ppermute | solution.py:165
  152.5 2.0 collective-permute-done.5
  155.2 14.6 %all_to_all.86 = bf16[8,16,3072]{2,1,0:T(8,128)(2,1)S(1)} all-to-all(bf16[8,16,3072]{2,1,0:T(8,128)(2,1)S(1)} %bitcast.256), channel_id=1, replica_groups={{0,2,4,6,8,10,12,14},{1,3,5,7,9,11,13,15},{16,18,20,22,24,26,28,30},{17..., dimensions={0} | all-to-all | bytes 1572864 | tf_op jit(solution)/shard_map/all_to_all | solution.py:20
  177.3 16.0 %all_to_all.87 = bf16[8,16,3072]{2,1,0:T(8,128)(2,1)S(1)} all-to-all(bf16[8,16,3072]{2,1,0:T(8,128)(2,1)S(1)} %bitcast.260), channel_id=1, replica_groups={{0,2,4,6,8,10,12,14},{1,3,5,7,9,11,13,15},{16,18,20,22,24,26,28,30},{17..., dimensions={0} | all-to-all | bytes 1572864 | tf_op jit(solution)/shard_map/all_to_all | solution.py:20
  193.5 16.0 %all_to_all.88 = bf16[4,16,3072]{2,1,0:T(8,128)(2,1)S(1)} all-to-all(bf16[4,16,3072]{2,1,0:T(8,128)(2,1)S(1)} %bitcast.267), channel_id=1, replica_groups={{0,16,32,48},{1,17,33,49},{2,18,34,50},{3,19,35,51},{4,20,36,52},{5,21,..., dimensions={0} | all-to-all | bytes 786432 | tf_op jit(solution)/shard_map/all_to_all | solution.py:20
  210.5 3.4 %collective-permute-start.8 = (bf16[24,3072]{1,0:T(8,128)(2,1)}, bf16[24,3072]{1,0:T(8,128)(2,1)S(1)}, u32[]{:S(2)}, u32[]{:S(2)}) collective-permute-start(bf16[24,3072]{1,0:T(8,128)(2,1)} %fusion.12), channel_id=1, source_target_pairs={{0,64},{64,128},{128,192},{1,65},{65,129},{129,193},{2,66},{66,130... | collective-permute-start | bytes 442376 | tf_op jit(solution)/shard_map/ppermute | solution.py:165
  215.8 2.2 collective-permute-done.8
  218.8 14.7 %all_to_all.89 = bf16[8,16,3072]{2,1,0:T(8,128)(2,1)S(1)} all-to-all(bf16[8,16,3072]{2,1,0:T(8,128)(2,1)S(1)} %bitcast.257), channel_id=1, replica_groups={{0,2,4,6,8,10,12,14},{1,3,5,7,9,11,13,15},{16,18,20,22,24,26,28,30},{17..., dimensions={0} | all-to-all | bytes 1572864 | tf_op jit(solution)/shard_map/all_to_all | solution.py:20
  234.3 1.5 collective-permute-done.9
  240.5 15.9 %all_to_all.90 = bf16[8,16,3072]{2,1,0:T(8,128)(2,1)S(1)} all-to-all(bf16[8,16,3072]{2,1,0:T(8,128)(2,1)S(1)} %bitcast.261), channel_id=1, replica_groups={{0,2,4,6,8,10,12,14},{1,3,5,7,9,11,13,15},{16,18,20,22,24,26,28,30},{17..., dimensions={0} | all-to-all | bytes 1572864 | tf_op jit(solution)/shard_map/all_to_all | solution.py:20
  256.7 15.8 %all_to_all.91 = bf16[4,16,3072]{2,1,0:T(8,128)(2,1)S(1)} all-to-all(bf16[4,16,3072]{2,1,0:T(8,128)(2,1)S(1)} %bitcast.268), channel_id=1, replica_groups={{0,16,32,48},{1,17,33,49},{2,18,34,50},{3,19,35,51},{4,20,36,52},{5,21,..., dimensions={0} | all-to-all | bytes 786432 | tf_op jit(solution)/shard_map/all_to_all | solution.py:20
  273.5 3.4 %collective-permute-start.11 = (bf16[24,3072]{1,0:T(8,128)(2,1)}, bf16[24,3072]{1,0:T(8,128)(2,1)S(1)}, u32[]{:S(2)}, u32[]{:S(2)}) collective-permute-start(bf16[24,3072]{1,0:T(8,128)(2,1)} %fusion.13), channel_id=1, source_target_pairs={{0,64},{64,128},{128,192},{1,65},{65,129},{129,193},{2,66},{66,130... | collective-permute-start | bytes 442376 | tf_op jit(solution)/shard_map/ppermute | solution.py:165
  279.0 2.0 collective-permute-done.11
  281.7 14.6 %all_to_all.92 = bf16[8,16,3072]{2,1,0:T(8,128)(2,1)S(1)} all-to-all(bf16[8,16,3072]{2,1,0:T(8,128)(2,1)S(1)} %bitcast.253), channel_id=1, replica_groups={{0,2,4,6,8,10,12,14},{1,3,5,7,9,11,13,15},{16,18,20,22,24,26,28,30},{17..., dimensions={0} | all-to-all | bytes 1572864 | tf_op jit(solution)/shard_map/all_to_all | solution.py:20
  303.8 15.9 %all_to_all.93 = bf16[8,16,3072]{2,1,0:T(8,128)(2,1)S(1)} all-to-all(bf16[8,16,3072]{2,1,0:T(8,128)(2,1)S(1)} %bitcast.262), channel_id=1, replica_groups={{0,2,4,6,8,10,12,14},{1,3,5,7,9,11,13,15},{16,18,20,22,24,26,28,30},{17..., dimensions={0} | all-to-all | bytes 1572864 | tf_op jit(solution)/shard_map/all_to_all | solution.py:20
  320.0 16.0 %all_to_all.94 = bf16[4,16,3072]{2,1,0:T(8,128)(2,1)S(1)} all-to-all(bf16[4,16,3072]{2,1,0:T(8,128)(2,1)S(1)} %bitcast.264), channel_id=1, replica_groups={{0,16,32,48},{1,17,33,49},{2,18,34,50},{3,19,35,51},{4,20,36,52},{5,21,..., dimensions={0} | all-to-all | bytes 786432 | tf_op jit(solution)/shard_map/all_to_all | solution.py:20
  (204 shorter events, 59.8 us)
Async XLA Ops:
  0.0 46.3 %copy-start = (bf16[1,512,3072]{2,1,0:T(8,128)(2,1)S(1)}, bf16[1,512,3072]{2,1,0:T(8,128)(2,1)}, u32[]{:S(2)}) copy-start(bf16[1,512,3072]{2,1,0:T(8,128)(2,1)} %param.13) | copy-start | bytes 9437188
  0.5 19.4 %copy-start.17 = (s32[64]{0:T(128)}, s32[64]{0:T(128)S(1)}, u32[]{:S(2)}) copy-start(s32[64]{0:T(128)S(1)} %get-tuple-element.170) | copy-start | bytes 772
  2.7 21.6 %all-to-all-start = ((bf16[4,16,3072]{2,1,0:T(8,128)(2,1)}), bf16[4,16,3072]{2,1,0:T(8,128)(2,1)S(1)}, u32[]{:S(2)}, u32[]{:S(2)}) async-start(bf16[4,16,3072]{2,1,0:T(8,128)(2,1)} %bitcast.263), calls=%async_computation | async-start | bytes 786432 | tf_op jit(solution)/shard_map/all_to_all | solution.py:20
  24.3 19.2 %copy-start.11 = (bf16[4,16,3072]{2,1,0:T(8,128)(2,1)}, bf16[4,16,3072]{2,1,0:T(8,128)(2,1)S(1)}, u32[]{:S(2)}) copy-start(bf16[4,16,3072]{2,1,0:T(8,128)(2,1)S(1)} %all-to-all-done) | copy-start | bytes 1179652
  24.3 18.6 %copy-start.1 = (bf16[1,3072,512]{2,1,0:T(8,128)(2,1)S(1)}, bf16[1,3072,512]{2,1,0:T(8,128)(2,1)}, u32[]{:S(2)}) copy-start(bf16[1,3072,512]{2,1,0:T(8,128)(2,1)} %param.12) | copy-start | bytes 9437188
  42.7 2.3 collective-permute-start
  47.0 2.4 collective-permute-start.1
  48.7 35.2 %copy-start.14 = (bf16[48,64]{1,0:T(8,128)(2,1)S(1)}, bf16[48,64]{1,0:T(8,128)(2,1)}, u32[]{:S(2)}) copy-start(bf16[48,64]{1,0:T(8,128)(2,1)} %get-tuple-element.111) | copy-start | bytes 18436
  48.7 35.4 %copy-start.13 = (bf16[48,64]{1,0:T(8,128)(2,1)S(1)}, bf16[48,64]{1,0:T(8,128)(2,1)}, u32[]{:S(2)}) copy-start(bf16[48,64]{1,0:T(8,128)(2,1)} %get-tuple-element.114) | copy-start | bytes 18436
  49.5 38.2 %copy-start.16 = (bf16[24,64]{1,0:T(8,128)(2,1)S(1)}, bf16[24,64]{1,0:T(8,128)(2,1)}, u32[]{:S(2)}) copy-start(bf16[24,64]{1,0:T(8,128)(2,1)} %fusion.111) | copy-start | bytes 9220
  49.5 42.2 %copy-start.12 = (f32[1,3072]{1,0:T(1,128)S(1)}, f32[1,3072]{1,0:T(1,128)}, u32[]{:S(2)}) copy-start(f32[1,3072]{1,0:T(1,128)} %param.9) | copy-start | bytes 36868
  49.6 42.3 %copy-start.15 = (bf16[48,128]{1,0:T(8,128)(2,1)S(1)}, bf16[48,128]{1,0:T(8,128)(2,1)}, u32[]{:S(2)}) copy-start(bf16[48,128]{1,0:T(8,128)(2,1)} %fusion.69) | copy-start | bytes 36868
  83.9 23.1 %copy-start.19 = (f32[48,4]{0,1:T(4,128)S(1)}, f32[48,4]{0,1:T(4,128)}, u32[]{:S(2)}) copy-start(f32[48,4]{0,1:T(4,128)} %convert_subtract_fusion) | copy-start | bytes 2308
  83.9 23.1 %copy-start.25 = (bf16[1,3072,4]{1,2,0:T(4,128)(2,1)S(1)}, bf16[1,3072,4]{1,2,0:T(4,128)(2,1)}, u32[]{:S(2)}) copy-start(bf16[1,3072,4]{1,2,0:T(4,128)(2,1)} %param.10) | copy-start | bytes 73732
  84.3 22.9 %copy-start.2 = (bf16[1,3072,512]{2,1,0:T(8,128)(2,1)S(1)}, bf16[1,3072,512]{2,1,0:T(8,128)(2,1)}, u32[]{:S(2)}) copy-start(bf16[1,3072,512]{2,1,0:T(8,128)(2,1)} %param.12) | copy-start | bytes 9437188
  84.3 7.3 %collective-permute-start.2 = (bf16[24,3072]{1,0:T(8,128)(2,1)S(1)}, bf16[24,3072]{1,0:T(8,128)(2,1)S(1)}, u32[]{:S(2)}, u32[]{:S(2)}) collective-permute-start(bf16[24,3072]{1,0:T(8,128)(2,1)S(1)} %fusion.10), channel_id=1, source_target_pairs={{0,64},{64,128},{128,192},{1,65},{65,129},{129,193},{2,66},{66,130... | collective-permute-start | bytes 442376 | tf_op jit(solution)/shard_map/ppermute | solution.py:165
  107.0 2.3 collective-permute-start.3
  111.2 2.6 collective-permute-start.4
  147.0 23.8 %copy-start.3 = (bf16[1,3072,512]{2,1,0:T(8,128)(2,1)S(1)}, bf16[1,3072,512]{2,1,0:T(8,128)(2,1)}, u32[]{:S(2)}) copy-start(bf16[1,3072,512]{2,1,0:T(8,128)(2,1)} %param.12) | copy-start | bytes 9437188
  147.0 7.5 %collective-permute-start.5 = (bf16[24,3072]{1,0:T(8,128)(2,1)}, bf16[24,3072]{1,0:T(8,128)(2,1)S(1)}, u32[]{:S(2)}, u32[]{:S(2)}) collective-permute-start(bf16[24,3072]{1,0:T(8,128)(2,1)} %fusion.11), channel_id=1, source_target_pairs={{0,64},{64,128},{128,192},{1,65},{65,129},{129,193},{2,66},{66,130... | collective-permute-start | bytes 442376 | tf_op jit(solution)/shard_map/ppermute | solution.py:165
  169.8 2.3 collective-permute-start.6
  174.6 2.5 collective-permute-start.7
  210.5 22.9 %copy-start.20 = (f32[48,4]{0,1:T(4,128)S(1)}, f32[48,4]{0,1:T(4,128)}, u32[]{:S(2)}) copy-start(f32[48,4]{0,1:T(4,128)} %convert_subtract_fusion) | copy-start | bytes 2308
  210.5 22.9 %copy-start.26 = (bf16[1,3072,4]{1,2,0:T(4,128)(2,1)S(1)}, bf16[1,3072,4]{1,2,0:T(4,128)(2,1)}, u32[]{:S(2)}) copy-start(bf16[1,3072,4]{1,2,0:T(4,128)(2,1)} %param.10) | copy-start | bytes 73732
  210.5 23.1 %copy-start.4 = (bf16[1,3072,512]{2,1,0:T(8,128)(2,1)S(1)}, bf16[1,3072,512]{2,1,0:T(8,128)(2,1)}, u32[]{:S(2)}) copy-start(bf16[1,3072,512]{2,1,0:T(8,128)(2,1)} %param.12) | copy-start | bytes 9437188
  210.5 7.5 %collective-permute-start.8 = (bf16[24,3072]{1,0:T(8,128)(2,1)}, bf16[24,3072]{1,0:T(8,128)(2,1)S(1)}, u32[]{:S(2)}, u32[]{:S(2)}) collective-permute-start(bf16[24,3072]{1,0:T(8,128)(2,1)} %fusion.12), channel_id=1, source_target_pairs={{0,64},{64,128},{128,192},{1,65},{65,129},{129,193},{2,66},{66,130... | collective-permute-start | bytes 442376 | tf_op jit(solution)/shard_map/ppermute | solution.py:165
  233.4 2.3 collective-permute-start.9
  237.7 2.6 collective-permute-start.10
  273.5 23.8 %copy-start.5 = (bf16[1,3072,512]{2,1,0:T(8,128)(2,1)S(1)}, bf16[1,3072,512]{2,1,0:T(8,128)(2,1)}, u32[]{:S(2)}) copy-start(bf16[1,3072,512]{2,1,0:T(8,128)(2,1)} %param.12) | copy-start | bytes 9437188
  273.5 7.5 %collective-permute-start.11 = (bf16[24,3072]{1,0:T(8,128)(2,1)}, bf16[24,3072]{1,0:T(8,128)(2,1)S(1)}, u32[]{:S(2)}, u32[]{:S(2)}) collective-permute-start(bf16[24,3072]{1,0:T(8,128)(2,1)} %fusion.13), channel_id=1, source_target_pairs={{0,64},{64,128},{128,192},{1,65},{65,129},{129,193},{2,66},{66,130... | collective-permute-start | bytes 442376 | tf_op jit(solution)/shard_map/ppermute | solution.py:165
  296.3 2.3 collective-permute-start.12
  301.1 2.5 collective-permute-start.13
  (10 other events, 56.6 us)

commit v6 on v5

--- a/solution.py
+++ b/solution.py
@@ -100,13 +100,11 @@
 
     pick_all, first_all, second_all, sign_all = tables(routes[0], expert, rest, tokens)
 
-    spare = 16
-    own_rows = jnp.swapaxes(inputs, 0, 1).reshape(tokens * micro_count, width)
-    lay_out = (
-        jnp.arange(E * spare, dtype=jnp.int32)[:, None] % spare
-        == jnp.arange(tokens * micro_count, dtype=jnp.int32)[None, :]
-    ).astype(jnp.bfloat16)
-    entering = exchange(choose(lay_out, own_rows).astype(jnp.bfloat16), EXPERTS, E)
+    spare = tokens * micro_count
+    copies = jnp.broadcast_to(jnp.swapaxes(inputs, 0, 1)[None], (E, tokens, micro_count, width))
+    entering = lax.all_to_all(
+        copies, "expert", split_axis=0, concat_axis=0, axis_index_groups=EXPERTS, tiled=True
+    ).reshape(E * spare, width)
     spot = jnp.arange(held, dtype=jnp.int32)
     spot_micro, spot_block, spot_token = (
         spot // (E * tokens),
@@ -125,6 +123,26 @@
 
     dues = [jnp.int32(tick) - section_pos for tick in range(ticks)]
     starts = [(jnp.clip(due, 0, pairs - 1) * held).astype(jnp.uint32) for due in dues]
+    few = 2 * PAIR * MOST
+    lane = jnp.arange(few, dtype=jnp.int32)
+    lane_row = jnp.where(lane < PAIR * MOST, lane // MOST * (E * MOST) + lane % MOST, -E * MOST)
+    experts = jnp.arange(E, dtype=jnp.int32)[:, None]
+    few_rows = (lane_row[None, :] + experts * MOST).reshape(E * few)
+    few_total = few_rows[:, None] == jnp.arange(SHARERS * sent_rows, dtype=jnp.int32)[None, :] % sent_rows
+    few_total = few_total.astype(jnp.bfloat16)
+    few_at = jnp.where(lane_row >= 0, lane_row + expert * MOST, -E * sent_rows)
+    few_at = (few_at[None, :] + experts * sent_rows).reshape(E * few)
+    few_columns = jnp.arange(E * sent_rows, dtype=jnp.int32)[:, None] == few_at[None, :]
+    seat = jnp.arange(4 * PAIR, dtype=jnp.int32)
+    seat_spot = jnp.where(seat % 4 < tokens, (seat // 4 * E + expert) * tokens + seat % 4, -1)
+    own_seats = (seat_spot[:, None] == spot[None, :]).astype(jnp.bfloat16)
+
+    def few_place(table):
+        part = lax.dynamic_slice_in_dim(table, starts[-1], held, 0)
+        part = choose(own_seats, part).astype(jnp.bfloat16)
+        return choose(part, few_columns.astype(jnp.bfloat16)).astype(jnp.bfloat16)
+
+    last = (few_total, own_seats, few_place(first_all), few_place(second_all))
     entries = [entry_picks(pair) for pair in range(pairs)]
     entry = choose(entries[0], entering).astype(jnp.bfloat16)
     arriving = jnp.zeros((held, width), jnp.bfloat16)
@@ -144,10 +162,12 @@
             pick, normed, (((0,), (0,)), ((), ())), preferred_element_type=jnp.float32
         ).astype(jnp.bfloat16)
         if tick == 0:
-            sent, first_all, second_all, sign_all, total, dues, starts, entries = barrier(
-                (sent, first_all, second_all, sign_all, total, dues, starts, entries)
+            sent, first_all, second_all, sign_all, total, dues, starts, entries, last = barrier(
+                (sent, first_all, second_all, sign_all, total, dues, starts, entries, last)
             )
         own = exchange(sent, SLICES, SHARERS)
+        if tick + 1 == ticks:
+            own, normed, hidden, share_seats = barrier((own, normed, hidden, last[1]))
         other = lax.ppermute(own, "expert", CORES)
         own_units = hidden_units(own)
         other_out = lax.ppermute(project(hidden_units(other)), "expert", CORES)
@@ -155,16 +175,23 @@
         both = (own_out.astype(jnp.float32) + other_out.astype(jnp.float32)).astype(jnp.bfloat16)
         logits = jnp.dot(normed, router_mat, preferred_element_type=jnp.float32)
         share = jax.nn.sigmoid(jnp.sum(logits * sign, axis=-1, keepdims=True))
-        both, share, rest_share = barrier((both, share, 1.0 - share))
+        if tick + 1 == ticks:
+            total, own_seats, first_place, second_place = last
+            wide = choose(share_seats, hidden)
+            share = jnp.dot(share_seats.astype(jnp.float32), share, precision=lax.Precision.HIGHEST)
+        both, share, rest_share, wide = barrier((both, share, 1.0 - share, wide))
         parts = exchange(both, SLICES, SHARERS)
         outs = exchange(choose(total, parts).astype(jnp.bfloat16), EXPERTS, E)
         first_out, second_out = choose(first_place, outs), choose(second_place, outs)
         result = (wide + share * first_out + rest_share * second_out).astype(jnp.bfloat16)
+        if tick + 1 == ticks:
+            result, due = barrier((result, due))
+            here = jnp.arange(pairs, dtype=jnp.int32)[:, None, None] == due
+            placed = jnp.where(here, result.astype(jnp.float32)[None], 0.0)
+            stored = stored + placed.reshape(stored.shape)
+            break
         result, entering, due = barrier((result, entering, due))
-        if tick + 1 < ticks:
-            arriving = lax.ppermute(
-                result, "section", [(i, i + 1) for i in range(sections - 1)]
-            )
+        arriving = lax.ppermute(result, "section", [(i, i + 1) for i in range(sections - 1)])
         if tick + 1 < pairs:
             entry = choose(entries[tick + 1], entering).astype(jnp.bfloat16)
         target = (due * PAIR + spot_micro) * 4 + spot_token
@@ -172,8 +199,7 @@
         target = jnp.where(held_now, target, -1)
         keep = target[None, :] == jnp.arange(16, dtype=jnp.int32)[:, None]
         stored = stored + choose(keep.astype(jnp.bfloat16), result)
-        if tick + 1 < ticks:
-            arriving, stored, entry = barrier((arriving, stored, entry))
+        arriving, stored, entry = barrier((arriving, stored, entry))
     stored = stored.astype(jnp.bfloat16).reshape(1, micro_count, 4, width)
     return stored[:, :, :tokens]
 

time: 340 us -> 332 us (0.976)
  blocking collectives: 235 us -> 229 us
  matrix products: 39.6 us -> 34.8 us
  waiting for transfers between devices: 20.1 us -> 24.6 us
    all_to_all x15, blocking collectives: 235 us -> 229 us  [exchange(): lax.all_to_all(chunks, 'expert', split_axis=0, concat_axis=0, axis_index_...]
    dot_general x23 -> x24, matrix products: 12.6 us -> 12.4 us  [choose(): return jnp.dot(picks, rows, preferred_element_type=jnp.float32)]
  transfers between devices with their start and end apart: 15 -> 15, of which waited for: 15 -> 15; matrix products, arithmetic and copies ran while one was open for 9% -> 7% of each run, Pallas kernels for 0% -> 0%
where the time goes in v6:
time: 332 us; the launch traced here: 330 us
  blocking collectives  229 us (69%)
  matrix products  34.8 us (10%)
  starting transfers between devices  24.6 us (7%)
  waiting for transfers between devices  24.6 us (7%)
  other arithmetic  10.5 us (3%)
  local copies, waits for them, and re-layouts  5.53 us (2%)
    all_to_all x15, blocking collectives, exchange(): lax.all_to_all(chunks, 'expert', split_axis=0, concat_axis=0, axis_index_...  229 us
    ppermute x4, starting transfers between devices, on_device(): lax.ppermute(result, 'section', [(i, i + 1) for i in range(sections - 1)])  13.8 us
    dot_general x24, matrix products, choose(): return jnp.dot(picks, rows, preferred_element_type=jnp.float32)  12.4 us
    all_to_all x1, starting transfers between devices, on_device(): lax.all_to_all(copies, 'expert', split_axis=0, concat_axis=0, axis_index_...  8.46 us
    ppermute x4, waiting for transfers between devices, on_device(): lax.ppermute(result, 'section', [(i, i + 1) for i in range(sections - 1)])  8 us
  transfers between devices with their start and end apart: 15, of which 15 were waited for; matrix products, arithmetic and copies ran while one was open for 7% of the time, Pallas kernels for 0%

profile of v6, /device:TPU:16, one launch (start us, length us, event | category | flops | bytes accessed | tf_op | source)
XLA Modules:
  0.0 330.5 jit_solution(12185466799005350638)
XLA Ops:
  0.0 1.8 broadcast_in_dim.54
  1.8 8.5 %all-to-all-start = ((bf16[4,3,4,3072]{3,2,1,0:T(4,128)(2,1)}), bf16[4,3,4,3072]{3,2,1,0:T(4,128)(2,1)}, u32[]{:S(2)}, u32[]{:S(2)}) async-start(bf16[4,3,4,3072]{3,2,1,0:T(4,128)(2,1)} %broadcast_in_dim.54), calls=%async_computation | async-start | bytes 589824 | tf_op jit(solution)/shard_map/all_to_all | solution.py:105
  15.5 6.2 %all-to-all-done = bf16[4,3,4,3072]{3,2,1,0:T(4,128)(2,1)} async-done(((bf16[4,3,4,3072]{3,2,1,0:T(4,128)(2,1)}), bf16[4,3,4,3072]{3,2,1,0:T(4,128)(2,1)}, u32[]{:S(2)}, u32[]{:S(2)}) %all-to-all-start) | async-done | bytes 294944 | tf_op jit(solution)/shard_map/all_to_all | solution.py:105
  23.1 1.1 multiply_convert_fusion.3
  24.7 15.8 %all_to_all.80 = bf16[8,16,3072]{2,1,0:T(8,128)(2,1)S(1)} all-to-all(bf16[8,16,3072]{2,1,0:T(8,128)(2,1)S(1)} %bitcast.265), channel_id=1, replica_groups={{0,2,4,6,8,10,12,14},{1,3,5,7,9,11,13,15},{16,18,20,22,24,26,28,30},{17..., dimensions={0} | all-to-all | bytes 1572864 | tf_op jit(solution)/shard_map/all_to_all | solution.py:20
  41.4 1.4 collective-permute-done
  47.4 15.8 %all_to_all.81 = bf16[8,16,3072]{2,1,0:T(8,128)(2,1)S(1)} all-to-all(bf16[8,16,3072]{2,1,0:T(8,128)(2,1)S(1)} %bitcast.269), channel_id=1, replica_groups={{0,2,4,6,8,10,12,14},{1,3,5,7,9,11,13,15},{16,18,20,22,24,26,28,30},{17..., dimensions={0} | all-to-all | bytes 1572864 | tf_op jit(solution)/shard_map/all_to_all | solution.py:20
  63.5 15.3 %all_to_all.82 = bf16[4,16,3072]{2,1,0:T(8,128)(2,1)S(1)} all-to-all(bf16[4,16,3072]{2,1,0:T(8,128)(2,1)S(1)} %bitcast.276), channel_id=1, replica_groups={{0,16,32,48},{1,17,33,49},{2,18,34,50},{3,19,35,51},{4,20,36,52},{5,21,..., dimensions={0} | all-to-all | bytes 786432 | tf_op jit(solution)/shard_map/all_to_all | solution.py:20
  79.2 3.5 %collective-permute-start.2 = (bf16[24,3072]{1,0:T(8,128)(2,1)S(1)}, bf16[24,3072]{1,0:T(8,128)(2,1)S(1)}, u32[]{:S(2)}, u32[]{:S(2)}) collective-permute-start(bf16[24,3072]{1,0:T(8,128)(2,1)S(1)} %fusion.8), channel_id=1, source_target_pairs={{0,64},{64,128},{128,192},{1,65},{65,129},{129,193},{2,66},{66,130... | collective-permute-start | bytes 442376 | tf_op jit(solution)/shard_map/ppermute | solution.py:194
  82.7 1.1 convolution_convert_fusion.20
  84.7 1.8 collective-permute-done.2
  87.2 14.5 %all_to_all.83 = bf16[8,16,3072]{2,1,0:T(8,128)(2,1)S(1)} all-to-all(bf16[8,16,3072]{2,1,0:T(8,128)(2,1)S(1)} %bitcast.266), channel_id=1, replica_groups={{0,2,4,6,8,10,12,14},{1,3,5,7,9,11,13,15},{16,18,20,22,24,26,28,30},{17..., dimensions={0} | all-to-all | bytes 1572864 | tf_op jit(solution)/shard_map/all_to_all | solution.py:20
  102.6 1.4 collective-permute-done.3
  108.8 15.9 %all_to_all.84 = bf16[8,16,3072]{2,1,0:T(8,128)(2,1)S(1)} all-to-all(bf16[8,16,3072]{2,1,0:T(8,128)(2,1)S(1)} %bitcast.270), channel_id=1, replica_groups={{0,2,4,6,8,10,12,14},{1,3,5,7,9,11,13,15},{16,18,20,22,24,26,28,30},{17..., dimensions={0} | all-to-all | bytes 1572864 | tf_op jit(solution)/shard_map/all_to_all | solution.py:20
  125.0 15.8 %all_to_all.85 = bf16[4,16,3072]{2,1,0:T(8,128)(2,1)S(1)} all-to-all(bf16[4,16,3072]{2,1,0:T(8,128)(2,1)S(1)} %bitcast.277), channel_id=1, replica_groups={{0,16,32,48},{1,17,33,49},{2,18,34,50},{3,19,35,51},{4,20,36,52},{5,21,..., dimensions={0} | all-to-all | bytes 786432 | tf_op jit(solution)/shard_map/all_to_all | solution.py:20
  141.8 3.4 %collective-permute-start.5 = (bf16[24,3072]{1,0:T(8,128)(2,1)}, bf16[24,3072]{1,0:T(8,128)(2,1)S(1)}, u32[]{:S(2)}, u32[]{:S(2)}) collective-permute-start(bf16[24,3072]{1,0:T(8,128)(2,1)} %fusion.9), channel_id=1, source_target_pairs={{0,64},{64,128},{128,192},{1,65},{65,129},{129,193},{2,66},{66,130... | collective-permute-start | bytes 442376 | tf_op jit(solution)/shard_map/ppermute | solution.py:194
  147.3 2.0 collective-permute-done.5
  150.0 14.7 %all_to_all.86 = bf16[8,16,3072]{2,1,0:T(8,128)(2,1)S(1)} all-to-all(bf16[8,16,3072]{2,1,0:T(8,128)(2,1)S(1)} %bitcast.267), channel_id=1, replica_groups={{0,2,4,6,8,10,12,14},{1,3,5,7,9,11,13,15},{16,18,20,22,24,26,28,30},{17..., dimensions={0} | all-to-all | bytes 1572864 | tf_op jit(solution)/shard_map/all_to_all | solution.py:20
  172.2 16.0 %all_to_all.87 = bf16[8,16,3072]{2,1,0:T(8,128)(2,1)S(1)} all-to-all(bf16[8,16,3072]{2,1,0:T(8,128)(2,1)S(1)} %bitcast.271), channel_id=1, replica_groups={{0,2,4,6,8,10,12,14},{1,3,5,7,9,11,13,15},{16,18,20,22,24,26,28,30},{17..., dimensions={0} | all-to-all | bytes 1572864 | tf_op jit(solution)/shard_map/all_to_all | solution.py:20
  188.4 15.9 %all_to_all.88 = bf16[4,16,3072]{2,1,0:T(8,128)(2,1)S(1)} all-to-all(bf16[4,16,3072]{2,1,0:T(8,128)(2,1)S(1)} %bitcast.278), channel_id=1, replica_groups={{0,16,32,48},{1,17,33,49},{2,18,34,50},{3,19,35,51},{4,20,36,52},{5,21,..., dimensions={0} | all-to-all | bytes 786432 | tf_op jit(solution)/shard_map/all_to_all | solution.py:20
  205.3 3.4 %collective-permute-start.8 = (bf16[24,3072]{1,0:T(8,128)(2,1)}, bf16[24,3072]{1,0:T(8,128)(2,1)S(1)}, u32[]{:S(2)}, u32[]{:S(2)}) collective-permute-start(bf16[24,3072]{1,0:T(8,128)(2,1)} %fusion.10), channel_id=1, source_target_pairs={{0,64},{64,128},{128,192},{1,65},{65,129},{129,193},{2,66},{66,130... | collective-permute-start | bytes 442376 | tf_op jit(solution)/shard_map/ppermute | solution.py:194
  210.6 2.2 collective-permute-done.8
  213.6 14.7 %all_to_all.89 = bf16[8,16,3072]{2,1,0:T(8,128)(2,1)S(1)} all-to-all(bf16[8,16,3072]{2,1,0:T(8,128)(2,1)S(1)} %bitcast.268), channel_id=1, replica_groups={{0,2,4,6,8,10,12,14},{1,3,5,7,9,11,13,15},{16,18,20,22,24,26,28,30},{17..., dimensions={0} | all-to-all | bytes 1572864 | tf_op jit(solution)/shard_map/all_to_all | solution.py:20
  229.1 1.4 collective-permute-done.9
  235.3 15.9 %all_to_all.90 = bf16[8,16,3072]{2,1,0:T(8,128)(2,1)S(1)} all-to-all(bf16[8,16,3072]{2,1,0:T(8,128)(2,1)S(1)} %bitcast.272), channel_id=1, replica_groups={{0,2,4,6,8,10,12,14},{1,3,5,7,9,11,13,15},{16,18,20,22,24,26,28,30},{17..., dimensions={0} | all-to-all | bytes 1572864 | tf_op jit(solution)/shard_map/all_to_all | solution.py:20
  251.5 15.8 %all_to_all.91 = bf16[4,16,3072]{2,1,0:T(8,128)(2,1)S(1)} all-to-all(bf16[4,16,3072]{2,1,0:T(8,128)(2,1)S(1)} %bitcast.275), channel_id=1, replica_groups={{0,16,32,48},{1,17,33,49},{2,18,34,50},{3,19,35,51},{4,20,36,52},{5,21,..., dimensions={0} | all-to-all | bytes 786432 | tf_op jit(solution)/shard_map/all_to_all | solution.py:20
  268.3 3.4 %collective-permute-start.11 = (bf16[24,3072]{1,0:T(8,128)(2,1)}, bf16[24,3072]{1,0:T(8,128)(2,1)S(1)}, u32[]{:S(2)}, u32[]{:S(2)}) collective-permute-start(bf16[24,3072]{1,0:T(8,128)(2,1)} %fusion.11), channel_id=1, source_target_pairs={{0,64},{64,128},{128,192},{1,65},{65,129},{129,193},{2,66},{66,130... | collective-permute-start | bytes 442376 | tf_op jit(solution)/shard_map/ppermute | solution.py:194
  273.9 2.0 collective-permute-done.11
  276.6 14.8 %all_to_all.92 = bf16[8,16,3072]{2,1,0:T(8,128)(2,1)S(1)} all-to-all(bf16[8,16,3072]{2,1,0:T(8,128)(2,1)S(1)} %bitcast.264), channel_id=1, replica_groups={{0,2,4,6,8,10,12,14},{1,3,5,7,9,11,13,15},{16,18,20,22,24,26,28,30},{17..., dimensions={0} | all-to-all | bytes 1572864 | tf_op jit(solution)/shard_map/all_to_all | solution.py:20
  297.0 1.7 collective-permute-done.13
  298.9 15.8 %all_to_all.93 = bf16[8,16,3072]{2,1,0:T(8,128)(2,1)S(1)} all-to-all(bf16[8,16,3072]{2,1,0:T(8,128)(2,1)S(1)} %bitcast.273), channel_id=1, replica_groups={{0,2,4,6,8,10,12,14},{1,3,5,7,9,11,13,15},{16,18,20,22,24,26,28,30},{17..., dimensions={0} | all-to-all | bytes 1572864 | tf_op jit(solution)/shard_map/all_to_all | solution.py:20
  314.9 12.7 %all_to_all.94 = bf16[4,8,3072]{2,1,0:T(8,128)(2,1)S(1)} all-to-all(bf16[4,8,3072]{2,1,0:T(8,128)(2,1)S(1)} %fusion.12), channel_id=1, replica_groups={{0,16,32,48},{1,17,33,49},{2,18,34,50},{3,19,35,51},{4,20,36,52},{5,21,..., dimensions={0} | all-to-all | bytes 393216 | tf_op jit(solution)/shard_map/all_to_all | solution.py:20
  (216 shorter events, 53.5 us)
Async XLA Ops:
  0.0 44.2 %copy-start = (bf16[1,512,3072]{2,1,0:T(8,128)(2,1)S(1)}, bf16[1,512,3072]{2,1,0:T(8,128)(2,1)}, u32[]{:S(2)}) copy-start(bf16[1,512,3072]{2,1,0:T(8,128)(2,1)} %param.13) | copy-start | bytes 9437188
  1.8 19.9 %all-to-all-start = ((bf16[4,3,4,3072]{3,2,1,0:T(4,128)(2,1)}), bf16[4,3,4,3072]{3,2,1,0:T(4,128)(2,1)}, u32[]{:S(2)}, u32[]{:S(2)}) async-start(bf16[4,3,4,3072]{3,2,1,0:T(4,128)(2,1)} %broadcast_in_dim.54), calls=%async_computation | async-start | bytes 589824 | tf_op jit(solution)/shard_map/all_to_all | solution.py:105
  11.5 90.3 %copy-start.17 = (f32[48,4]{0,1:T(4,128)}, f32[48,4]{0,1:T(4,128)S(1)}, u32[]{:S(2)}) copy-start(f32[48,4]{0,1:T(4,128)S(1)} %convert_subtract_fusion) | copy-start | bytes 2308
  14.7 25.8 %copy-start.20 = (bf16[1,3072,4]{1,2,0:T(4,128)(2,1)S(1)}, bf16[1,3072,4]{1,2,0:T(4,128)(2,1)}, u32[]{:S(2)}) copy-start(bf16[1,3072,4]{1,2,0:T(4,128)(2,1)} %param.10) | copy-start | bytes 73732
  22.7 18.6 %copy-start.11 = (bf16[48,3072]{1,0:T(8,128)(2,1)}, bf16[48,3072]{1,0:T(8,128)(2,1)S(1)}, u32[]{:S(2)}) copy-start(bf16[48,3072]{1,0:T(8,128)(2,1)S(1)} %reshape.663) | copy-start | bytes 884740
  22.7 18.0 %copy-start.1 = (bf16[1,3072,512]{2,1,0:T(8,128)(2,1)S(1)}, bf16[1,3072,512]{2,1,0:T(8,128)(2,1)}, u32[]{:S(2)}) copy-start(bf16[1,3072,512]{2,1,0:T(8,128)(2,1)} %param.12) | copy-start | bytes 9437188
  40.5 2.3 collective-permute-start
  40.8 2.7 copy-start.6
  44.8 2.4 collective-permute-start.1
  47.4 39.3 %copy-start.12 = (f32[1,3072]{1,0:T(1,128)S(1)}, f32[1,3072]{1,0:T(1,128)}, u32[]{:S(2)}) copy-start(f32[1,3072]{1,0:T(1,128)} %param.9) | copy-start | bytes 36868
  79.2 22.8 %copy-start.2 = (bf16[1,3072,512]{2,1,0:T(8,128)(2,1)S(1)}, bf16[1,3072,512]{2,1,0:T(8,128)(2,1)}, u32[]{:S(2)}) copy-start(bf16[1,3072,512]{2,1,0:T(8,128)(2,1)} %param.12) | copy-start | bytes 9437188
  79.2 7.3 %collective-permute-start.2 = (bf16[24,3072]{1,0:T(8,128)(2,1)S(1)}, bf16[24,3072]{1,0:T(8,128)(2,1)S(1)}, u32[]{:S(2)}, u32[]{:S(2)}) collective-permute-start(bf16[24,3072]{1,0:T(8,128)(2,1)S(1)} %fusion.8), channel_id=1, source_target_pairs={{0,64},{64,128},{128,192},{1,65},{65,129},{129,193},{2,66},{66,130... | collective-permute-start | bytes 442376 | tf_op jit(solution)/shard_map/ppermute | solution.py:194
  101.7 2.3 collective-permute-start.3
  106.0 2.6 collective-permute-start.4
  141.8 23.9 %copy-start.3 = (bf16[1,3072,512]{2,1,0:T(8,128)(2,1)S(1)}, bf16[1,3072,512]{2,1,0:T(8,128)(2,1)}, u32[]{:S(2)}) copy-start(bf16[1,3072,512]{2,1,0:T(8,128)(2,1)} %param.12) | copy-start | bytes 9437188
  141.8 7.5 %collective-permute-start.5 = (bf16[24,3072]{1,0:T(8,128)(2,1)}, bf16[24,3072]{1,0:T(8,128)(2,1)S(1)}, u32[]{:S(2)}, u32[]{:S(2)}) collective-permute-start(bf16[24,3072]{1,0:T(8,128)(2,1)} %fusion.9), channel_id=1, source_target_pairs={{0,64},{64,128},{128,192},{1,65},{65,129},{129,193},{2,66},{66,130... | collective-permute-start | bytes 442376 | tf_op jit(solution)/shard_map/ppermute | solution.py:194
  164.7 2.3 collective-permute-start.6
  169.5 2.5 collective-permute-start.7
  205.3 22.9 %copy-start.18 = (f32[48,4]{0,1:T(4,128)S(1)}, f32[48,4]{0,1:T(4,128)}, u32[]{:S(2)}) copy-start(f32[48,4]{0,1:T(4,128)} %copy-done.17) | copy-start | bytes 2308
  205.3 22.9 %copy-start.21 = (bf16[1,3072,4]{1,2,0:T(4,128)(2,1)S(1)}, bf16[1,3072,4]{1,2,0:T(4,128)(2,1)}, u32[]{:S(2)}) copy-start(bf16[1,3072,4]{1,2,0:T(4,128)(2,1)} %param.10) | copy-start | bytes 73732
  205.3 23.2 %copy-start.4 = (bf16[1,3072,512]{2,1,0:T(8,128)(2,1)S(1)}, bf16[1,3072,512]{2,1,0:T(8,128)(2,1)}, u32[]{:S(2)}) copy-start(bf16[1,3072,512]{2,1,0:T(8,128)(2,1)} %param.12) | copy-start | bytes 9437188
  205.3 7.5 %collective-permute-start.8 = (bf16[24,3072]{1,0:T(8,128)(2,1)}, bf16[24,3072]{1,0:T(8,128)(2,1)S(1)}, u32[]{:S(2)}, u32[]{:S(2)}) collective-permute-start(bf16[24,3072]{1,0:T(8,128)(2,1)} %fusion.10), channel_id=1, source_target_pairs={{0,64},{64,128},{128,192},{1,65},{65,129},{129,193},{2,66},{66,130... | collective-permute-start | bytes 442376 | tf_op jit(solution)/shard_map/ppermute | solution.py:194
  228.3 2.3 collective-permute-start.9
  232.5 2.6 collective-permute-start.10
  268.3 23.0 %copy-start.5 = (bf16[1,3072,512]{2,1,0:T(8,128)(2,1)S(1)}, bf16[1,3072,512]{2,1,0:T(8,128)(2,1)}, u32[]{:S(2)}) copy-start(bf16[1,3072,512]{2,1,0:T(8,128)(2,1)} %param.12) | copy-start | bytes 9437188
  268.3 7.5 %collective-permute-start.11 = (bf16[24,3072]{1,0:T(8,128)(2,1)}, bf16[24,3072]{1,0:T(8,128)(2,1)S(1)}, u32[]{:S(2)}, u32[]{:S(2)}) collective-permute-start(bf16[24,3072]{1,0:T(8,128)(2,1)} %fusion.11), channel_id=1, source_target_pairs={{0,64},{64,128},{128,192},{1,65},{65,129},{129,193},{2,66},{66,130... | collective-permute-start | bytes 442376 | tf_op jit(solution)/shard_map/ppermute | solution.py:194
  276.1 15.9 %copy-start.10 = (bf16[1,3072,512]{2,1,0:T(8,128)(2,1)S(1)}, bf16[1,3072,512]{2,1,0:T(8,128)(2,1)}, u32[]{:S(2)}) copy-start(bf16[1,3072,512]{2,1,0:T(8,128)(2,1)} %param.11) | copy-start | bytes 9437188
  291.9 2.4 collective-permute-start.12
  296.2 18.4 %copy-start.13 = (bf16[32,128]{1,0:T(8,128)(2,1)S(1)}, bf16[32,128]{1,0:T(8,128)(2,1)}, u32[]{:S(2)}) copy-start(bf16[32,128]{1,0:T(8,128)(2,1)} %compare_convert_fusion.1) | copy-start | bytes 24580
  296.3 31.4 %copy-start.16 = (bf16[8,32]{1,0:T(8,128)(2,1)S(1)}, bf16[8,32]{1,0:T(8,128)(2,1)}, u32[]{:S(2)}) copy-start(bf16[8,32]{1,0:T(8,128)(2,1)} %convolution_convert_fusion.26) | copy-start | bytes 1540
  296.3 31.5 %copy-start.15 = (bf16[8,32]{1,0:T(8,128)(2,1)S(1)}, bf16[8,32]{1,0:T(8,128)(2,1)}, u32[]{:S(2)}) copy-start(bf16[8,32]{1,0:T(8,128)(2,1)} %convolution_convert_fusion.27) | copy-start | bytes 1540
  296.3 2.4 collective-permute-start.13
  (6 other events, 9.2 us)

commit v7 on v6

--- a/solution.py
+++ b/solution.py
@@ -121,8 +121,10 @@
     total = total == jnp.arange(SHARERS * sent_rows, dtype=jnp.int32)[None, :] % sent_rows
     total = total.astype(jnp.bfloat16)
 
-    dues = [jnp.int32(tick) - section_pos for tick in range(ticks)]
-    starts = [(jnp.clip(due, 0, pairs - 1) * held).astype(jnp.uint32) for due in dues]
+    starts = [
+        (jnp.clip(tick - section_pos, 0, pairs - 1) * held).astype(jnp.uint32)
+        for tick in range(ticks)
+    ]
     few = 2 * PAIR * MOST
     lane = jnp.arange(few, dtype=jnp.int32)
     lane_row = jnp.where(lane < PAIR * MOST, lane // MOST * (E * MOST) + lane % MOST, -E * MOST)
@@ -134,7 +136,8 @@
     few_at = (few_at[None, :] + experts * sent_rows).reshape(E * few)
     few_columns = jnp.arange(E * sent_rows, dtype=jnp.int32)[:, None] == few_at[None, :]
     seat = jnp.arange(4 * PAIR, dtype=jnp.int32)
-    seat_spot = jnp.where(seat % 4 < tokens, (seat // 4 * E + expert) * tokens + seat % 4, -1)
+    seat_spot = (seat % PAIR * E + expert) * tokens + seat // PAIR
+    seat_spot = jnp.where(seat // PAIR < tokens, seat_spot, -1)
     own_seats = (seat_spot[:, None] == spot[None, :]).astype(jnp.bfloat16)
 
     def few_place(table):
@@ -142,13 +145,23 @@
         part = choose(own_seats, part).astype(jnp.bfloat16)
         return choose(part, few_columns.astype(jnp.bfloat16)).astype(jnp.bfloat16)
 
-    last = (few_total, own_seats, few_place(first_all), few_place(second_all))
+    line = jnp.arange(16, dtype=jnp.int32)[:, None]
+    seen = jnp.arange((ticks - 1) * held, dtype=jnp.int32)
+    due, spot_of = seen // held - section_pos, seen % held
+    target = spot_of % tokens * micro_count + due * PAIR + spot_of // (E * tokens)
+    mine = (spot_of // tokens % E == expert) & (due >= 0) & (due < pairs)
+    keep_all = (jnp.where(mine, target, -1)[None, :] == line).astype(jnp.bfloat16)
+    due = jnp.full((4 * PAIR,), ticks - 1, jnp.int32) - section_pos
+    target = seat // PAIR * micro_count + due * PAIR + seat % PAIR
+    keep_last = jnp.where((due >= 0) & (due < pairs), target, -1)
+    keep_last = (keep_last[None, :] == line).astype(jnp.bfloat16)
+    last = (few_total, own_seats, few_place(first_all), few_place(second_all), keep_all, keep_last)
     entries = [entry_picks(pair) for pair in range(pairs)]
     entry = choose(entries[0], entering).astype(jnp.bfloat16)
     arriving = jnp.zeros((held, width), jnp.bfloat16)
-    stored = jnp.zeros((16, width), jnp.float32)
+    stored, results = jnp.zeros((), jnp.float32), []
     for tick in range(ticks):
-        due, start = dues[tick], starts[tick]
+        start = starts[tick]
         pick, first_place, second_place, sign = (
             lax.dynamic_slice_in_dim(table, start, held, 0)
             for table in (pick_all, first_all, second_all, sign_all)
@@ -162,12 +175,14 @@
             pick, normed, (((0,), (0,)), ((), ())), preferred_element_type=jnp.float32
         ).astype(jnp.bfloat16)
         if tick == 0:
-            sent, first_all, second_all, sign_all, total, dues, starts, entries, last = barrier(
-                (sent, first_all, second_all, sign_all, total, dues, starts, entries, last)
+            sent, first_all, second_all, sign_all, total, starts, entries, last = barrier(
+                (sent, first_all, second_all, sign_all, total, starts, entries, last)
             )
         own = exchange(sent, SLICES, SHARERS)
         if tick + 1 == ticks:
-            own, normed, hidden, share_seats = barrier((own, normed, hidden, last[1]))
+            own, normed, hidden, share_seats, results = barrier(
+                (own, normed, hidden, last[1], results)
+            )
         other = lax.ppermute(own, "expert", CORES)
         own_units = hidden_units(own)
         other_out = lax.ppermute(project(hidden_units(other)), "expert", CORES)
@@ -176,32 +191,26 @@
         logits = jnp.dot(normed, router_mat, preferred_element_type=jnp.float32)
         share = jax.nn.sigmoid(jnp.sum(logits * sign, axis=-1, keepdims=True))
         if tick + 1 == ticks:
-            total, own_seats, first_place, second_place = last
+            total, own_seats, first_place, second_place, keep_all, keep_last = last
+            stored = choose(keep_all, jnp.concatenate(results, axis=0))
             wide = choose(share_seats, hidden)
             share = jnp.dot(share_seats.astype(jnp.float32), share, precision=lax.Precision.HIGHEST)
-        both, share, rest_share, wide = barrier((both, share, 1.0 - share, wide))
+        both, share, rest_share, wide, stored = barrier((both, share, 1.0 - share, wide, stored))
         parts = exchange(both, SLICES, SHARERS)
         outs = exchange(choose(total, parts).astype(jnp.bfloat16), EXPERTS, E)
         first_out, second_out = choose(first_place, outs), choose(second_place, outs)
         result = (wide + share * first_out + rest_share * second_out).astype(jnp.bfloat16)
         if tick + 1 == ticks:
-            result, due = barrier((result, due))
-            here = jnp.arange(pairs, dtype=jnp.int32)[:, None, None] == due
-            placed = jnp.where(here, result.astype(jnp.float32)[None], 0.0)
-            stored = stored + placed.reshape(stored.shape)
+            stored = stored + choose(keep_last, result)
             break
-        result, entering, due = barrier((result, entering, due))
+        result, entering = barrier((result, entering))
+        results.append(result)
         arriving = lax.ppermute(result, "section", [(i, i + 1) for i in range(sections - 1)])
         if tick + 1 < pairs:
             entry = choose(entries[tick + 1], entering).astype(jnp.bfloat16)
-        target = (due * PAIR + spot_micro) * 4 + spot_token
-        held_now = (spot_block == expert) & (due >= 0) & (due < pairs)
-        target = jnp.where(held_now, target, -1)
-        keep = target[None, :] == jnp.arange(16, dtype=jnp.int32)[:, None]
-        stored = stored + choose(keep.astype(jnp.bfloat16), result)
-        arriving, stored, entry = barrier((arriving, stored, entry))
-    stored = stored.astype(jnp.bfloat16).reshape(1, micro_count, 4, width)
-    return stored[:, :, :tokens]
+        arriving, entry = barrier((arriving, entry))
+    stored = stored.astype(jnp.bfloat16)[: tokens * micro_count]
+    return jnp.swapaxes(stored.reshape(1, tokens, micro_count, width), 1, 2)
 
 
 def solution(mesh):

time: 332 us -> 327 us (0.985)
  waiting for transfers between devices: 24.6 us -> 33.6 us
  matrix products: 34.8 us -> 29.2 us
  other arithmetic: 10.5 us -> 6.7 us
    ppermute x4, waiting for transfers between devices: 8 us -> 15.2 us  [on_device(): lax.ppermute(result, 'section', [(i, i + 1) for i in range(sections - 1)])]
    dot_general x24 -> x21, matrix products: 12.4 us -> 7.45 us  [choose(): return jnp.dot(picks, rows, preferred_element_type=jnp.float32)]
  transfers between devices with their start and end apart: 15 -> 15, of which waited for: 15 -> 15; matrix products, arithmetic and copies ran while one was open for 7% -> 5% of each run, Pallas kernels for 0% -> 0%
where the time goes in v7:
time: 327 us; the launch traced here: 326 us
  blocking collectives  229 us (70%)
  waiting for transfers between devices  33.6 us (10%)
  matrix products  29.2 us (9%)
  starting transfers between devices  22.6 us (7%)
  other arithmetic  6.7 us (2%)
  local copies, waits for them, and re-layouts  3.74 us (1%)
    all_to_all x15, blocking collectives, exchange(): lax.all_to_all(chunks, 'expert', split_axis=0, concat_axis=0, axis_index_...  229 us
    ppermute x4, waiting for transfers between devices, on_device(): lax.ppermute(result, 'section', [(i, i + 1) for i in range(sections - 1)])  15.2 us
    ppermute x4, starting transfers between devices, on_device(): lax.ppermute(result, 'section', [(i, i + 1) for i in range(sections - 1)])  12.8 us
    all_to_all x1, waiting for transfers between devices, on_device(): lax.all_to_all(copies, 'expert', split_axis=0, concat_axis=0, axis_index_...  8.47 us
    all_to_all x1, starting transfers between devices, on_device(): lax.all_to_all(copies, 'expert', split_axis=0, concat_axis=0, axis_index_...  8.46 us
    dot_general x21, matrix products, choose(): return jnp.dot(picks, rows, preferred_element_type=jnp.float32)  7.45 us
  transfers between devices with their start and end apart: 15, of which 15 were waited for; matrix products, arithmetic and copies ran while one was open for 5% of the time, Pallas kernels for 0%

profile of v7, /device:TPU:16, one launch (start us, length us, event | category | flops | bytes accessed | tf_op | source)
XLA Modules:
  0.0 325.7 jit_solution(9785585410253508684)
XLA Ops:
  0.0 1.8 broadcast_in_dim.32
  1.8 8.5 %all-to-all-start = ((bf16[4,3,4,3072]{3,2,1,0:T(4,128)(2,1)}), bf16[4,3,4,3072]{3,2,1,0:T(4,128)(2,1)}, u32[]{:S(2)}, u32[]{:S(2)}) async-start(bf16[4,3,4,3072]{3,2,1,0:T(4,128)(2,1)} %broadcast_in_dim.32), calls=%async_computation | async-start | bytes 589824 | tf_op jit(solution)/shard_map/all_to_all | solution.py:105
  13.2 8.5 %all-to-all-done = bf16[4,3,4,3072]{3,2,1,0:T(4,128)(2,1)} async-done(((bf16[4,3,4,3072]{3,2,1,0:T(4,128)(2,1)}), bf16[4,3,4,3072]{3,2,1,0:T(4,128)(2,1)}, u32[]{:S(2)}, u32[]{:S(2)}) %all-to-all-start) | async-done | bytes 294944 | tf_op jit(solution)/shard_map/all_to_all | solution.py:105
  23.1 1.0 multiply_convert_fusion.3
  24.6 15.8 %all_to_all.80 = bf16[8,16,3072]{2,1,0:T(8,128)(2,1)S(1)} all-to-all(bf16[8,16,3072]{2,1,0:T(8,128)(2,1)S(1)} %bitcast.258), channel_id=1, replica_groups={{0,2,4,6,8,10,12,14},{1,3,5,7,9,11,13,15},{16,18,20,22,24,26,28,30},{17..., dimensions={0} | all-to-all | bytes 1572864 | tf_op jit(solution)/shard_map/all_to_all | solution.py:20
  41.3 1.4 collective-permute-done
  47.2 16.0 %all_to_all.81 = bf16[8,16,3072]{2,1,0:T(8,128)(2,1)S(1)} all-to-all(bf16[8,16,3072]{2,1,0:T(8,128)(2,1)S(1)} %bitcast.262), channel_id=1, replica_groups={{0,2,4,6,8,10,12,14},{1,3,5,7,9,11,13,15},{16,18,20,22,24,26,28,30},{17..., dimensions={0} | all-to-all | bytes 1572864 | tf_op jit(solution)/shard_map/all_to_all | solution.py:20
  63.5 15.5 %all_to_all.82 = bf16[4,16,3072]{2,1,0:T(8,128)(2,1)S(1)} all-to-all(bf16[4,16,3072]{2,1,0:T(8,128)(2,1)S(1)} %bitcast.269), channel_id=1, replica_groups={{0,16,32,48},{1,17,33,49},{2,18,34,50},{3,19,35,51},{4,20,36,52},{5,21,..., dimensions={0} | all-to-all | bytes 786432 | tf_op jit(solution)/shard_map/all_to_all | solution.py:20
  79.3 3.2 collective-permute-start.2
  82.7 3.7 %collective-permute-done.2 = bf16[24,3072]{1,0:T(8,128)(2,1)S(1)} collective-permute-done((bf16[24,3072]{1,0:T(8,128)(2,1)S(1)}, bf16[24,3072]{1,0:T(8,128)(2,1)S(1)}, u32[]{:S(2)}, u32[]{:S(2)}) %collective-permute-start.2) | collective-permute-done | bytes 147488 | tf_op jit(solution)/shard_map/ppermute | solution.py:208
  87.0 14.7 %all_to_all.83 = bf16[8,16,3072]{2,1,0:T(8,128)(2,1)S(1)} all-to-all(bf16[8,16,3072]{2,1,0:T(8,128)(2,1)S(1)} %bitcast.259), channel_id=1, replica_groups={{0,2,4,6,8,10,12,14},{1,3,5,7,9,11,13,15},{16,18,20,22,24,26,28,30},{17..., dimensions={0} | all-to-all | bytes 1572864 | tf_op jit(solution)/shard_map/all_to_all | solution.py:20
  102.6 1.4 collective-permute-done.3
  108.5 15.9 %all_to_all.84 = bf16[8,16,3072]{2,1,0:T(8,128)(2,1)S(1)} all-to-all(bf16[8,16,3072]{2,1,0:T(8,128)(2,1)S(1)} %bitcast.263), channel_id=1, replica_groups={{0,2,4,6,8,10,12,14},{1,3,5,7,9,11,13,15},{16,18,20,22,24,26,28,30},{17..., dimensions={0} | all-to-all | bytes 1572864 | tf_op jit(solution)/shard_map/all_to_all | solution.py:20
  124.7 15.8 %all_to_all.85 = bf16[4,16,3072]{2,1,0:T(8,128)(2,1)S(1)} all-to-all(bf16[4,16,3072]{2,1,0:T(8,128)(2,1)S(1)} %bitcast.270), channel_id=1, replica_groups={{0,16,32,48},{1,17,33,49},{2,18,34,50},{3,19,35,51},{4,20,36,52},{5,21,..., dimensions={0} | all-to-all | bytes 786432 | tf_op jit(solution)/shard_map/all_to_all | solution.py:20
  140.9 3.2 collective-permute-start.5
  144.1 3.8 %collective-permute-done.5 = bf16[24,3072]{1,0:T(8,128)(2,1)S(1)} collective-permute-done((bf16[24,3072]{1,0:T(8,128)(2,1)S(1)}, bf16[24,3072]{1,0:T(8,128)(2,1)S(1)}, u32[]{:S(2)}, u32[]{:S(2)}) %collective-permute-start.5) | collective-permute-done | bytes 147488 | tf_op jit(solution)/shard_map/ppermute | solution.py:208
  148.6 14.7 %all_to_all.86 = bf16[8,16,3072]{2,1,0:T(8,128)(2,1)S(1)} all-to-all(bf16[8,16,3072]{2,1,0:T(8,128)(2,1)S(1)} %bitcast.260), channel_id=1, replica_groups={{0,2,4,6,8,10,12,14},{1,3,5,7,9,11,13,15},{16,18,20,22,24,26,28,30},{17..., dimensions={0} | all-to-all | bytes 1572864 | tf_op jit(solution)/shard_map/all_to_all | solution.py:20
  164.2 1.4 collective-permute-done.6
  170.1 15.8 %all_to_all.87 = bf16[8,16,3072]{2,1,0:T(8,128)(2,1)S(1)} all-to-all(bf16[8,16,3072]{2,1,0:T(8,128)(2,1)S(1)} %bitcast.264), channel_id=1, replica_groups={{0,2,4,6,8,10,12,14},{1,3,5,7,9,11,13,15},{16,18,20,22,24,26,28,30},{17..., dimensions={0} | all-to-all | bytes 1572864 | tf_op jit(solution)/shard_map/all_to_all | solution.py:20
  186.2 15.7 %all_to_all.88 = bf16[4,16,3072]{2,1,0:T(8,128)(2,1)S(1)} all-to-all(bf16[4,16,3072]{2,1,0:T(8,128)(2,1)S(1)} %bitcast.271), channel_id=1, replica_groups={{0,16,32,48},{1,17,33,49},{2,18,34,50},{3,19,35,51},{4,20,36,52},{5,21,..., dimensions={0} | all-to-all | bytes 786432 | tf_op jit(solution)/shard_map/all_to_all | solution.py:20
  202.3 3.2 collective-permute-start.8
  205.5 3.8 %collective-permute-done.8 = bf16[24,3072]{1,0:T(8,128)(2,1)S(1)} collective-permute-done((bf16[24,3072]{1,0:T(8,128)(2,1)S(1)}, bf16[24,3072]{1,0:T(8,128)(2,1)S(1)}, u32[]{:S(2)}, u32[]{:S(2)}) %collective-permute-start.8) | collective-permute-done | bytes 147488 | tf_op jit(solution)/shard_map/ppermute | solution.py:208
  210.1 14.4 %all_to_all.89 = bf16[8,16,3072]{2,1,0:T(8,128)(2,1)S(1)} all-to-all(bf16[8,16,3072]{2,1,0:T(8,128)(2,1)S(1)} %bitcast.261), channel_id=1, replica_groups={{0,2,4,6,8,10,12,14},{1,3,5,7,9,11,13,15},{16,18,20,22,24,26,28,30},{17..., dimensions={0} | all-to-all | bytes 1572864 | tf_op jit(solution)/shard_map/all_to_all | solution.py:20
  225.3 1.4 collective-permute-done.9
  231.2 15.8 %all_to_all.90 = bf16[8,16,3072]{2,1,0:T(8,128)(2,1)S(1)} all-to-all(bf16[8,16,3072]{2,1,0:T(8,128)(2,1)S(1)} %bitcast.265), channel_id=1, replica_groups={{0,2,4,6,8,10,12,14},{1,3,5,7,9,11,13,15},{16,18,20,22,24,26,28,30},{17..., dimensions={0} | all-to-all | bytes 1572864 | tf_op jit(solution)/shard_map/all_to_all | solution.py:20
  247.3 15.8 %all_to_all.91 = bf16[4,16,3072]{2,1,0:T(8,128)(2,1)S(1)} all-to-all(bf16[4,16,3072]{2,1,0:T(8,128)(2,1)S(1)} %bitcast.268), channel_id=1, replica_groups={{0,16,32,48},{1,17,33,49},{2,18,34,50},{3,19,35,51},{4,20,36,52},{5,21,..., dimensions={0} | all-to-all | bytes 786432 | tf_op jit(solution)/shard_map/all_to_all | solution.py:20
  263.5 3.2 collective-permute-start.11
  266.7 3.8 %collective-permute-done.11 = bf16[24,3072]{1,0:T(8,128)(2,1)S(1)} collective-permute-done((bf16[24,3072]{1,0:T(8,128)(2,1)S(1)}, bf16[24,3072]{1,0:T(8,128)(2,1)S(1)}, u32[]{:S(2)}, u32[]{:S(2)}) %collective-permute-start.11) | collective-permute-done | bytes 147488 | tf_op jit(solution)/shard_map/ppermute | solution.py:208
  271.3 14.5 %all_to_all.92 = bf16[8,16,3072]{2,1,0:T(8,128)(2,1)S(1)} all-to-all(bf16[8,16,3072]{2,1,0:T(8,128)(2,1)S(1)} %bitcast.257), channel_id=1, replica_groups={{0,2,4,6,8,10,12,14},{1,3,5,7,9,11,13,15},{16,18,20,22,24,26,28,30},{17..., dimensions={0} | all-to-all | bytes 1572864 | tf_op jit(solution)/shard_map/all_to_all | solution.py:20
  293.3 15.8 %all_to_all.93 = bf16[8,16,3072]{2,1,0:T(8,128)(2,1)S(1)} all-to-all(bf16[8,16,3072]{2,1,0:T(8,128)(2,1)S(1)} %bitcast.266), channel_id=1, replica_groups={{0,2,4,6,8,10,12,14},{1,3,5,7,9,11,13,15},{16,18,20,22,24,26,28,30},{17..., dimensions={0} | all-to-all | bytes 1572864 | tf_op jit(solution)/shard_map/all_to_all | solution.py:20
  309.4 12.6 %all_to_all.94 = bf16[4,8,3072]{2,1,0:T(8,128)(2,1)S(1)} all-to-all(bf16[4,8,3072]{2,1,0:T(8,128)(2,1)S(1)} %fusion.12), channel_id=1, replica_groups={{0,16,32,48},{1,17,33,49},{2,18,34,50},{3,19,35,51},{4,20,36,52},{5,21,..., dimensions={0} | all-to-all | bytes 393216 | tf_op jit(solution)/shard_map/all_to_all | solution.py:20
  322.8 1.2 fusion.67
  (169 shorter events, 41.3 us)
Async XLA Ops:
  0.0 44.1 %copy-start = (bf16[1,512,3072]{2,1,0:T(8,128)(2,1)S(1)}, bf16[1,512,3072]{2,1,0:T(8,128)(2,1)}, u32[]{:S(2)}) copy-start(bf16[1,512,3072]{2,1,0:T(8,128)(2,1)} %param.13) | copy-start | bytes 9437188
  1.8 19.9 %all-to-all-start = ((bf16[4,3,4,3072]{3,2,1,0:T(4,128)(2,1)}), bf16[4,3,4,3072]{3,2,1,0:T(4,128)(2,1)}, u32[]{:S(2)}, u32[]{:S(2)}) async-start(bf16[4,3,4,3072]{3,2,1,0:T(4,128)(2,1)} %broadcast_in_dim.32), calls=%async_computation | async-start | bytes 589824 | tf_op jit(solution)/shard_map/all_to_all | solution.py:105
  22.7 17.7 %copy-start.4 = (bf16[1,3072,4]{1,2,0:T(4,128)(2,1)S(1)}, bf16[1,3072,4]{1,2,0:T(4,128)(2,1)}, u32[]{:S(2)}) copy-start(bf16[1,3072,4]{1,2,0:T(4,128)(2,1)} %param.10) | copy-start | bytes 73732
  22.7 17.9 %copy-start.1 = (bf16[1,3072,512]{2,1,0:T(8,128)(2,1)S(1)}, bf16[1,3072,512]{2,1,0:T(8,128)(2,1)}, u32[]{:S(2)}) copy-start(bf16[1,3072,512]{2,1,0:T(8,128)(2,1)} %param.12) | copy-start | bytes 9437188
  40.4 2.3 collective-permute-start
  41.3 2.0 copy-start.2
  44.7 2.4 collective-permute-start.1
  47.2 39.3 %copy-start.3 = (f32[1,3072]{1,0:T(1,128)S(1)}, f32[1,3072]{1,0:T(1,128)}, u32[]{:S(2)}) copy-start(f32[1,3072]{1,0:T(1,128)} %param.9) | copy-start | bytes 36868
  79.3 7.0 %collective-permute-start.2 = (bf16[24,3072]{1,0:T(8,128)(2,1)S(1)}, bf16[24,3072]{1,0:T(8,128)(2,1)S(1)}, u32[]{:S(2)}, u32[]{:S(2)}) collective-permute-start(bf16[24,3072]{1,0:T(8,128)(2,1)S(1)} %fusion.8), channel_id=1, source_target_pairs={{0,64},{64,128},{128,192},{1,65},{65,129},{129,193},{2,66},{66,130... | collective-permute-start | bytes 442376 | tf_op jit(solution)/shard_map/ppermute | solution.py:208
  101.7 2.3 collective-permute-start.3
  105.9 2.4 collective-permute-start.4
  140.9 7.0 %collective-permute-start.5 = (bf16[24,3072]{1,0:T(8,128)(2,1)S(1)}, bf16[24,3072]{1,0:T(8,128)(2,1)S(1)}, u32[]{:S(2)}, u32[]{:S(2)}) collective-permute-start(bf16[24,3072]{1,0:T(8,128)(2,1)S(1)} %fusion.9), channel_id=1, source_target_pairs={{0,64},{64,128},{128,192},{1,65},{65,129},{129,193},{2,66},{66,130... | collective-permute-start | bytes 442376 | tf_op jit(solution)/shard_map/ppermute | solution.py:208
  163.3 2.3 collective-permute-start.6
  167.5 2.4 collective-permute-start.7
  202.3 7.0 %collective-permute-start.8 = (bf16[24,3072]{1,0:T(8,128)(2,1)S(1)}, bf16[24,3072]{1,0:T(8,128)(2,1)S(1)}, u32[]{:S(2)}, u32[]{:S(2)}) collective-permute-start(bf16[24,3072]{1,0:T(8,128)(2,1)S(1)} %fusion.10), channel_id=1, source_target_pairs={{0,64},{64,128},{128,192},{1,65},{65,129},{129,193},{2,66},{66,130... | collective-permute-start | bytes 442376 | tf_op jit(solution)/shard_map/ppermute | solution.py:208
  224.4 2.3 collective-permute-start.9
  228.7 2.4 collective-permute-start.10
  263.5 7.0 %collective-permute-start.11 = (bf16[24,3072]{1,0:T(8,128)(2,1)S(1)}, bf16[24,3072]{1,0:T(8,128)(2,1)S(1)}, u32[]{:S(2)}, u32[]{:S(2)}) collective-permute-start(bf16[24,3072]{1,0:T(8,128)(2,1)S(1)} %fusion.11), channel_id=1, source_target_pairs={{0,64},{64,128},{128,192},{1,65},{65,129},{129,193},{2,66},{66,130... | collective-permute-start | bytes 442376 | tf_op jit(solution)/shard_map/ppermute | solution.py:208
  286.4 2.4 collective-permute-start.12
  290.8 2.4 collective-permute-start.13

commit v8 on v7

--- a/solution.py
+++ b/solution.py
@@ -101,10 +101,6 @@
     pick_all, first_all, second_all, sign_all = tables(routes[0], expert, rest, tokens)
 
     spare = tokens * micro_count
-    copies = jnp.broadcast_to(jnp.swapaxes(inputs, 0, 1)[None], (E, tokens, micro_count, width))
-    entering = lax.all_to_all(
-        copies, "expert", split_axis=0, concat_axis=0, axis_index_groups=EXPERTS, tiled=True
-    ).reshape(E * spare, width)
     spot = jnp.arange(held, dtype=jnp.int32)
     spot_micro, spot_block, spot_token = (
         spot // (E * tokens),
@@ -157,6 +153,14 @@
     keep_last = (keep_last[None, :] == line).astype(jnp.bfloat16)
     last = (few_total, own_seats, few_place(first_all), few_place(second_all), keep_all, keep_last)
     entries = [entry_picks(pair) for pair in range(pairs)]
+    own_rows, at_entry = jnp.swapaxes(inputs, 0, 1), section_pos == 0
+    (own_rows, at_entry, pick_all, first_all, second_all, sign_all, total, starts, entries, last) = barrier(
+        (own_rows, at_entry, pick_all, first_all, second_all, sign_all, total, starts, entries, last)
+    )
+    copies = jnp.broadcast_to(own_rows[None], (E, tokens, micro_count, width))
+    entering = lax.all_to_all(
+        copies, "expert", split_axis=0, concat_axis=0, axis_index_groups=EXPERTS, tiled=True
+    ).reshape(E * spare, width)
     entry = choose(entries[0], entering).astype(jnp.bfloat16)
     arriving = jnp.zeros((held, width), jnp.bfloat16)
     stored, results = jnp.zeros((), jnp.float32), []
@@ -166,7 +170,7 @@
             lax.dynamic_slice_in_dim(table, start, held, 0)
             for table in (pick_all, first_all, second_all, sign_all)
         )
-        hidden = jnp.where(section_pos == 0, entry, arriving)
+        hidden = jnp.where(at_entry, entry, arriving)
         hidden = barrier(hidden)
         wide = hidden.astype(jnp.float32)
         inv_rms = lax.rsqrt(jnp.mean(wide * wide, axis=-1, keepdims=True) + EPSILON)

time: 327 us -> 328 us (level)
  blocking collectives: 229 us -> 248 us
  starting transfers between devices: 22.6 us -> 14 us
  waiting for transfers between devices: 33.6 us -> 25.3 us
    all_to_all x0 -> x1, blocking collectives: none -> 20.4 us  [on_device(): lax.all_to_all(copies, 'expert', split_axis=0, concat_axis=0, axis_index_...]
    all_to_all x1 -> x0, waiting for transfers between devices: 8.47 us -> none  [on_device(): lax.all_to_all(copies, 'expert', split_axis=0, concat_axis=0, axis_index_...]
    all_to_all x1 -> x0, starting transfers between devices: 8.46 us -> none  [on_device(): lax.all_to_all(copies, 'expert', split_axis=0, concat_axis=0, axis_index_...]
  transfers between devices with their start and end apart: 15 -> 14, of which waited for: 15 -> 14; matrix products, arithmetic and copies ran while one was open for 5% -> 4% of each run, Pallas kernels for 0% -> 0%
where the time goes in v8:
time: 328 us; the launch traced here: 327 us
  blocking collectives  248 us (76%)
  matrix products  29.1 us (9%)
  waiting for transfers between devices  25.3 us (8%)
  starting transfers between devices  14 us (4%)
  other arithmetic  6.81 us (2%)
    all_to_all x15, blocking collectives, exchange(): lax.all_to_all(chunks, 'expert', split_axis=0, concat_axis=0, axis_index_...  228 us
    all_to_all x1, blocking collectives, on_device(): lax.all_to_all(copies, 'expert', split_axis=0, concat_axis=0, axis_index_...  20.4 us
    ppermute x4, waiting for transfers between devices, on_device(): lax.ppermute(result, 'section', [(i, i + 1) for i in range(sections - 1)])  15.2 us
    ppermute x4, starting transfers between devices, on_device(): lax.ppermute(result, 'section', [(i, i + 1) for i in range(sections - 1)])  12.8 us
    dot_general x21, matrix products, choose(): return jnp.dot(picks, rows, preferred_element_type=jnp.float32)  7.38 us
  transfers between devices with their start and end apart: 14, of which 14 were waited for; matrix products, arithmetic and copies ran while one was open for 4% of the time, Pallas kernels for 0%

profile of v8, /device:TPU:16, one launch (start us, length us, event | category | flops | bytes accessed | tf_op | source)
XLA Modules:
  0.0 327.2 jit_solution(14488649870059105413)
XLA Ops:
  3.1 1.0 broadcast_in_dim.34
  4.1 20.4 %all_to_all.80 = bf16[4,3,4,3072]{3,2,1,0:T(4,128)(2,1)} all-to-all(bf16[4,3,4,3072]{3,2,1,0:T(4,128)(2,1)S(1)} %broadcast_in_dim.34), channel_id=1, replica_groups={{0,16,32,48},{1,17,33,49},{2,18,34,50},{3,19,35,51},{4,20,36,52},{5,21,..., dimensions={0} | all-to-all | bytes 589824 | tf_op jit(solution)/shard_map/all_to_all | solution.py:161
  24.4 1.0 reshape.648
  25.8 1.0 multiply_convert_fusion.3
  27.2 15.2 %all_to_all.81 = bf16[8,16,3072]{2,1,0:T(8,128)(2,1)S(1)} all-to-all(bf16[8,16,3072]{2,1,0:T(8,128)(2,1)S(1)} %bitcast.259), channel_id=1, replica_groups={{0,2,4,6,8,10,12,14},{1,3,5,7,9,11,13,15},{16,18,20,22,24,26,28,30},{17..., dimensions={0} | all-to-all | bytes 1572864 | tf_op jit(solution)/shard_map/all_to_all | solution.py:20
  43.3 1.4 collective-permute-done
  49.2 15.8 %all_to_all.82 = bf16[8,16,3072]{2,1,0:T(8,128)(2,1)S(1)} all-to-all(bf16[8,16,3072]{2,1,0:T(8,128)(2,1)S(1)} %bitcast.263), channel_id=1, replica_groups={{0,2,4,6,8,10,12,14},{1,3,5,7,9,11,13,15},{16,18,20,22,24,26,28,30},{17..., dimensions={0} | all-to-all | bytes 1572864 | tf_op jit(solution)/shard_map/all_to_all | solution.py:20
  65.3 15.3 %all_to_all.83 = bf16[4,16,3072]{2,1,0:T(8,128)(2,1)S(1)} all-to-all(bf16[4,16,3072]{2,1,0:T(8,128)(2,1)S(1)} %bitcast.270), channel_id=1, replica_groups={{0,16,32,48},{1,17,33,49},{2,18,34,50},{3,19,35,51},{4,20,36,52},{5,21,..., dimensions={0} | all-to-all | bytes 786432 | tf_op jit(solution)/shard_map/all_to_all | solution.py:20
  81.0 3.2 collective-permute-start.2
  84.4 3.7 %collective-permute-done.2 = bf16[24,3072]{1,0:T(8,128)(2,1)S(1)} collective-permute-done((bf16[24,3072]{1,0:T(8,128)(2,1)S(1)}, bf16[24,3072]{1,0:T(8,128)(2,1)S(1)}, u32[]{:S(2)}, u32[]{:S(2)}) %collective-permute-start.2) | collective-permute-done | bytes 147488 | tf_op jit(solution)/shard_map/ppermute | solution.py:212
  88.7 14.5 %all_to_all.84 = bf16[8,16,3072]{2,1,0:T(8,128)(2,1)S(1)} all-to-all(bf16[8,16,3072]{2,1,0:T(8,128)(2,1)S(1)} %bitcast.260), channel_id=1, replica_groups={{0,2,4,6,8,10,12,14},{1,3,5,7,9,11,13,15},{16,18,20,22,24,26,28,30},{17..., dimensions={0} | all-to-all | bytes 1572864 | tf_op jit(solution)/shard_map/all_to_all | solution.py:20
  104.1 1.4 collective-permute-done.3
  110.0 15.9 %all_to_all.85 = bf16[8,16,3072]{2,1,0:T(8,128)(2,1)S(1)} all-to-all(bf16[8,16,3072]{2,1,0:T(8,128)(2,1)S(1)} %bitcast.264), channel_id=1, replica_groups={{0,2,4,6,8,10,12,14},{1,3,5,7,9,11,13,15},{16,18,20,22,24,26,28,30},{17..., dimensions={0} | all-to-all | bytes 1572864 | tf_op jit(solution)/shard_map/all_to_all | solution.py:20
  126.2 15.8 %all_to_all.86 = bf16[4,16,3072]{2,1,0:T(8,128)(2,1)S(1)} all-to-all(bf16[4,16,3072]{2,1,0:T(8,128)(2,1)S(1)} %bitcast.271), channel_id=1, replica_groups={{0,16,32,48},{1,17,33,49},{2,18,34,50},{3,19,35,51},{4,20,36,52},{5,21,..., dimensions={0} | all-to-all | bytes 786432 | tf_op jit(solution)/shard_map/all_to_all | solution.py:20
  142.4 3.2 collective-permute-start.5
  145.6 3.8 %collective-permute-done.5 = bf16[24,3072]{1,0:T(8,128)(2,1)S(1)} collective-permute-done((bf16[24,3072]{1,0:T(8,128)(2,1)S(1)}, bf16[24,3072]{1,0:T(8,128)(2,1)S(1)}, u32[]{:S(2)}, u32[]{:S(2)}) %collective-permute-start.5) | collective-permute-done | bytes 147488 | tf_op jit(solution)/shard_map/ppermute | solution.py:212
  150.2 14.6 %all_to_all.87 = bf16[8,16,3072]{2,1,0:T(8,128)(2,1)S(1)} all-to-all(bf16[8,16,3072]{2,1,0:T(8,128)(2,1)S(1)} %bitcast.261), channel_id=1, replica_groups={{0,2,4,6,8,10,12,14},{1,3,5,7,9,11,13,15},{16,18,20,22,24,26,28,30},{17..., dimensions={0} | all-to-all | bytes 1572864 | tf_op jit(solution)/shard_map/all_to_all | solution.py:20
  165.7 1.4 collective-permute-done.6
  171.6 15.8 %all_to_all.88 = bf16[8,16,3072]{2,1,0:T(8,128)(2,1)S(1)} all-to-all(bf16[8,16,3072]{2,1,0:T(8,128)(2,1)S(1)} %bitcast.265), channel_id=1, replica_groups={{0,2,4,6,8,10,12,14},{1,3,5,7,9,11,13,15},{16,18,20,22,24,26,28,30},{17..., dimensions={0} | all-to-all | bytes 1572864 | tf_op jit(solution)/shard_map/all_to_all | solution.py:20
  187.7 15.8 %all_to_all.89 = bf16[4,16,3072]{2,1,0:T(8,128)(2,1)S(1)} all-to-all(bf16[4,16,3072]{2,1,0:T(8,128)(2,1)S(1)} %bitcast.272), channel_id=1, replica_groups={{0,16,32,48},{1,17,33,49},{2,18,34,50},{3,19,35,51},{4,20,36,52},{5,21,..., dimensions={0} | all-to-all | bytes 786432 | tf_op jit(solution)/shard_map/all_to_all | solution.py:20
  203.9 3.2 collective-permute-start.8
  207.1 3.8 %collective-permute-done.8 = bf16[24,3072]{1,0:T(8,128)(2,1)S(1)} collective-permute-done((bf16[24,3072]{1,0:T(8,128)(2,1)S(1)}, bf16[24,3072]{1,0:T(8,128)(2,1)S(1)}, u32[]{:S(2)}, u32[]{:S(2)}) %collective-permute-start.8) | collective-permute-done | bytes 147488 | tf_op jit(solution)/shard_map/ppermute | solution.py:212
  211.7 14.2 %all_to_all.90 = bf16[8,16,3072]{2,1,0:T(8,128)(2,1)S(1)} all-to-all(bf16[8,16,3072]{2,1,0:T(8,128)(2,1)S(1)} %bitcast.262), channel_id=1, replica_groups={{0,2,4,6,8,10,12,14},{1,3,5,7,9,11,13,15},{16,18,20,22,24,26,28,30},{17..., dimensions={0} | all-to-all | bytes 1572864 | tf_op jit(solution)/shard_map/all_to_all | solution.py:20
  226.7 1.4 collective-permute-done.9
  232.6 15.8 %all_to_all.91 = bf16[8,16,3072]{2,1,0:T(8,128)(2,1)S(1)} all-to-all(bf16[8,16,3072]{2,1,0:T(8,128)(2,1)S(1)} %bitcast.266), channel_id=1, replica_groups={{0,2,4,6,8,10,12,14},{1,3,5,7,9,11,13,15},{16,18,20,22,24,26,28,30},{17..., dimensions={0} | all-to-all | bytes 1572864 | tf_op jit(solution)/shard_map/all_to_all | solution.py:20
  248.7 15.9 %all_to_all.92 = bf16[4,16,3072]{2,1,0:T(8,128)(2,1)S(1)} all-to-all(bf16[4,16,3072]{2,1,0:T(8,128)(2,1)S(1)} %bitcast.269), channel_id=1, replica_groups={{0,16,32,48},{1,17,33,49},{2,18,34,50},{3,19,35,51},{4,20,36,52},{5,21,..., dimensions={0} | all-to-all | bytes 786432 | tf_op jit(solution)/shard_map/all_to_all | solution.py:20
  265.0 3.2 collective-permute-start.11
  268.2 3.8 %collective-permute-done.11 = bf16[24,3072]{1,0:T(8,128)(2,1)S(1)} collective-permute-done((bf16[24,3072]{1,0:T(8,128)(2,1)S(1)}, bf16[24,3072]{1,0:T(8,128)(2,1)S(1)}, u32[]{:S(2)}, u32[]{:S(2)}) %collective-permute-start.11) | collective-permute-done | bytes 147488 | tf_op jit(solution)/shard_map/ppermute | solution.py:212
  272.8 14.5 %all_to_all.93 = bf16[8,16,3072]{2,1,0:T(8,128)(2,1)S(1)} all-to-all(bf16[8,16,3072]{2,1,0:T(8,128)(2,1)S(1)} %bitcast.258), channel_id=1, replica_groups={{0,2,4,6,8,10,12,14},{1,3,5,7,9,11,13,15},{16,18,20,22,24,26,28,30},{17..., dimensions={0} | all-to-all | bytes 1572864 | tf_op jit(solution)/shard_map/all_to_all | solution.py:20
  294.8 15.8 %all_to_all.94 = bf16[8,16,3072]{2,1,0:T(8,128)(2,1)S(1)} all-to-all(bf16[8,16,3072]{2,1,0:T(8,128)(2,1)S(1)} %bitcast.267), channel_id=1, replica_groups={{0,2,4,6,8,10,12,14},{1,3,5,7,9,11,13,15},{16,18,20,22,24,26,28,30},{17..., dimensions={0} | all-to-all | bytes 1572864 | tf_op jit(solution)/shard_map/all_to_all | solution.py:20
  310.9 12.6 %all_to_all.95 = bf16[4,8,3072]{2,1,0:T(8,128)(2,1)S(1)} all-to-all(bf16[4,8,3072]{2,1,0:T(8,128)(2,1)S(1)} %fusion.12), channel_id=1, replica_groups={{0,16,32,48},{1,17,33,49},{2,18,34,50},{3,19,35,51},{4,20,36,52},{5,21,..., dimensions={0} | all-to-all | bytes 393216 | tf_op jit(solution)/shard_map/all_to_all | solution.py:20
  324.3 1.2 fusion.67
  (168 shorter events, 40.3 us)
Async XLA Ops:
  0.0 46.0 %copy-start = (bf16[1,512,3072]{2,1,0:T(8,128)(2,1)S(1)}, bf16[1,512,3072]{2,1,0:T(8,128)(2,1)}, u32[]{:S(2)}) copy-start(bf16[1,512,3072]{2,1,0:T(8,128)(2,1)} %param.13) | copy-start | bytes 9437188
  25.5 17.0 %copy-start.4 = (bf16[1,3072,4]{1,2,0:T(4,128)(2,1)S(1)}, bf16[1,3072,4]{1,2,0:T(4,128)(2,1)}, u32[]{:S(2)}) copy-start(bf16[1,3072,4]{1,2,0:T(4,128)(2,1)} %param.10) | copy-start | bytes 73732
  25.5 17.2 %copy-start.1 = (bf16[1,3072,512]{2,1,0:T(8,128)(2,1)S(1)}, bf16[1,3072,512]{2,1,0:T(8,128)(2,1)}, u32[]{:S(2)}) copy-start(bf16[1,3072,512]{2,1,0:T(8,128)(2,1)} %param.12) | copy-start | bytes 9437188
  42.4 2.3 collective-permute-start
  42.6 2.7 copy-start.2
  46.6 2.4 collective-permute-start.1
  49.2 39.0 %copy-start.3 = (f32[1,3072]{1,0:T(1,128)S(1)}, f32[1,3072]{1,0:T(1,128)}, u32[]{:S(2)}) copy-start(f32[1,3072]{1,0:T(1,128)} %param.9) | copy-start | bytes 36868
  81.0 7.0 %collective-permute-start.2 = (bf16[24,3072]{1,0:T(8,128)(2,1)S(1)}, bf16[24,3072]{1,0:T(8,128)(2,1)S(1)}, u32[]{:S(2)}, u32[]{:S(2)}) collective-permute-start(bf16[24,3072]{1,0:T(8,128)(2,1)S(1)} %fusion.8), channel_id=1, source_target_pairs={{0,64},{64,128},{128,192},{1,65},{65,129},{129,193},{2,66},{66,130... | collective-permute-start | bytes 442376 | tf_op jit(solution)/shard_map/ppermute | solution.py:212
  103.2 2.3 collective-permute-start.3
  107.5 2.4 collective-permute-start.4
  142.4 7.0 %collective-permute-start.5 = (bf16[24,3072]{1,0:T(8,128)(2,1)S(1)}, bf16[24,3072]{1,0:T(8,128)(2,1)S(1)}, u32[]{:S(2)}, u32[]{:S(2)}) collective-permute-start(bf16[24,3072]{1,0:T(8,128)(2,1)S(1)} %fusion.9), channel_id=1, source_target_pairs={{0,64},{64,128},{128,192},{1,65},{65,129},{129,193},{2,66},{66,130... | collective-permute-start | bytes 442376 | tf_op jit(solution)/shard_map/ppermute | solution.py:212
  164.8 2.3 collective-permute-start.6
  169.0 2.4 collective-permute-start.7
  203.9 7.0 %collective-permute-start.8 = (bf16[24,3072]{1,0:T(8,128)(2,1)S(1)}, bf16[24,3072]{1,0:T(8,128)(2,1)S(1)}, u32[]{:S(2)}, u32[]{:S(2)}) collective-permute-start(bf16[24,3072]{1,0:T(8,128)(2,1)S(1)} %fusion.10), channel_id=1, source_target_pairs={{0,64},{64,128},{128,192},{1,65},{65,129},{129,193},{2,66},{66,130... | collective-permute-start | bytes 442376 | tf_op jit(solution)/shard_map/ppermute | solution.py:212
  225.9 2.3 collective-permute-start.9
  230.1 2.4 collective-permute-start.10
  265.0 7.0 %collective-permute-start.11 = (bf16[24,3072]{1,0:T(8,128)(2,1)S(1)}, bf16[24,3072]{1,0:T(8,128)(2,1)S(1)}, u32[]{:S(2)}, u32[]{:S(2)}) collective-permute-start(bf16[24,3072]{1,0:T(8,128)(2,1)S(1)} %fusion.11), channel_id=1, source_target_pairs={{0,64},{64,128},{128,192},{1,65},{65,129},{129,193},{2,66},{66,130... | collective-permute-start | bytes 442376 | tf_op jit(solution)/shard_map/ppermute | solution.py:212
  287.9 2.4 collective-permute-start.12
  292.3 2.4 collective-permute-start.13
